TPU v7x, 128 devices: a whole 4x4x4 slice. The times are simulated.
128 devices in a mesh: grp: 8 (over y, z_lo), dev: 16 (over x, z_hi, core).
Axes of the slice: x: 4, y: 4, z: 4 (z_hi: 2, z_lo: 2; z = z_hi * 2 + z_lo), core: 2. Of those that a mesh axis runs over, the one named last changes fastest.
Arguments:
- table: bfloat16 [8, 131072, 256], P('grp', 'dev'), may hold values from -0.75 to 0.75
- token_ids: int32 [32768], P(('grp', 'dev')), may hold values from 0 to 131071, as said below
- hidden: bfloat16 [32768, 2560], P(('grp', 'dev')), may hold values from -6 to 6
- w_proj: bfloat16 [2560, 2048], replicated, may hold values from -0.125 to 0.125
- norm_gain: float32 [256], replicated, may hold values from 0.5 to 1.5
Outputs:
- served_table: bfloat16 [16, 8, 1024, 2048], P('dev', 'grp')
- layer_inputs: bfloat16 [32768, 8, 256], P(('grp', 'dev'))
Inputs may be any that keep to these rules, and one draw needn't show every extreme that they name: `token_ids`: of the 256 tokens of one device, at most 4 have ids in any one aligned block of 1024 vocabulary rows, and exactly 4 in some block.
All inputs are finite; a program needn't handle non-finite values.
Results may differ from a plain program's by a relative error of at most 0.001.
Values may be sent and summed in bfloat16 or wider, within the bound.
No kernel may reach another device: no remote copies, remote signals or barrier semaphores. Data moves between devices by JAX's collectives and lax.ppermute only.
A program may use at most 128 MiB of HBM per device.

v0:
```python
import math

import jax
import jax.numpy as jnp
from jax import lax
from jax.sharding import PartitionSpec as P


def cut_along(x, dim, count):
    shape = x.shape
    pieces = x.reshape(*shape[:dim], count, shape[dim] // count, *shape[dim + 1 :])
    return jnp.moveaxis(pieces, dim, 0)


def cut_rows(length, count):
    unit = 8 if length >= 8 * count else 1
    return [length // unit * k // count * unit for k in range(1, count)]


def joined_along(pieces, dim):
    shape = list(pieces.shape[1:])
    shape[dim] *= pieces.shape[0]
    return jnp.moveaxis(pieces, 0, dim).reshape(shape)


def several_exchanges(x, axis, pieces, split_dim, concat_dim):
    blocks = cut_along(x, split_dim, lax.axis_size(axis))
    cut = max(range(1, max(2, blocks.ndim - 1)), key=lambda d: blocks.shape[d])
    finished = []
    for piece in jnp.split(blocks, cut_rows(blocks.shape[cut], pieces), axis=cut):
        if piece.size:
            finished.append(lax.all_to_all(piece, axis, split_axis=0, concat_axis=0, tiled=True))
    return joined_along(jnp.concatenate(finished, axis=cut), concat_dim)


def lookup(all_ids, local_rows, base):
    owned = local_rows.shape[0]
    count = all_ids.shape[0]
    block = math.gcd(count, 512)
    blocks = all_ids.reshape(count // block, block)

    def one_block(ids_block):
        onehot = (ids_block[:, None] - base == jnp.arange(owned, dtype=jnp.int32)[None, :]).astype(
            jnp.bfloat16
        )
        return jnp.dot(onehot, local_rows, preferred_element_type=jnp.float32).astype(jnp.bfloat16)

    return lax.map(one_block, blocks).reshape(count, local_rows.shape[1])


def on_device(table, token_ids, hidden, w_proj, norm_gain):
    n_grp = lax.axis_size("grp")
    n_dev = lax.axis_size("dev")
    g_index = lax.axis_index("grp")
    d_index = lax.axis_index("dev")
    layer_share, vocab_share, width = table.shape
    layers = layer_share * n_grp
    tok_count = token_ids.shape[0]
    moved = several_exchanges(table, "grp", 2, 1, 0)
    row_count = moved.shape[1]
    served_rows = jnp.transpose(moved, (1, 0, 2)).reshape(row_count, layers * width)
    served_table = served_rows.reshape(1, 1, row_count, layers * width)
    peers = n_grp * n_dev
    capacity = max(2, 2 * tok_count // peers)
    owner_block = token_ids // row_count
    owner_peer = owner_block % n_grp * n_dev + owner_block // n_grp
    positions = jnp.arange(tok_count, dtype=jnp.int32)
    same_peer = owner_peer[:, None] == owner_peer[None, :]
    earlier = positions[None, :] < positions[:, None]
    slot_index = jnp.sum((same_peer & earlier).astype(jnp.int32), axis=1)
    wanted = owner_peer * capacity + slot_index
    slot_hit = (wanted[:, None] == jnp.arange(peers * capacity, dtype=jnp.int32)[None, :]).astype(
        jnp.int32
    )
    outgoing = jnp.sum(slot_hit * (token_ids + 1)[:, None], axis=0) - 1
    base = (d_index * n_grp + g_index) * row_count
    incoming = lax.all_to_all(
        outgoing.reshape(peers, capacity), ("grp", "dev"), split_axis=0, concat_axis=0, tiled=True
    )
    found = lookup(incoming.reshape(peers * capacity), served_rows, base)
    found = found.reshape(peers, capacity, layers * width)
    replies = lax.all_to_all(found, ("grp", "dev"), split_axis=0, concat_axis=0, tiled=True)
    picker = slot_hit.astype(jnp.bfloat16)
    emb = jnp.dot(
        picker,
        replies.reshape(peers * capacity, layers * width),
        preferred_element_type=jnp.float32,
    )
    proj = jnp.dot(hidden, w_proj, preferred_element_type=jnp.float32).reshape(
        tok_count, layers, width
    )
    mean_sq = jnp.mean(proj * proj, axis=-1, keepdims=True)
    normed = proj / jnp.sqrt(mean_sq + 1e-06) * norm_gain
    emb = emb.reshape(tok_count, layers, width)
    layer_inputs = ((normed + math.sqrt(width) * emb) / math.sqrt(2.0)).astype(jnp.bfloat16)
    return (served_table, layer_inputs)


def solution(mesh):
    in_specs = (P("grp", "dev", None), P(("grp", "dev")), P(("grp", "dev"), None), P(), P())
    out_specs = (P("dev", "grp", None, None), P(("grp", "dev"), None, None))
    return jax.shard_map(
        on_device, mesh=mesh, in_specs=in_specs, out_specs=out_specs, check_vma=False
    )
```

profile of v0, /device:TPU:0, one launch (start us, length us, event | category | flops | bytes accessed | tf_op | source)
XLA Modules:
  0.0 142.2 jit_solution(10128674087388023267)
XLA Ops:
  0.6 0.8 fusion.10
  1.8 0.7 sub.35
  2.5 11.1 %all-to-all-start.2 = ((s32[128,1,4]{2,1,0:T(1,128)}), s32[128,1,4]{2,1,0:T(1,128)S(1)}, u32[]{:S(2)}, u32[]{:S(2)}) async-start(s32[128,1,4]{2,1,0:T(1,128)} %bitcast.5), calls=%async_computation.2 | async-start | bytes 131072 | tf_op jit(solution)/shard_map/all_to_all | solution.py:77
  13.7 3.9 %fusion.11 = (bf16[8,1,512,256]{3,2,1,0:T(8,128)(2,1)S(1)}, bf16[8,1,512,256]{3,2,1,0:T(8,128)(2,1)}) fusion(bf16[8,1,1024,256]{3,2,1,0:T(8,128)(2,1)} %bitcast.35), kind=kLoop, calls=%fused_computation.34 | loop fusion | bytes 8388608 | tf_op jit(solution)/shard_map/split | solution.py:30
  17.6 5.5 %all-to-all-done.2 = s32[128,1,4]{2,1,0:T(1,128)S(1)} async-done(((s32[128,1,4]{2,1,0:T(1,128)}), s32[128,1,4]{2,1,0:T(1,128)S(1)}, u32[]{:S(2)}, u32[]{:S(2)}) %all-to-all-start.2) | async-done | bytes 2080 | tf_op jit(solution)/shard_map/all_to_all | solution.py:77
  23.1 29.8 %all_to_all.21 = bf16[8,1,512,256]{3,2,1,0:T(8,128)(2,1)} all-to-all(bf16[8,1,512,256]{3,2,1,0:T(8,128)(2,1)S(1)} %get-tuple-element.29), channel_id=1, replica_groups=mesh['grp'=8,'dev'=16] {'grp'}, dimensions={0} | all-to-all | bytes 4194304 | tf_op jit(solution)/shard_map/all_to_all | solution.py:32
  52.9 3.6 %all-to-all-start.1 = ((bf16[8,1,512,256]{3,2,1,0:T(8,128)(2,1)}), bf16[8,1,512,256]{3,2,1,0:T(8,128)(2,1)S(1)}, u32[]{:S(2)}, u32[]{:S(2)}) async-start(bf16[8,1,512,256]{3,2,1,0:T(8,128)(2,1)} %get-tuple-element.30), calls=%async_computation.1 | async-start | bytes 4194304 | tf_op jit(solution)/shard_map/all_to_all | solution.py:32
  56.8 3.9 %copy.38 = bf16[8,1,512,256]{2,3,0,1:T(8,128)(2,1)} copy(bf16[8,1,512,256]{3,2,1,0:T(8,128)(2,1)} %all_to_all.21) | data formatting | bytes 4194304 | tf_op jit(solution)/shard_map/all_to_all | solution.py:32
  60.8 25.3 %all-to-all-done.1 = bf16[8,1,512,256]{3,2,1,0:T(8,128)(2,1)S(1)} async-done(((bf16[8,1,512,256]{3,2,1,0:T(8,128)(2,1)}), bf16[8,1,512,256]{3,2,1,0:T(8,128)(2,1)S(1)}, u32[]{:S(2)}, u32[]{:S(2)}) %all-to-all-start.1) | async-done | bytes 2097184 | tf_op jit(solution)/shard_map/all_to_all | solution.py:32
  86.1 2.4 %copy.39 = bf16[8,1,512,256]{2,3,0,1:T(8,128)(2,1)} copy(bf16[8,1,512,256]{3,2,1,0:T(8,128)(2,1)S(1)} %all-to-all-done.1) | data formatting | bytes 4194304 | tf_op jit(solution)/shard_map/all_to_all | solution.py:32
  88.5 2.7 %pad_maximum_fusion = bf16[8,1,1024,256]{2,3,0,1:T(8,128)(2,1)S(1)} fusion(bf16[8,1,512,256]{2,3,0,1:T(8,128)(2,1)} %copy.39, bf16[8,1,512,256]{2,3,0,1:T(8,128)(2,1)} %copy.38), kind=kLoop, calls=%fused_computation | loop fusion | flops 8388608 | bytes 8388608 | tf_op jit(solution)/shard_map/concatenate | solution.py:33
  91.2 1.9 %copy-done.1 = bf16[8,1,1024,256]{2,3,0,1:T(8,128)(2,1)} copy-done((bf16[8,1,1024,256]{2,3,0,1:T(8,128)(2,1)}, bf16[8,1,1024,256]{2,3,0,1:T(8,128)(2,1)S(1)}, u32[]{:S(2)}) %copy-start.1) | copy-done | bytes 4194328
  93.1 2.4 %convolution_convert_fusion = bf16[512,2048]{1,0:T(8,128)(2,1)S(1)} fusion(bf16[1024,2048]{0,1:T(8,128)(2,1)S(1)} %bitcast.32, s32[512]{0:T(512)S(1)} %sub.38), kind=kOutput, calls=%fused_computation.1 | convolution fusion | flops 2149056512 | bytes 6293504 | tf_op jit(solution)/shard_map/while/body/eval_jaxpr/dot_general | solution.py:46
  95.5 2.2 %reshape_reshape.8 = bf16[128,4,2048]{2,1,0:T(4,128)(2,1)} reshape(bf16[512,2048]{1,0:T(8,128)(2,1)S(1)} %convolution_convert_fusion) | data formatting | bytes 4194304 | tf_op jit(solution)/shard_map/reshape;reshape | solution.py:81
  97.8 4.6 %all-to-all-start.3 = ((bf16[128,4,2048]{2,1,0:T(4,128)(2,1)}), bf16[128,4,2048]{2,1,0:T(4,128)(2,1)S(1)}, u32[]{:S(2)}, u32[]{:S(2)}) async-start(bf16[128,4,2048]{2,1,0:T(4,128)(2,1)} %reshape_reshape.8), calls=%async_computation.3 | async-start | bytes 4194304 | tf_op jit(solution)/shard_map/all_to_all | solution.py:82
  102.4 5.6 %fusion.12 = f32[256,2048]{1,0:T(8,128)S(1)} fusion(bf16[256,2560]{1,0:T(8,128)(2,1)S(1)} %copy-done, bf16[2560,2048]{1,0:T(8,128)(2,1)} %param.8), kind=kOutput, calls=%fused_computation.35 | convolution fusion | flops 2684354560 | bytes 13893632 | tf_op jit(solution)/shard_map/dot_general | solution.py:89
  108.0 0.9 copy.47
  108.9 0.4 copy-done.2
  109.8 6.4 %copy.44 = bf16[1,1,1024,2048]{3,2,1,0:T(8,128)(2,1)} copy(bf16[1,1,1024,2048]{2,3,1,0:T(8,128)(2,1)} %bitcast.33) | data formatting | bytes 8388608
  116.3 15.9 %all-to-all-done.3 = bf16[128,4,2048]{2,1,0:T(4,128)(2,1)S(1)} async-done(((bf16[128,4,2048]{2,1,0:T(4,128)(2,1)}), bf16[128,4,2048]{2,1,0:T(4,128)(2,1)S(1)}, u32[]{:S(2)}, u32[]{:S(2)}) %all-to-all-start.3) | async-done | bytes 2097184 | tf_op jit(solution)/shard_map/all_to_all | solution.py:82
  132.1 2.0 %reshape.63 = bf16[512,2048]{1,0:T(8,128)(2,1)} reshape(bf16[128,4,2048]{2,1,0:T(4,128)(2,1)S(1)} %all-to-all-done.3) | data formatting | bytes 4194304 | tf_op jit(solution)/shard_map/reshape | solution.py:86
  134.2 4.1 %copy.43 = bf16[512,2048]{0,1:T(8,128)(2,1)} copy(bf16[512,2048]{1,0:T(8,128)(2,1)} %reshape.63) | data formatting | bytes 4194304 | tf_op jit(solution)/shard_map/reshape | solution.py:86
  138.2 2.4 %fusion.3 = bf16[256,8,256]{2,0,1:T(8,128)(2,1)S(1)} fusion(f32[32,8,8,256]{3,2,1,0:T(8,128)S(1)} %bitcast.37, bf16[8,256,512]{2,1,0:T(8,128)(2,1)} %bitcast.38, f32[256]{0:T(256)S(1)} %copy-done.4, f32[256,8]{0,1:T(8,128)S(1)} %add_sqrt_fusion, s32[256]{0:T(256)S(1)} %multiply_add_fusion), kind=kOutput, calls=%fused_computation.8 | convolution fusion | flops 540409856 | bytes 5253120 | tf_op jit(solution)/shard_map/dot_general | solution.py:84
  140.6 1.6 %copy.45 = bf16[256,8,256]{2,1,0:T(8,128)(2,1)} copy(bf16[256,8,256]{2,0,1:T(8,128)(2,1)S(1)} %fusion.3) | data formatting | bytes 2097152
  (17 shorter events, 1.1 us)
Async XLA Ops:
  0.6 101.8 %copy-start = (bf16[256,2560]{1,0:T(8,128)(2,1)S(1)}, bf16[256,2560]{1,0:T(8,128)(2,1)}, u32[]{:S(2)}) copy-start(bf16[256,2560]{1,0:T(8,128)(2,1)} %param.7) | copy-start | bytes 3932164
  2.5 20.6 %all-to-all-start.2 = ((s32[128,1,4]{2,1,0:T(1,128)}), s32[128,1,4]{2,1,0:T(1,128)S(1)}, u32[]{:S(2)}, u32[]{:S(2)}) async-start(s32[128,1,4]{2,1,0:T(1,128)} %bitcast.5), calls=%async_computation.2 | async-start | bytes 131072 | tf_op jit(solution)/shard_map/all_to_all | solution.py:77
  52.9 33.1 %all-to-all-start.1 = ((bf16[8,1,512,256]{3,2,1,0:T(8,128)(2,1)}), bf16[8,1,512,256]{3,2,1,0:T(8,128)(2,1)S(1)}, u32[]{:S(2)}, u32[]{:S(2)}) async-start(bf16[8,1,512,256]{3,2,1,0:T(8,128)(2,1)} %get-tuple-element.30), calls=%async_computation.1 | async-start | bytes 4194304 | tf_op jit(solution)/shard_map/all_to_all | solution.py:32
  91.2 1.9 %copy-start.1 = (bf16[8,1,1024,256]{2,3,0,1:T(8,128)(2,1)}, bf16[8,1,1024,256]{2,3,0,1:T(8,128)(2,1)S(1)}, u32[]{:S(2)}) copy-start(bf16[8,1,1024,256]{2,3,0,1:T(8,128)(2,1)S(1)} %pad_maximum_fusion) | copy-start | bytes 12582916
  97.8 34.4 %all-to-all-start.3 = ((bf16[128,4,2048]{2,1,0:T(4,128)(2,1)}), bf16[128,4,2048]{2,1,0:T(4,128)(2,1)S(1)}, u32[]{:S(2)}, u32[]{:S(2)}) async-start(bf16[128,4,2048]{2,1,0:T(4,128)(2,1)} %reshape_reshape.8), calls=%async_computation.3 | async-start | bytes 4194304 | tf_op jit(solution)/shard_map/all_to_all | solution.py:82
  108.0 1.4 copy-start.2
  134.1 4.1 %copy-start.3 = (f32[256,2048]{1,0:T(8,128)S(1)}, f32[256,2048]{1,0:T(8,128)}, u32[]{:S(2)}) copy-start(f32[256,2048]{1,0:T(8,128)} %copy-done.2) | copy-start | bytes 6291460
  134.2 4.1 %copy-start.4 = (f32[256]{0:T(256)S(1)}, f32[256]{0:T(256)}, u32[]{:S(2)}) copy-start(f32[256]{0:T(256)} %param.9) | copy-start | bytes 3076
where the time goes:
time: 143 us; the launch traced here: 142 us
  waiting for transfers between devices  46.7 us (33%)
  local copies, waits for them, and re-layouts  30.7 us (21%)
  blocking collectives  29.8 us (21%)
  starting transfers between devices  19.4 us (14%)
  matrix products  10.3 us (7%)
  other arithmetic  4.43 us (3%)
    all_to_all x1, blocking collectives, several_exchanges(): lax.all_to_all(piece, axis, split_axis=0, concat_axis=0, tiled=True)  29.8 us
    all_to_all x1, waiting for transfers between devices, several_exchanges(): lax.all_to_all(piece, axis, split_axis=0, concat_axis=0, tiled=True)  25.3 us
    all_to_all x1, waiting for transfers between devices, on_device(): lax.all_to_all(found, ('grp', 'dev'), split_axis=0, concat_axis=0, tiled=...  15.9 us
    unnamed x13, local copies, waits for them, and re-layouts  11.3 us
    all_to_all x1, starting transfers between devices, on_device(): lax.all_to_all(outgoing.reshape(peers, capacity), ('grp', 'dev'), split_a...  11.1 us
    all_to_all x2, local copies, waits for them, and re-layouts, several_exchanges(): lax.all_to_all(piece, axis, split_axis=0, concat_axis=0, tiled=True)  6.31 us
    reshape x2, local copies, waits for them, and re-layouts, on_device(): replies.reshape(peers * capacity, layers * width)  6.1 us
    dot_general x1, matrix products, on_device(): jnp.dot(hidden, w_proj, preferred_element_type=jnp.float32)  5.61 us
  transfers between devices with their start and end apart: 3, of which 3 were waited for; matrix products, arithmetic and copies ran while one was open for 15% of the time, Pallas kernels for 0%

commit v1 on v0

v1 whole, which is shorter than its diff:
```python
import math

import jax
import jax.numpy as jnp
from jax import lax
from jax.experimental import pallas as pl
from jax.experimental.pallas import tpu as pltpu
from jax.sharding import PartitionSpec as P

CAP = 4


def rows_side_by_side(stacked):
    layers, rows, width = stacked.shape

    def body(x_ref, o_ref):
        o_ref[...] = x_ref[0]

    return pl.pallas_call(
        body,
        grid=(layers,),
        in_specs=[pl.BlockSpec((1, rows, width), lambda l: (l, 0, 0))],
        out_specs=pl.BlockSpec((rows, width), lambda l: (0, l)),
        out_shape=jax.ShapeDtypeStruct((rows, layers * width), stacked.dtype),
        cost_estimate=pl.CostEstimate(
            flops=0, bytes_accessed=2 * stacked.size * 2, transcendentals=0
        ),
    )(stacked)


def normed_projection(hidden, w_proj, norm_gain, layers):
    tok, depth = hidden.shape
    width = w_proj.shape[1] // layers

    def body(h_ref, w_ref, g_ref, o_ref):
        proj = jnp.dot(h_ref[...], w_ref[...], preferred_element_type=jnp.float32)
        mean_sq = jnp.mean(proj * proj, axis=-1, keepdims=True)
        o_ref[0] = proj / jnp.sqrt(mean_sq + 1e-06) * g_ref[...]

    return pl.pallas_call(
        body,
        grid=(layers,),
        in_specs=[
            pl.BlockSpec((tok, depth), lambda l: (0, 0)),
            pl.BlockSpec((depth, width), lambda l: (0, l)),
            pl.BlockSpec((1, width), lambda l: (0, 0)),
        ],
        out_specs=pl.BlockSpec((1, tok, width), lambda l: (l, 0, 0)),
        out_shape=jax.ShapeDtypeStruct((layers, tok, width), jnp.float32),
        cost_estimate=pl.CostEstimate(
            flops=2 * tok * depth * layers * width,
            bytes_accessed=2 * depth * (tok + layers * width) + 4 * tok * layers * width,
            transcendentals=0,
        ),
    )(hidden, w_proj, norm_gain.reshape(1, width))


def pick_and_add(slots, replies, normed):
    layers, count, width = replies.shape
    tok = normed.shape[1]

    def body(s_ref, r_ref, n_ref, o_ref, acc_ref):
        picker = (
            s_ref[...] == lax.broadcasted_iota(jnp.int32, (tok, count), 1)
        ).astype(jnp.bfloat16)
        for l in range(layers):
            emb = jnp.dot(picker, r_ref[l], preferred_element_type=jnp.float32)
            acc_ref[:, l, :] = (n_ref[l] + math.sqrt(width) * emb) / math.sqrt(2.0)
        o_ref[...] = acc_ref[...].astype(jnp.bfloat16)

    return pl.pallas_call(
        body,
        out_shape=jax.ShapeDtypeStruct((tok, layers, width), jnp.bfloat16),
        scratch_shapes=[pltpu.VMEM((tok, layers, width), jnp.float32)],
        cost_estimate=pl.CostEstimate(
            flops=2 * tok * count * layers * width,
            bytes_accessed=2 * layers * width * (count + 3 * tok),
            transcendentals=0,
        ),
    )(slots.reshape(tok, 1), replies, normed)


def on_device(table, token_ids, hidden, w_proj, norm_gain):
    n_grp = lax.axis_size("grp")
    n_dev = lax.axis_size("dev")
    peers = n_grp * n_dev
    _, shard_rows, width = table.shape
    layers = w_proj.shape[1] // width
    row_count = shard_rows // n_grp
    tok_count = token_ids.shape[0]
    blocks = peers
    slots = blocks * CAP
    dev_slots = slots // n_dev
    both = ("grp", "dev")

    owner = token_ids // row_count
    positions = jnp.arange(tok_count, dtype=jnp.int32)
    same = (owner[:, None] == owner[None, :]) & (positions[None, :] < positions[:, None])
    slot = owner * CAP + jnp.sum(same.astype(jnp.int32), axis=1)
    hit = (slot[:, None] == jnp.arange(slots, dtype=jnp.int32)[None, :]).astype(jnp.int32)
    local = token_ids % row_count
    outgoing = (jnp.sum(hit * (local + 1)[:, None], axis=0) - 1).reshape(1, n_dev, dev_slots)
    outgoing = jnp.broadcast_to(outgoing, (n_grp, n_dev, dev_slots)).reshape(peers, dev_slots)
    incoming = lax.all_to_all(outgoing, both, split_axis=0, concat_axis=0, tiled=True)

    shard = table.reshape(n_grp, row_count, width)
    gated, incoming = lax.optimization_barrier((shard, incoming))
    moved = lax.all_to_all(gated, "grp", split_axis=0, concat_axis=0, tiled=True)

    wanted = incoming.reshape(peers, n_grp, CAP).transpose(1, 0, 2).reshape(n_grp, peers * CAP)
    onehot = (
        wanted[:, :, None] == jnp.arange(row_count, dtype=jnp.int32)[None, None, :]
    ).astype(jnp.bfloat16)
    found = lax.dot_general(
        onehot, shard, (((2,), (1,)), ((0,), (0,))), preferred_element_type=jnp.float32
    ).astype(jnp.bfloat16)
    found = found.reshape(n_grp, peers, CAP, width).transpose(1, 0, 2, 3)
    found = found.reshape(peers, dev_slots, width)
    normed = normed_projection(hidden, w_proj, norm_gain, layers)
    moved, found, normed = lax.optimization_barrier((moved, found, normed))

    replies = lax.all_to_all(found, both, split_axis=0, concat_axis=0, tiled=True)
    served = rows_side_by_side(moved).reshape(1, 1, row_count, layers * width)
    layer_inputs = pick_and_add(slot, replies.reshape(layers, slots, width), normed)
    return (served, layer_inputs)


def solution(mesh):
    in_specs = (P("grp", "dev", None), P(("grp", "dev")), P(("grp", "dev"), None), P(), P())
    out_specs = (P("dev", "grp", None, None), P(("grp", "dev"), None, None))
    return jax.shard_map(
        on_device, mesh=mesh, in_specs=in_specs, out_specs=out_specs, check_vma=False
    )
```

time: 143 us -> 128 us (0.90)
  Pallas kernels: 0 us -> 21.4 us
  local copies, waits for them, and re-layouts: 30.7 us -> 11.6 us
  starting transfers between devices: 19.4 us -> 9.44 us
  waiting for transfers between devices: 46.7 us -> 56.2 us
  blocking collectives: 29.8 us -> 20.4 us
  matrix products: 10.3 us -> 6.27 us
  other arithmetic: 4.43 us -> 1.04 us
    pallas_call x0 -> x3, Pallas kernels: none -> 21.4 us  [the longest x1 10.1 us: normed_projection(): pl.pallas_call(body, grid=(layers,), in_specs=[pl.BlockSpec((tok, depth),...]
    all_to_all x3 -> x2, starting transfers between devices: 19.4 us -> 9.44 us  [the longest x1 4.88 us: on_device(): lax.all_to_all(found, both, split_axis=0, concat_axis=0, tiled=True)]
    unnamed x13 -> x2, local copies, waits for them, and re-layouts: 11.3 us -> 1.35 us
    all_to_all x3 -> x2, waiting for transfers between devices: 46.7 us -> 56.2 us  [the longest x1 33.9 us: on_device(): lax.all_to_all(gated, 'grp', split_axis=0, concat_axis=0, tiled=True)]
    all_to_all x1, blocking collectives: 29.8 us -> 20.4 us  [on_device(): lax.all_to_all(outgoing, both, split_axis=0, concat_axis=0, tiled=True)]
    all_to_all x2 -> x1, local copies, waits for them, and re-layouts: 6.31 us -> 0.05 us  [on_device(): lax.all_to_all(outgoing, both, split_axis=0, concat_axis=0, tiled=True)]
    dot_general x3 -> x1, matrix products: 10.3 us -> 6.27 us  [on_device(): lax.dot_general(onehot, shard, (((2,), (1,)), ((0,), (0,))), preferred_el...]
    split x1 -> x0, local copies, waits for them, and re-layouts: 3.87 us -> none  [several_exchanges(): jnp.split(blocks, cut_rows(blocks.shape[cut], pieces), axis=cut)]
  transfers between devices with their start and end apart: 3 -> 2, of which waited for: 3 -> 2; matrix products, arithmetic and copies ran while one was open for 15% -> 13% of each run, Pallas kernels for 0% -> 13%
where the time goes in v1:
time: 128 us; the launch traced here: 127 us
  waiting for transfers between devices  56.2 us (44%)
  Pallas kernels  21.4 us (17%)
  blocking collectives  20.4 us (16%)
  local copies, waits for them, and re-layouts  11.6 us (9%)
  starting transfers between devices  9.44 us (7%)
  matrix products  6.27 us (5%)
    all_to_all x1, waiting for transfers between devices, on_device(): lax.all_to_all(gated, 'grp', split_axis=0, concat_axis=0, tiled=True)  33.9 us
    all_to_all x1, waiting for transfers between devices, on_device(): lax.all_to_all(found, both, split_axis=0, concat_axis=0, tiled=True)  22.3 us
    all_to_all x1, blocking collectives, on_device(): lax.all_to_all(outgoing, both, split_axis=0, concat_axis=0, tiled=True)  20.4 us
    pallas_call x1, Pallas kernels, normed_projection(): pl.pallas_call(body, grid=(layers,), in_specs=[pl.BlockSpec((tok, depth),...  10.1 us
    pallas_call x1, Pallas kernels, rows_side_by_side(): pl.pallas_call(body, grid=(layers,), in_specs=[pl.BlockSpec((1, rows, wid...  6.58 us
    dot_general x1, matrix products, on_device(): lax.dot_general(onehot, shard, (((2,), (1,)), ((0,), (0,))), preferred_el...  6.27 us
    all_to_all x1, starting transfers between devices, on_device(): lax.all_to_all(found, both, split_axis=0, concat_axis=0, tiled=True)  4.88 us
    pallas_call x1, Pallas kernels, pick_and_add(): pl.pallas_call(body, out_shape=jax.ShapeDtypeStruct((tok, layers, width),...  4.71 us
  transfers between devices with their start and end apart: 2, of which 2 were waited for; matrix products, arithmetic and copies ran while one was open for 13% of the time, Pallas kernels for 13%

profile of v1, /device:TPU:0, one launch (start us, length us, event | category | flops | bytes accessed | tf_op | source)
XLA Modules:
  0.0 127.1 jit_solution(10765280858777632803)
XLA Ops:
  0.6 0.7 and_select_fusion.1
  1.3 0.2 convert_reduce_fusion
  1.5 0.2 select_reduce_fusion
  1.7 0.1 sub.14
  1.8 20.4 %all_to_all.22 = s32[128,1,32]{2,1,0:T(1,128)S(1)} all-to-all(s32[128,1,32]{2,1,0:T(1,128)S(1)} %bitcast.21), channel_id=1, replica_groups=mesh['grp'=8,'dev'=16] {'grp','dev'}, dimensions={0} | all-to-all | bytes 32768 | tf_op jit(solution)/shard_map/all_to_all | solution.py:104
  22.2 0.1 copy.24
  22.2 4.6 %all-to-all-start.1 = ((bf16[8,1024,256]{2,1,0:T(8,128)(2,1)}), bf16[8,1024,256]{2,1,0:T(8,128)(2,1)}, u32[]{:S(2)}, u32[]{:S(2)}) async-start(bf16[8,1024,256]{2,1,0:T(8,128)(2,1)} %bitcast.17), calls=%async_computation.1 | async-start | bytes 8388608 | tf_op jit(solution)/shard_map/all_to_all | solution.py:108
  26.8 10.1 %shard_map.68.n_ref = f32[8,256,256]{2,1,0:T(8,128)} custom-call(bf16[256,2560]{1,0:T(8,128)(2,1)} %h_ref.1, bf16[2560,2048]{1,0:T(8,128)(2,1)} %w_ref.1, f32[1,256]{1,0:T(1,128)} %bitcast.24), custom_call_target="tpu_custom_call" | custom-call | flops 2684354560 | bytes 13893632 | tf_op jit(solution)/shard_map/pallas_call | solution.py:40
  36.9 0.1 copy.25
  37.1 0.1 copy.26
  37.2 6.3 %fusion.2 = bf16[8,512,256]{2,1,0:T(8,128)(2,1)} fusion(bf16[8,1024,256]{2,1,0:T(8,128)(2,1)} %bitcast.18, s32[8,512]{1,0:T(8,128)S(1)} %copy.26), kind=kOutput, calls=%fused_computation.3 | convolution fusion | flops 2152726528 | bytes 6307840 | tf_op jit(solution)/shard_map/dot_general | solution.py:114
  43.4 2.5 %reshape.45 = bf16[8,128,4,256]{3,2,1,0:T(4,128)(2,1)S(1)} reshape(bf16[8,512,256]{2,1,0:T(8,128)(2,1)} %fusion.2) | data formatting | bytes 4194304 | tf_op jit(solution)/shard_map/reshape | solution.py:117
  46.0 2.5 %copy.27 = bf16[128,8,4,256]{3,2,1,0:T(4,128)(2,1)} copy(bf16[128,8,4,256]{3,2,0,1:T(4,128)(2,1)S(1)} %bitcast.15) | data formatting | bytes 4194304 | tf_op jit(solution)/shard_map/transpose | solution.py:117
  48.5 4.0 %reshape.46 = bf16[128,32,256]{2,1,0:T(8,128)(2,1)} reshape(bf16[128,8,4,256]{3,2,1,0:T(4,128)(2,1)} %copy.27) | data formatting | bytes 4194304 | tf_op jit(solution)/shard_map/reshape | solution.py:118
  52.5 33.9 %all-to-all-done.1.x_ref = bf16[8,1024,256]{2,1,0:T(8,128)(2,1)} async-done(((bf16[8,1024,256]{2,1,0:T(8,128)(2,1)}), bf16[8,1024,256]{2,1,0:T(8,128)(2,1)}, u32[]{:S(2)}, u32[]{:S(2)}) %all-to-all-start.1) | async-done | bytes 4194336 | tf_op jit(solution)/shard_map/all_to_all | solution.py:108
  86.4 4.9 %all-to-all-start.2 = ((bf16[128,32,256]{2,1,0:T(8,128)(2,1)}), bf16[128,32,256]{2,1,0:T(8,128)(2,1)S(1)}, u32[]{:S(2)}, u32[]{:S(2)}) async-start(bf16[128,32,256]{2,1,0:T(8,128)(2,1)} %reshape.46), calls=%async_computation.2 | async-start | bytes 4194304 | tf_op jit(solution)/shard_map/all_to_all | solution.py:122
  91.3 0.8 copy.28.s_ref
  92.1 6.6 %shard_map.69 = bf16[1024,2048]{1,0:T(8,128)(2,1)} custom-call(bf16[8,1024,256]{2,1,0:T(8,128)(2,1)} %all-to-all-done.1.x_ref), custom_call_target="tpu_custom_call" | custom-call | bytes 8388608 | tf_op jit(solution)/shard_map/pallas_call | solution.py:19
  98.7 22.3 %all-to-all-done.2 = bf16[128,32,256]{2,1,0:T(8,128)(2,1)S(1)} async-done(((bf16[128,32,256]{2,1,0:T(8,128)(2,1)}), bf16[128,32,256]{2,1,0:T(8,128)(2,1)S(1)}, u32[]{:S(2)}, u32[]{:S(2)}) %all-to-all-start.2) | async-done | bytes 2097184 | tf_op jit(solution)/shard_map/all_to_all | solution.py:122
  121.0 0.0 copy-start
  121.0 1.3 %copy-done = bf16[128,32,256]{2,1,0:T(8,128)(2,1)} copy-done((bf16[128,32,256]{2,1,0:T(8,128)(2,1)}, bf16[128,32,256]{2,1,0:T(8,128)(2,1)S(1)}, u32[]{:S(2)}) %copy-start) | copy-done | bytes 2097176
  122.3 4.7 %shard_map.70 = bf16[256,8,256]{2,1,0:T(8,128)(2,1)} custom-call(s32[256,1]{1,0:T(8,128)} %copy.28.s_ref, bf16[8,512,256]{2,1,0:T(8,128)(2,1)} %bitcast.16, f32[8,256,256]{2,1,0:T(8,128)} %shard_map.68.n_ref), custom_call_target="tpu_custom_call" | custom-call | flops 536870912 | bytes 5242880 | tf_op jit(solution)/shard_map/pallas_call | solution.py:71
  (3 shorter events, 0.0 us)
Async XLA Ops:
  22.2 64.2 %all-to-all-start.1 = ((bf16[8,1024,256]{2,1,0:T(8,128)(2,1)}), bf16[8,1024,256]{2,1,0:T(8,128)(2,1)}, u32[]{:S(2)}, u32[]{:S(2)}) async-start(bf16[8,1024,256]{2,1,0:T(8,128)(2,1)} %bitcast.17), calls=%async_computation.1 | async-start | bytes 8388608 | tf_op jit(solution)/shard_map/all_to_all | solution.py:108
  86.4 34.6 %all-to-all-start.2 = ((bf16[128,32,256]{2,1,0:T(8,128)(2,1)}), bf16[128,32,256]{2,1,0:T(8,128)(2,1)S(1)}, u32[]{:S(2)}, u32[]{:S(2)}) async-start(bf16[128,32,256]{2,1,0:T(8,128)(2,1)} %reshape.46), calls=%async_computation.2 | async-start | bytes 4194304 | tf_op jit(solution)/shard_map/all_to_all | solution.py:122
  121.0 1.3 %copy-start = (bf16[128,32,256]{2,1,0:T(8,128)(2,1)}, bf16[128,32,256]{2,1,0:T(8,128)(2,1)S(1)}, u32[]{:S(2)}) copy-start(bf16[128,32,256]{2,1,0:T(8,128)(2,1)S(1)} %all-to-all-done.2) | copy-start | bytes 6291460

commit v2 on v1

v2 whole, which is shorter than its diff:
```python
import functools
import math

import jax
import jax.numpy as jnp
from jax import lax
from jax.experimental import pallas as pl
from jax.experimental.pallas import tpu as pltpu
from jax.sharding import PartitionSpec as P

CAP = 4
LANES = 128
BOTH = ("grp", "dev")


def flat_index(y, zl, x, zh, c, n_x):
    return (y * 2 + zl) * (n_x * 4) + x * 4 + zh * 2 + c


def send(value, n_y, n_x, dx=0, flip=0, core=0):
    moves = []
    for y in range(n_y):
        for x in range(n_x):
            for rest in range(8):
                zl, zh, c = rest // 4, rest // 2 % 2, rest % 2
                here = flat_index(y, zl, x, zh, c, n_x)
                there = flat_index(y, zl ^ flip, (x + dx) % n_x, zh ^ flip, c ^ core, n_x)
                moves.append((here, there))
    return lax.ppermute(value, BOTH, moves)


def rows_side_by_side(stacked):
    layers, rows, width = stacked.shape

    def body(x_ref, o_ref):
        o_ref[...] = x_ref[0]

    return pl.pallas_call(
        body,
        grid=(layers,),
        in_specs=[pl.BlockSpec((1, rows, width), lambda l: (l, 0, 0))],
        out_specs=pl.BlockSpec((rows, width), lambda l: (0, l)),
        out_shape=jax.ShapeDtypeStruct((rows, layers * width), stacked.dtype),
        cost_estimate=pl.CostEstimate(
            flops=0, bytes_accessed=2 * stacked.size * 2, transcendentals=0
        ),
    )(stacked)


def column_of(line):
    lanes = line.shape[1]
    return jnp.transpose(jnp.broadcast_to(line, (lanes, lanes)))


def onehot_of(line, depth):
    col = column_of(line)
    lane = lax.broadcasted_iota(jnp.int32, col.shape, 1)
    return jnp.concatenate(
        [(col == lane + k * LANES).astype(jnp.bfloat16) for k in range(depth // LANES)], axis=1
    )


def look_up(shard, wanted, n_x, n_grp, first, x_first):
    pairs, lines, lanes = wanted.shape
    rows, width = shard.shape
    depth = rows // pairs
    half = pairs // 2
    run = 2 * CAP
    outs = (n_x, 2) if x_first else (2, n_x)

    def body(w_ref, t_ref, *o_refs):
        for r in range(lines):
            kx, s = r // 2, r % 2
            got = jnp.dot(
                onehot_of(w_ref[0, r : r + 1, :], depth),
                t_ref[...],
                preferred_element_type=jnp.float32,
            )
            got = got.reshape(2, n_grp, run, width).astype(jnp.bfloat16)
            if x_first:
                o_refs[kx][s] = got
            else:
                o_refs[s][kx] = got

    return pl.pallas_call(
        body,
        grid=(half,),
        in_specs=[
            pl.BlockSpec((1, lines, lanes), lambda p: (p + first, 0, 0)),
            pl.BlockSpec((depth, width), lambda p: (p + first, 0)),
        ],
        out_specs=[
            pl.BlockSpec((outs[1], 2, n_grp, run, width), lambda p: (0, 0, 0, p, 0))
        ]
        * outs[0],
        out_shape=[
            jax.ShapeDtypeStruct((outs[1], 2, n_grp, half * run, width), jnp.bfloat16)
        ]
        * outs[0],
        cost_estimate=pl.CostEstimate(
            flops=2 * half * lines * lanes * depth * width,
            bytes_accessed=2 * half * (depth + lines * lanes) * width,
            transcendentals=0,
        ),
    )(wanted, shard)


def in_token_order(own, other, places):
    n_grp, tok = places.shape
    width = own.shape[-1]
    run = own.shape[-2]
    parts = own.size // (n_grp * run * width)
    count = 2 * parts * run

    def body(p_ref, a_ref, b_ref, o_ref):
        rows = jnp.concatenate(
            [a_ref[i, 0] for i in range(parts)] + [b_ref[i, 0] for i in range(parts)], axis=0
        )
        for t in range(tok // LANES):
            line = p_ref[0, :, t * LANES : (t + 1) * LANES]
            got = jnp.dot(onehot_of(line, count), rows, preferred_element_type=jnp.float32)
            o_ref[0, t * LANES : (t + 1) * LANES] = got.astype(jnp.bfloat16)

    piece = pl.BlockSpec((parts, 1, run, width), lambda g: (0, g, 0, 0))
    return pl.pallas_call(
        body,
        grid=(n_grp,),
        in_specs=[pl.BlockSpec((1, 1, tok), lambda g: (g, 0, 0)), piece, piece],
        out_specs=pl.BlockSpec((1, tok, width), lambda g: (g, 0, 0)),
        out_shape=jax.ShapeDtypeStruct((n_grp, tok, width), jnp.bfloat16),
        cost_estimate=pl.CostEstimate(
            flops=2 * n_grp * tok * count * width,
            bytes_accessed=2 * n_grp * (count + tok) * width,
            transcendentals=0,
        ),
    )(
        places.reshape(n_grp, 1, tok),
        own.reshape(parts, n_grp, run, width),
        other.reshape(parts, n_grp, run, width),
    )


def normed_projection(hidden, w_proj, norm_gain, layers):
    tok, depth = hidden.shape
    width = w_proj.shape[1] // layers

    def body(h_ref, w_ref, g_ref, o_ref):
        proj = jnp.dot(h_ref[...], w_ref[...], preferred_element_type=jnp.float32)
        mean_sq = jnp.mean(proj * proj, axis=-1, keepdims=True)
        o_ref[0] = proj / jnp.sqrt(mean_sq + 1e-06) * g_ref[...]

    return pl.pallas_call(
        body,
        grid=(layers,),
        in_specs=[
            pl.BlockSpec((tok, depth), lambda l: (0, 0)),
            pl.BlockSpec((depth, width), lambda l: (0, l)),
            pl.BlockSpec((1, width), lambda l: (0, 0)),
        ],
        out_specs=pl.BlockSpec((1, tok, width), lambda l: (l, 0, 0)),
        out_shape=jax.ShapeDtypeStruct((layers, tok, width), jnp.float32),
        cost_estimate=pl.CostEstimate(
            flops=2 * tok * depth * layers * width,
            bytes_accessed=2 * depth * (tok + layers * width) + 4 * tok * layers * width,
            transcendentals=0,
        ),
    )(hidden, w_proj, norm_gain.reshape(1, width))


def add_embedding(crossed, pieces, normed):
    layers, tok, width = pieces.shape

    def body(s_ref, r_ref, n_ref, o_ref, acc_ref):
        swap = s_ref[...] > 0
        for l in range(layers):
            emb = jnp.where(
                swap, r_ref[l ^ 1].astype(jnp.float32), r_ref[l].astype(jnp.float32)
            )
            acc_ref[:, l, :] = (n_ref[l] + math.sqrt(width) * emb) / math.sqrt(2.0)
        o_ref[...] = acc_ref[...].astype(jnp.bfloat16)

    vmem = pl.BlockSpec(memory_space=pltpu.VMEM)
    return pl.pallas_call(
        body,
        in_specs=[vmem, vmem, vmem],
        out_specs=vmem,
        out_shape=jax.ShapeDtypeStruct((tok, layers, width), jnp.bfloat16),
        scratch_shapes=[pltpu.VMEM((tok, layers, width), jnp.float32)],
        compiler_params=pltpu.CompilerParams(vmem_limit_bytes=16 << 20),
        cost_estimate=pl.CostEstimate(
            flops=6 * tok * layers * width,
            bytes_accessed=8 * layers * width * tok,
            transcendentals=0,
        ),
    )(crossed.reshape(tok, 1), pieces, normed)


def on_device(table, token_ids, hidden, w_proj, norm_gain):
    n_grp = lax.axis_size("grp")
    n_dev = lax.axis_size("dev")
    n_y, n_x = n_grp // 2, n_dev // 4
    peers = n_grp * n_dev
    d_index = lax.axis_index("dev")
    my_x, my_zh, my_c = d_index // 4, d_index // 2 % 2, d_index % 2
    _, shard_rows, width = table.shape
    layers = w_proj.shape[1] // width
    row_count = shard_rows // n_grp
    tok_count = token_ids.shape[0]
    slots = peers * CAP
    dev_slots = slots // n_dev
    pairs = n_grp // 2
    shard = table.reshape(shard_rows, width)
    hop = functools.partial(send, n_y=n_y, n_x=n_x)

    block = token_ids // row_count
    positions = jnp.arange(tok_count, dtype=jnp.int32)
    same = (block[:, None] == block[None, :]) & (positions[None, :] < positions[:, None])
    rank = jnp.sum(same.astype(jnp.int32), axis=1)
    slot = block * CAP + rank
    hit = (slot[:, None] == jnp.arange(slots, dtype=jnp.int32)[None, :]).astype(jnp.int32)
    local = token_ids % (2 * row_count)
    requests = (jnp.sum(hit * (local + 1)[:, None], axis=0) - 1).reshape(1, n_dev, dev_slots)
    holder = block // n_grp
    k = (my_x - holder // 4 + n_x) % n_x
    crossed = (holder // 2 % 2) ^ my_zh
    kc = (holder % 2) ^ my_c
    in_shard = block % n_grp
    half_run = n_grp // 2 * CAP
    place = kc * 2 + in_shard // (n_grp // 2)
    place = (place * 2 + crossed) * n_x + k
    place = place * half_run + in_shard % (n_grp // 2) * CAP + rank
    outgoing = jnp.concatenate(
        [
            jnp.broadcast_to(requests, (n_grp, n_dev, dev_slots)).reshape(peers, dev_slots),
            jnp.broadcast_to(place[None], (peers, tok_count)),
        ],
        axis=1,
    )
    incoming = lax.all_to_all(outgoing, BOTH, split_axis=0, concat_axis=0, tiled=True)

    gated, incoming = lax.optimization_barrier((table.reshape(n_grp, row_count, width), incoming))
    moved = lax.all_to_all(gated, "grp", split_axis=0, concat_axis=0, tiled=True)

    places = lax.dynamic_index_in_dim(
        incoming.reshape(n_grp, n_dev, dev_slots + tok_count)[:, :, dev_slots:], d_index, 1, False
    )
    asked = incoming[:, :dev_slots].reshape(n_grp, n_x, 2, 2, pairs, 2 * CAP)
    asked = lax.dynamic_slice_in_dim(jnp.concatenate([asked, asked], axis=1), my_x, n_x, 1)
    asked = jnp.where(my_zh == 1, asked[:, :, ::-1], asked)
    asked = jnp.where(my_c == 1, asked[:, :, :, ::-1], asked)
    wanted = asked.transpose(4, 1, 2, 3, 0, 5).reshape(pairs, n_x * 2, 2 * n_grp * 2 * CAP)

    to_x = look_up(shard, wanted, n_x, n_grp, 0, True)
    near, far = look_up(shard, wanted, n_x, n_grp, pairs // 2, False)
    a_x = [to_x[0]] + [hop(to_x[q], dx=q) for q in range(1, n_x)]
    b_far = hop(far, flip=1)
    a_far = hop(jnp.stack([a[1] for a in a_x]), flip=1)
    b_x = [jnp.stack([near[0], b_far[0]])]
    for q in range(1, n_x):
        b_x.append(hop(jnp.stack([near[q], b_far[q]]), dx=q))
    held = jnp.stack(
        [
            jnp.stack([jnp.stack([a[0] for a in a_x]), a_far]),
            jnp.stack(b_x, axis=1),
        ]
    )
    own, other = held[:, :, :, 0], hop(held[:, :, :, 1], core=1)
    sorted_rows = in_token_order(own, other, places)
    normed = normed_projection(hidden, w_proj, norm_gain, layers)
    moved, sorted_rows, normed = lax.optimization_barrier((moved, sorted_rows, normed))

    pieces = lax.all_to_all(sorted_rows, "grp", split_axis=0, concat_axis=0, tiled=True)
    served = rows_side_by_side(moved).reshape(1, 1, row_count, layers * width)
    layer_inputs = add_embedding(crossed, pieces, normed)
    return (served, layer_inputs)


def solution(mesh):
    in_specs = (P("grp", "dev", None), P(("grp", "dev")), P(("grp", "dev"), None), P(), P())
    out_specs = (P("dev", "grp", None, None), P(("grp", "dev"), None, None))
    return jax.shard_map(
        on_device, mesh=mesh, in_specs=in_specs, out_specs=out_specs, check_vma=False
    )
```

time: 128 us -> 118 us (0.922)
  starting transfers between devices: 9.44 us -> 33 us
  blocking collectives: 20.4 us -> 0 us
  waiting for transfers between devices: 56.2 us -> 38.9 us
  Pallas kernels: 21.4 us -> 35 us
  matrix products: 6.27 us -> 0 us
  local copies, waits for them, and re-layouts: 11.6 us -> 6.7 us
    all_to_all x1, waiting for transfers between devices: 33.9 us -> 0.01 us  [on_device(): lax.all_to_all(gated, 'grp', split_axis=0, concat_axis=0, tiled=True)]
    all_to_all x1 -> x0, blocking collectives: 20.4 us -> none  [on_device(): lax.all_to_all(outgoing, both, split_axis=0, concat_axis=0, tiled=True)]
    ppermute x0 -> x9, waiting for transfers between devices: none -> 18.2 us  [send(): return lax.ppermute(value, BOTH, moves)]
    pallas_call x1 -> x4, Pallas kernels: 4.71 us -> 18.2 us  [the longest x2 9.3 us: look_up(): pl.pallas_call(body, grid=(half,), in_specs=[pl.BlockSpec((1, lines, lane...]
    ppermute x0 -> x9, starting transfers between devices: none -> 13.2 us  [send(): return lax.ppermute(value, BOTH, moves)]
    all_to_all x1 -> x2, starting transfers between devices: 4.88 us -> 15.3 us  [the longest x1 11.1 us: on_device(): lax.all_to_all(outgoing, BOTH, split_axis=0, concat_axis=0, tiled=True)]
    dot_general x1 -> x0, matrix products: 6.27 us -> none  [on_device(): lax.dot_general(onehot, shard, (((2,), (1,)), ((0,), (0,))), preferred_el...]
    reshape x2 -> x4, local copies, waits for them, and re-layouts: 6.53 us -> 1.1 us  [the longest x1 0.74 us: on_device(): asked.transpose(4, 1, 2, 3, 0, 5)]
  transfers between devices with their start and end apart: 2 -> 12, of which waited for: 2 -> 7; matrix products, arithmetic and copies ran while one was open for 13% -> 4% of each run, Pallas kernels for 13% -> 28%
where the time goes in v2:
time: 118 us; the launch traced here: 117 us
  waiting for transfers between devices  38.9 us (33%)
  Pallas kernels  35 us (30%)
  starting transfers between devices  33 us (28%)
  local copies, waits for them, and re-layouts  6.7 us (6%)
  other arithmetic  2.05 us (2%)
    ppermute x9, waiting for transfers between devices, send(): return lax.ppermute(value, BOTH, moves)  18.2 us
    ppermute x9, starting transfers between devices, send(): return lax.ppermute(value, BOTH, moves)  13.2 us
    all_to_all x1, starting transfers between devices, on_device(): lax.all_to_all(outgoing, BOTH, split_axis=0, concat_axis=0, tiled=True)  11.1 us
    all_to_all x1, waiting for transfers between devices, on_device(): lax.all_to_all(sorted_rows, 'grp', split_axis=0, concat_axis=0, tiled=True)  10.5 us
    all_to_all x1, waiting for transfers between devices, on_device(): lax.all_to_all(outgoing, BOTH, split_axis=0, concat_axis=0, tiled=True)  10.2 us
    pallas_call x1, Pallas kernels, normed_projection(): pl.pallas_call(body, grid=(layers,), in_specs=[pl.BlockSpec((tok, depth),...  10.1 us
    pallas_call x2, Pallas kernels, look_up(): pl.pallas_call(body, grid=(half,), in_specs=[pl.BlockSpec((1, lines, lane...  9.3 us
    pallas_call x1, Pallas kernels, rows_side_by_side(): pl.pallas_call(body, grid=(layers,), in_specs=[pl.BlockSpec((1, rows, wid...  6.73 us
  transfers between devices with their start and end apart: 12, of which 7 were waited for; matrix products, arithmetic and copies ran while one was open for 4% of the time, Pallas kernels for 28%

profile of v2, /device:TPU:0, one launch (start us, length us, event | category | flops | bytes accessed | tf_op | source)
XLA Modules:
  0.0 116.6 jit_solution(17508391119462522458)
XLA Ops:
  2.1 0.8 copy.42
  2.9 11.1 %all-to-all-start = ((s32[128,1,288]{2,1,0:T(1,128)}), s32[128,1,288]{2,1,0:T(1,128)S(1)}, u32[]{:S(2)}, u32[]{:S(2)}) async-start(s32[128,1,288]{2,1,0:T(1,128)} %copy.42), calls=%async_computation | async-start | bytes 393216 | tf_op jit(solution)/shard_map/all_to_all | solution.py:239
  14.1 10.2 %all-to-all-done = s32[128,1,288]{2,1,0:T(1,128)S(1)} async-done(((s32[128,1,288]{2,1,0:T(1,128)}), s32[128,1,288]{2,1,0:T(1,128)S(1)}, u32[]{:S(2)}, u32[]{:S(2)}) %all-to-all-start) | async-done | bytes 147488 | tf_op jit(solution)/shard_map/all_to_all | solution.py:239
  25.9 4.6 %all-to-all-start.1 = ((bf16[8,1024,256]{2,1,0:T(8,128)(2,1)}), bf16[8,1024,256]{2,1,0:T(8,128)(2,1)}, u32[]{:S(2)}, u32[]{:S(2)}) async-start(bf16[8,1024,256]{2,1,0:T(8,128)(2,1)} %bitcast.34), calls=%async_computation.1 | async-start | bytes 8388608 | tf_op jit(solution)/shard_map/all_to_all | solution.py:242
  30.4 4.6 %shard_map.68 = (bf16[2,2,8,16,256]{4,3,2,1,0:T(8,128)(2,1)}, bf16[2,2,8,16,256]{4,3,2,1,0:T(8,128)(2,1)}, bf16[2,2,8,16,256]{4,3,2,1,0:T(8,128)(2,1)}, bf16[2,2,8,16,256]{4,3,2,1,0:T(8,128)(2,1)}) custom-call(s32[4,8,128]{2,1,0:T(8,128)} %reshape.54.w_ref, bf16[8192,256]{1,0:T(8,128)(2,1)} %bitcast.35), custom_call_target="tpu_custom_call" | custom-call | flops 2147483648 | bytes 3145728 | tf_op jit(solution)/shard_map/pallas_call | solution.py:85
  35.0 4.7 %shard_map.69 = (bf16[4,2,8,16,256]{4,3,2,1,0:T(8,128)(2,1)}, bf16[4,2,8,16,256]{4,3,2,1,0:T(8,128)(2,1)}) custom-call(s32[4,8,128]{2,1,0:T(8,128)} %reshape.54.w_ref, bf16[8192,256]{1,0:T(8,128)(2,1)} %bitcast.36), custom_call_target="tpu_custom_call" | custom-call | flops 2147483648 | bytes 3145728 | tf_op jit(solution)/shard_map/pallas_call | solution.py:85
  40.3 2.0 %collective-permute-start.1 = (bf16[2,2,8,16,256]{4,3,2,1,0:T(8,128)(2,1)S(1)}, bf16[2,2,8,16,256]{4,3,2,1,0:T(8,128)(2,1)S(1)}, u32[]{:S(2)}, u32[]{:S(2)}) collective-permute-start(bf16[2,2,8,16,256]{4,3,2,1,0:T(8,128)(2,1)S(1)} %copy-done.3), channel_id=1, source_target_pairs={{0,8},{1,9},{2,10},{3,11},{16,24},{17,25},{18,26},{19,27},{4,12},{... | collective-permute-start | bytes 786440 | tf_op jit(solution)/shard_map/ppermute | solution.py:29
  42.3 1.3 %collective-permute-start.2 = (bf16[2,2,8,16,256]{4,3,2,1,0:T(8,128)(2,1)S(1)}, bf16[2,2,8,16,256]{4,3,2,1,0:T(8,128)(2,1)S(1)}, u32[]{:S(2)}, u32[]{:S(2)}) collective-permute-start(bf16[2,2,8,16,256]{4,3,2,1,0:T(8,128)(2,1)S(1)} %copy-done.2), channel_id=1, source_target_pairs={{0,12},{1,13},{2,14},{3,15},{16,28},{17,29},{18,30},{19,31},{4,0},... | collective-permute-start | bytes 786440 | tf_op jit(solution)/shard_map/ppermute | solution.py:29
  43.6 1.3 %collective-permute-start.4 = (bf16[4,2,8,16,256]{4,3,2,1,0:T(8,128)(2,1)}, bf16[4,2,8,16,256]{4,3,2,1,0:T(8,128)(2,1)S(1)}, u32[]{:S(2)}, u32[]{:S(2)}) collective-permute-start(bf16[4,2,8,16,256]{4,3,2,1,0:T(8,128)(2,1)} %get-tuple-element.20), channel_id=1, source_target_pairs={{0,18},{1,19},{2,16},{3,17},{16,2},{17,3},{18,0},{19,1},{4,22},{5,... | collective-permute-start | bytes 1572872 | tf_op jit(solution)/shard_map/ppermute | solution.py:29
  44.9 1.1 fusion.16
  46.1 8.6 %collective-permute-done = bf16[2,2,8,16,256]{4,3,2,1,0:T(8,128)(2,1)S(1)} collective-permute-done((bf16[2,2,8,16,256]{4,3,2,1,0:T(8,128)(2,1)S(1)}, bf16[2,2,8,16,256]{4,3,2,1,0:T(8,128)(2,1)S(1)}, u32[]{:S(2)}, u32[]{:S(2)}) %collective-permute-start) | collective-permute-done | bytes 262176 | tf_op jit(solution)/shard_map/ppermute | solution.py:29
  55.4 1.7 %collective-permute-start.3 = (bf16[4,2,8,16,256]{4,3,2,1,0:T(8,128)(2,1)S(1)}, bf16[4,2,8,16,256]{4,3,2,1,0:T(8,128)(2,1)S(1)}, u32[]{:S(2)}, u32[]{:S(2)}) collective-permute-start(bf16[4,2,8,16,256]{4,3,2,1,0:T(8,128)(2,1)S(1)} %pad_maximum_fusion.1), channel_id=1, source_target_pairs={{0,18},{1,19},{2,16},{3,17},{16,2},{17,3},{18,0},{19,1},{4,22},{5,... | collective-permute-start | bytes 1572872 | tf_op jit(solution)/shard_map/ppermute | solution.py:29
  58.6 2.8 %collective-permute-start.6 = (bf16[2,2,8,16,256]{4,3,2,1,0:T(8,128)(2,1)S(1)}, bf16[2,2,8,16,256]{4,3,2,1,0:T(8,128)(2,1)S(1)}, u32[]{:S(2)}, u32[]{:S(2)}) collective-permute-start(bf16[2,2,8,16,256]{4,3,2,1,0:T(8,128)(2,1)S(1)} %pad_maximum_fusion.3), channel_id=1, source_target_pairs={{0,8},{1,9},{2,10},{3,11},{16,24},{17,25},{18,26},{19,27},{4,12},{... | collective-permute-start | bytes 786440 | tf_op jit(solution)/shard_map/ppermute | solution.py:29
  61.4 2.7 %collective-permute-start.7 = (bf16[2,2,8,16,256]{4,3,2,1,0:T(8,128)(2,1)S(1)}, bf16[2,2,8,16,256]{4,3,2,1,0:T(8,128)(2,1)S(1)}, u32[]{:S(2)}, u32[]{:S(2)}) collective-permute-start(bf16[2,2,8,16,256]{4,3,2,1,0:T(8,128)(2,1)S(1)} %pad_maximum_fusion.4), channel_id=1, source_target_pairs={{0,12},{1,13},{2,14},{3,15},{16,28},{17,29},{18,30},{19,31},{4,0},... | collective-permute-start | bytes 786440 | tf_op jit(solution)/shard_map/ppermute | solution.py:29
  64.2 5.2 %collective-permute-done.3 = bf16[4,2,8,16,256]{4,3,2,1,0:T(8,128)(2,1)S(1)} collective-permute-done((bf16[4,2,8,16,256]{4,3,2,1,0:T(8,128)(2,1)S(1)}, bf16[4,2,8,16,256]{4,3,2,1,0:T(8,128)(2,1)S(1)}, u32[]{:S(2)}, u32[]{:S(2)}) %collective-permute-start.3) | collective-permute-done | bytes 524320 | tf_op jit(solution)/shard_map/ppermute | solution.py:29
  69.5 3.2 %collective-permute-done.6 = bf16[2,2,8,16,256]{4,3,2,1,0:T(8,128)(2,1)S(1)} collective-permute-done((bf16[2,2,8,16,256]{4,3,2,1,0:T(8,128)(2,1)S(1)}, bf16[2,2,8,16,256]{4,3,2,1,0:T(8,128)(2,1)S(1)}, u32[]{:S(2)}, u32[]{:S(2)}) %collective-permute-start.6) | collective-permute-done | bytes 262176 | tf_op jit(solution)/shard_map/ppermute | solution.py:29
  73.2 10.1 %shard_map.71.n_ref = f32[8,256,256]{2,1,0:T(8,128)} custom-call(bf16[256,2560]{1,0:T(8,128)(2,1)} %h_ref.1, bf16[2560,2048]{1,0:T(8,128)(2,1)} %w_ref.1, f32[1,256]{1,0:T(1,128)} %bitcast.47), custom_call_target="tpu_custom_call" | custom-call | flops 2684354560 | bytes 13893632 | tf_op jit(solution)/shard_map/pallas_call | solution.py:152
  84.1 1.1 copy.48
  85.1 1.1 copy.49
  86.2 6.5 %shard_map.70 = bf16[8,256,256]{2,1,0:T(8,128)(2,1)} custom-call(s32[8,1,256]{2,1,0:T(1,128)} %constant_dynamic-slice_fusion.p_ref, bf16[16,8,16,256]{3,2,1,0:T(8,128)(2,1)} %bitcast.32, bf16[16,8,16,256]{3,2,1,0:T(8,128)(2,1)} %bitcast.33), custom_call_target="tpu_custom_call" | custom-call | flops 536870912 | bytes 3145728 | tf_op jit(solution)/shard_map/pallas_call | solution.py:125
  92.7 4.2 %all-to-all-start.2 = ((bf16[8,256,256]{2,1,0:T(8,128)(2,1)}), bf16[8,256,256]{2,1,0:T(8,128)(2,1)S(1)}, u32[]{:S(2)}, u32[]{:S(2)}) async-start(bf16[8,256,256]{2,1,0:T(8,128)(2,1)} %shard_map.70), calls=%async_computation.2 | async-start | bytes 2097152 | tf_op jit(solution)/shard_map/all_to_all | solution.py:272
  97.1 6.7 %shard_map.72 = bf16[1024,2048]{1,0:T(8,128)(2,1)} custom-call(bf16[8,1024,256]{2,1,0:T(8,128)(2,1)} %all-to-all-done.1.x_ref), custom_call_target="tpu_custom_call" | custom-call | bytes 8388608 | tf_op jit(solution)/shard_map/pallas_call | solution.py:38
  103.8 10.5 %all-to-all-done.2.r_ref = bf16[8,256,256]{2,1,0:T(8,128)(2,1)S(1)} async-done(((bf16[8,256,256]{2,1,0:T(8,128)(2,1)}), bf16[8,256,256]{2,1,0:T(8,128)(2,1)S(1)}, u32[]{:S(2)}, u32[]{:S(2)}) %all-to-all-start.2) | async-done | bytes 1048608 | tf_op jit(solution)/shard_map/all_to_all | solution.py:272
  114.2 2.4 %shard_map.73 = bf16[256,8,256]{2,1,0:T(8,128)(2,1)} custom-call(s32[256,1]{1,0:T(8,128)S(1)} %copy.50.s_ref, bf16[8,256,256]{2,1,0:T(8,128)(2,1)S(1)} %all-to-all-done.2.r_ref, f32[8,256,256]{2,1,0:T(8,128)S(1)} %copy-done), custom_call_target="tpu_custom_call" | custom-call | flops 3145728 | bytes 4194304 | tf_op jit(solution)/shard_map/pallas_call | solution.py:183
  (57 shorter events, 7.3 us)
Async XLA Ops:
  2.9 21.4 %all-to-all-start = ((s32[128,1,288]{2,1,0:T(1,128)}), s32[128,1,288]{2,1,0:T(1,128)S(1)}, u32[]{:S(2)}, u32[]{:S(2)}) async-start(s32[128,1,288]{2,1,0:T(1,128)} %copy.42), calls=%async_computation | async-start | bytes 393216 | tf_op jit(solution)/shard_map/all_to_all | solution.py:239
  25.9 66.9 %all-to-all-start.1 = ((bf16[8,1024,256]{2,1,0:T(8,128)(2,1)}), bf16[8,1024,256]{2,1,0:T(8,128)(2,1)}, u32[]{:S(2)}, u32[]{:S(2)}) async-start(bf16[8,1024,256]{2,1,0:T(8,128)(2,1)} %bitcast.34), calls=%async_computation.1 | async-start | bytes 8388608 | tf_op jit(solution)/shard_map/all_to_all | solution.py:242
  35.0 4.8 %copy-start.4 = (bf16[2,2,8,16,256]{4,3,2,1,0:T(8,128)(2,1)S(1)}, bf16[2,2,8,16,256]{4,3,2,1,0:T(8,128)(2,1)}, u32[]{:S(2)}) copy-start(bf16[2,2,8,16,256]{4,3,2,1,0:T(8,128)(2,1)} %get-tuple-element.16) | copy-start | bytes 786436
  35.0 5.4 %copy-start.3 = (bf16[2,2,8,16,256]{4,3,2,1,0:T(8,128)(2,1)S(1)}, bf16[2,2,8,16,256]{4,3,2,1,0:T(8,128)(2,1)}, u32[]{:S(2)}) copy-start(bf16[2,2,8,16,256]{4,3,2,1,0:T(8,128)(2,1)} %get-tuple-element.17) | copy-start | bytes 786436
  35.0 7.4 %copy-start.2 = (bf16[2,2,8,16,256]{4,3,2,1,0:T(8,128)(2,1)S(1)}, bf16[2,2,8,16,256]{4,3,2,1,0:T(8,128)(2,1)}, u32[]{:S(2)}) copy-start(bf16[2,2,8,16,256]{4,3,2,1,0:T(8,128)(2,1)} %get-tuple-element.18) | copy-start | bytes 786436
  35.0 11.0 %copy-start.1 = (bf16[2,2,8,16,256]{4,3,2,1,0:T(8,128)(2,1)S(1)}, bf16[2,2,8,16,256]{4,3,2,1,0:T(8,128)(2,1)}, u32[]{:S(2)}) copy-start(bf16[2,2,8,16,256]{4,3,2,1,0:T(8,128)(2,1)} %get-tuple-element.15) | copy-start | bytes 786436
  39.7 14.9 %collective-permute-start = (bf16[2,2,8,16,256]{4,3,2,1,0:T(8,128)(2,1)S(1)}, bf16[2,2,8,16,256]{4,3,2,1,0:T(8,128)(2,1)S(1)}, u32[]{:S(2)}, u32[]{:S(2)}) collective-permute-start(bf16[2,2,8,16,256]{4,3,2,1,0:T(8,128)(2,1)S(1)} %copy-done.4), channel_id=1, source_target_pairs={{0,4},{1,5},{2,6},{3,7},{16,20},{17,21},{18,22},{19,23},{4,8},{5,9... | collective-permute-start | bytes 786440 | tf_op jit(solution)/shard_map/ppermute | solution.py:29
  40.3 14.4 %collective-permute-start.1 = (bf16[2,2,8,16,256]{4,3,2,1,0:T(8,128)(2,1)S(1)}, bf16[2,2,8,16,256]{4,3,2,1,0:T(8,128)(2,1)S(1)}, u32[]{:S(2)}, u32[]{:S(2)}) collective-permute-start(bf16[2,2,8,16,256]{4,3,2,1,0:T(8,128)(2,1)S(1)} %copy-done.3), channel_id=1, source_target_pairs={{0,8},{1,9},{2,10},{3,11},{16,24},{17,25},{18,26},{19,27},{4,12},{... | collective-permute-start | bytes 786440 | tf_op jit(solution)/shard_map/ppermute | solution.py:29
  42.3 13.0 %collective-permute-start.2 = (bf16[2,2,8,16,256]{4,3,2,1,0:T(8,128)(2,1)S(1)}, bf16[2,2,8,16,256]{4,3,2,1,0:T(8,128)(2,1)S(1)}, u32[]{:S(2)}, u32[]{:S(2)}) collective-permute-start(bf16[2,2,8,16,256]{4,3,2,1,0:T(8,128)(2,1)S(1)} %copy-done.2), channel_id=1, source_target_pairs={{0,12},{1,13},{2,14},{3,15},{16,28},{17,29},{18,30},{19,31},{4,0},... | collective-permute-start | bytes 786440 | tf_op jit(solution)/shard_map/ppermute | solution.py:29
  43.6 14.1 %collective-permute-start.4 = (bf16[4,2,8,16,256]{4,3,2,1,0:T(8,128)(2,1)}, bf16[4,2,8,16,256]{4,3,2,1,0:T(8,128)(2,1)S(1)}, u32[]{:S(2)}, u32[]{:S(2)}) collective-permute-start(bf16[4,2,8,16,256]{4,3,2,1,0:T(8,128)(2,1)} %get-tuple-element.20), channel_id=1, source_target_pairs={{0,18},{1,19},{2,16},{3,17},{16,2},{17,3},{18,0},{19,1},{4,22},{5,... | collective-permute-start | bytes 1572872 | tf_op jit(solution)/shard_map/ppermute | solution.py:29
  55.4 14.0 %collective-permute-start.3 = (bf16[4,2,8,16,256]{4,3,2,1,0:T(8,128)(2,1)S(1)}, bf16[4,2,8,16,256]{4,3,2,1,0:T(8,128)(2,1)S(1)}, u32[]{:S(2)}, u32[]{:S(2)}) collective-permute-start(bf16[4,2,8,16,256]{4,3,2,1,0:T(8,128)(2,1)S(1)} %pad_maximum_fusion.1), channel_id=1, source_target_pairs={{0,18},{1,19},{2,16},{3,17},{16,2},{17,3},{18,0},{19,1},{4,22},{5,... | collective-permute-start | bytes 1572872 | tf_op jit(solution)/shard_map/ppermute | solution.py:29
  57.8 11.7 %collective-permute-start.5 = (bf16[2,2,8,16,256]{4,3,2,1,0:T(8,128)(2,1)S(1)}, bf16[2,2,8,16,256]{4,3,2,1,0:T(8,128)(2,1)S(1)}, u32[]{:S(2)}, u32[]{:S(2)}) collective-permute-start(bf16[2,2,8,16,256]{4,3,2,1,0:T(8,128)(2,1)S(1)} %pad_maximum_fusion.2), channel_id=1, source_target_pairs={{0,4},{1,5},{2,6},{3,7},{16,20},{17,21},{18,22},{19,23},{4,8},{5,9... | collective-permute-start | bytes 786440 | tf_op jit(solution)/shard_map/ppermute | solution.py:29
  58.6 14.1 %collective-permute-start.6 = (bf16[2,2,8,16,256]{4,3,2,1,0:T(8,128)(2,1)S(1)}, bf16[2,2,8,16,256]{4,3,2,1,0:T(8,128)(2,1)S(1)}, u32[]{:S(2)}, u32[]{:S(2)}) collective-permute-start(bf16[2,2,8,16,256]{4,3,2,1,0:T(8,128)(2,1)S(1)} %pad_maximum_fusion.3), channel_id=1, source_target_pairs={{0,8},{1,9},{2,10},{3,11},{16,24},{17,25},{18,26},{19,27},{4,12},{... | collective-permute-start | bytes 786440 | tf_op jit(solution)/shard_map/ppermute | solution.py:29
  61.4 11.3 %collective-permute-start.7 = (bf16[2,2,8,16,256]{4,3,2,1,0:T(8,128)(2,1)S(1)}, bf16[2,2,8,16,256]{4,3,2,1,0:T(8,128)(2,1)S(1)}, u32[]{:S(2)}, u32[]{:S(2)}) collective-permute-start(bf16[2,2,8,16,256]{4,3,2,1,0:T(8,128)(2,1)S(1)} %pad_maximum_fusion.4), channel_id=1, source_target_pairs={{0,12},{1,13},{2,14},{3,15},{16,28},{17,29},{18,30},{19,31},{4,0},... | collective-permute-start | bytes 786440 | tf_op jit(solution)/shard_map/ppermute | solution.py:29
  73.1 12.1 %collective-permute-start.8 = (bf16[2,2,4,8,16,256]{5,4,3,1,2,0:T(8,128)(2,1)S(1)}, bf16[2,2,4,8,16,256]{5,4,3,1,2,0:T(8,128)(2,1)S(1)}, u32[]{:S(2)}, u32[]{:S(2)}) collective-permute-start(bf16[2,2,4,8,16,256]{5,4,3,1,2,0:T(8,128)(2,1)S(1)} %get-tuple-element.26), channel_id=1, source_target_pairs={{0,1},{1,0},{2,3},{3,2},{16,17},{17,16},{18,19},{19,18},{4,5},{5,4... | collective-permute-start | bytes 3145736 | tf_op jit(solution)/shard_map/ppermute | solution.py:29
  92.7 21.5 %all-to-all-start.2 = ((bf16[8,256,256]{2,1,0:T(8,128)(2,1)}), bf16[8,256,256]{2,1,0:T(8,128)(2,1)S(1)}, u32[]{:S(2)}, u32[]{:S(2)}) async-start(bf16[8,256,256]{2,1,0:T(8,128)(2,1)} %shard_map.70), calls=%async_computation.2 | async-start | bytes 2097152 | tf_op jit(solution)/shard_map/all_to_all | solution.py:272
  97.0 17.2 %copy-start = (f32[8,256,256]{2,1,0:T(8,128)S(1)}, f32[8,256,256]{2,1,0:T(8,128)}, u32[]{:S(2)}) copy-start(f32[8,256,256]{2,1,0:T(8,128)} %shard_map.71.n_ref) | copy-start | bytes 6291460

commit v3 on v2

--- a/solution.py
+++ b/solution.py
@@ -97,47 +97,76 @@
             jax.ShapeDtypeStruct((outs[1], 2, n_grp, half * run, width), jnp.bfloat16)
         ]
         * outs[0],
-        cost_estimate=pl.CostEstimate(
-            flops=2 * half * lines * lanes * depth * width,
-            bytes_accessed=2 * half * (depth + lines * lanes) * width,
-            transcendentals=0,
-        ),
+        cost_estimate=pl.CostEstimate(flops=0, bytes_accessed=1 << 16, transcendentals=0),
     )(wanted, shard)
 
 
-def in_token_order(own, other, places):
+def near_call(body, outs, operands):
+    vmem = pl.BlockSpec(memory_space=pltpu.VMEM)
+    return pl.pallas_call(
+        body,
+        in_specs=[vmem] * len(operands),
+        out_specs=[vmem] * len(outs),
+        out_shape=[jax.ShapeDtypeStruct(shape, jnp.bfloat16) for shape in outs],
+        compiler_params=pltpu.CompilerParams(vmem_limit_bytes=16 << 20),
+        cost_estimate=pl.CostEstimate(flops=0, bytes_accessed=1 << 16, transcendentals=0),
+    )(*operands)
+
+
+def flip_parts(a_x):
+    def body(*refs):
+        for k, ref in enumerate(refs[:-1]):
+            refs[-1][k] = ref[1]
+
+    return near_call(body, [(len(a_x), *a_x[0].shape[1:])], a_x)[0]
+
+
+def x_parts(near, b_far):
+    n_x = near.shape[0]
+
+    def body(n_ref, f_ref, *o_refs):
+        for k, o_ref in enumerate(o_refs):
+            o_ref[0] = n_ref[k + 1]
+            o_ref[1] = f_ref[k + 1]
+
+    return near_call(body, [(2, *near.shape[1:])] * (n_x - 1), [near, b_far])
+
+
+def rows_by_core(refs, n_x, core, pick):
+    a_refs, far_ref, near_ref, b_far_ref = refs[:n_x], refs[n_x], refs[n_x + 1], refs[n_x + 2]
+    b_refs = refs[n_x + 3 : 2 * n_x + 2]
+    rows = [r[(0, core) + pick] for r in a_refs]
+    rows += [far_ref[(k, core) + pick] for k in range(n_x)]
+    for s, ref in ((0, near_ref), (1, b_far_ref)):
+        rows += [ref[(0, core) + pick]] + [r[(s, core) + pick] for r in b_refs]
+    return rows
+
+
+def core_parts(parts, n_x):
+    def body(*refs):
+        for i, rows in enumerate(rows_by_core(refs[:-1], n_x, 1, ())):
+            refs[-1][i] = rows
+
+    return near_call(body, [(4 * n_x, *parts[0].shape[2:])], parts)[0]
+
+
+def in_token_order(places, parts, other, n_x):
     n_grp, tok = places.shape
-    width = own.shape[-1]
-    run = own.shape[-2]
-    parts = own.size // (n_grp * run * width)
-    count = 2 * parts * run
-
-    def body(p_ref, a_ref, b_ref, o_ref):
-        rows = jnp.concatenate(
-            [a_ref[i, 0] for i in range(parts)] + [b_ref[i, 0] for i in range(parts)], axis=0
-        )
-        for t in range(tok // LANES):
-            line = p_ref[0, :, t * LANES : (t + 1) * LANES]
-            got = jnp.dot(onehot_of(line, count), rows, preferred_element_type=jnp.float32)
-            o_ref[0, t * LANES : (t + 1) * LANES] = got.astype(jnp.bfloat16)
-
-    piece = pl.BlockSpec((parts, 1, run, width), lambda g: (0, g, 0, 0))
-    return pl.pallas_call(
-        body,
-        grid=(n_grp,),
-        in_specs=[pl.BlockSpec((1, 1, tok), lambda g: (g, 0, 0)), piece, piece],
-        out_specs=pl.BlockSpec((1, tok, width), lambda g: (g, 0, 0)),
-        out_shape=jax.ShapeDtypeStruct((n_grp, tok, width), jnp.bfloat16),
-        cost_estimate=pl.CostEstimate(
-            flops=2 * n_grp * tok * count * width,
-            bytes_accessed=2 * n_grp * (count + tok) * width,
-            transcendentals=0,
-        ),
-    )(
-        places.reshape(n_grp, 1, tok),
-        own.reshape(parts, n_grp, run, width),
-        other.reshape(parts, n_grp, run, width),
-    )
+    pieces, _, run, width = other.shape
+    count = 2 * pieces * run
+
+    def body(p_ref, *refs):
+        o_ref, other_ref = refs[-1], refs[-2]
+        for g in range(n_grp):
+            rows = rows_by_core(refs[:-2], n_x, 0, (g,))
+            rows += [other_ref[i, g] for i in range(pieces)]
+            rows = jnp.concatenate(rows, axis=0)
+            for t in range(tok // LANES):
+                line = p_ref[g : g + 1, t * LANES : (t + 1) * LANES]
+                got = jnp.dot(onehot_of(line, count), rows, preferred_element_type=jnp.float32)
+                o_ref[g, t * LANES : (t + 1) * LANES] = got.astype(jnp.bfloat16)
+
+    return near_call(body, [(n_grp, tok, width)], [places, *parts, other])[0]
 
 
 def normed_projection(hidden, w_proj, norm_gain, layers):
@@ -238,7 +267,10 @@
     )
     incoming = lax.all_to_all(outgoing, BOTH, split_axis=0, concat_axis=0, tiled=True)
 
-    gated, incoming = lax.optimization_barrier((table.reshape(n_grp, row_count, width), incoming))
+    normed = normed_projection(hidden, w_proj, norm_gain, layers)
+    gated, incoming, normed = lax.optimization_barrier(
+        (table.reshape(n_grp, row_count, width), incoming, normed)
+    )
     moved = lax.all_to_all(gated, "grp", split_axis=0, concat_axis=0, tiled=True)
 
     places = lax.dynamic_index_in_dim(
@@ -250,24 +282,16 @@
     asked = jnp.where(my_c == 1, asked[:, :, :, ::-1], asked)
     wanted = asked.transpose(4, 1, 2, 3, 0, 5).reshape(pairs, n_x * 2, 2 * n_grp * 2 * CAP)
 
-    to_x = look_up(shard, wanted, n_x, n_grp, 0, True)
+    a_x = look_up(shard, wanted, n_x, n_grp, 0, True)
     near, far = look_up(shard, wanted, n_x, n_grp, pairs // 2, False)
-    a_x = [to_x[0]] + [hop(to_x[q], dx=q) for q in range(1, n_x)]
+    a_x = [a_x[0]] + [hop(a_x[q], dx=q) for q in range(1, n_x)]
     b_far = hop(far, flip=1)
-    a_far = hop(jnp.stack([a[1] for a in a_x]), flip=1)
-    b_x = [jnp.stack([near[0], b_far[0]])]
-    for q in range(1, n_x):
-        b_x.append(hop(jnp.stack([near[q], b_far[q]]), dx=q))
-    held = jnp.stack(
-        [
-            jnp.stack([jnp.stack([a[0] for a in a_x]), a_far]),
-            jnp.stack(b_x, axis=1),
-        ]
-    )
-    own, other = held[:, :, :, 0], hop(held[:, :, :, 1], core=1)
-    sorted_rows = in_token_order(own, other, places)
-    normed = normed_projection(hidden, w_proj, norm_gain, layers)
-    moved, sorted_rows, normed = lax.optimization_barrier((moved, sorted_rows, normed))
+    a_far = hop(flip_parts(a_x), flip=1)
+    b_x = [hop(part, dx=q + 1) for q, part in enumerate(x_parts(near, b_far))]
+    parts = [*a_x, a_far, near, b_far, *b_x]
+    other = hop(core_parts(parts, n_x), core=1)
+    sorted_rows = in_token_order(places, parts, other, n_x)
+    moved, sorted_rows = lax.optimization_barrier((moved, sorted_rows))
 
     pieces = lax.all_to_all(sorted_rows, "grp", split_axis=0, concat_axis=0, tiled=True)
     served = rows_side_by_side(moved).reshape(1, 1, row_count, layers * width)

time: 118 us -> 111 us (0.941)
  waiting for transfers between devices: 38.9 us -> 34.4 us
  Pallas kernels: 35 us -> 32.6 us
  starting transfers between devices: 33 us -> 34.9 us
    all_to_all x1, waiting for transfers between devices: 10.2 us -> 0.13 us  [on_device(): lax.all_to_all(outgoing, BOTH, split_axis=0, concat_axis=0, tiled=True)]
    all_to_all x1, waiting for transfers between devices: 0.01 us -> 5.84 us  [on_device(): lax.all_to_all(gated, 'grp', split_axis=0, concat_axis=0, tiled=True)]
    all_to_all x1, waiting for transfers between devices: 10.5 us -> 7.33 us  [on_device(): lax.all_to_all(sorted_rows, 'grp', split_axis=0, concat_axis=0, tiled=True)]
    ppermute x9, waiting for transfers between devices: 18.2 us -> 21.1 us  [send(): return lax.ppermute(value, BOTH, moves)]
    pallas_call x1 -> x4, Pallas kernels: 6.54 us -> 4.11 us  [near_call(): pl.pallas_call(body, in_specs=[vmem] * len(operands), out_specs=[vmem] *...]
    slice x7 -> x0, local copies, waits for them, and re-layouts: 2.3 us -> none  [the longest x2 1.16 us: on_device(): b_x = [jnp.stack([near[0], b_far[0]])]]
    ppermute x9, starting transfers between devices: 13.2 us -> 15.3 us  [send(): return lax.ppermute(value, BOTH, moves)]
  transfers between devices with their start and end apart: 12 -> 12, of which waited for: 7 -> 8; matrix products, arithmetic and copies ran while one was open for 4% -> 4% of each run, Pallas kernels for 28% -> 27%
where the time goes in v3:
time: 111 us
  starting transfers between devices  34.9 us (31%)
  waiting for transfers between devices  34.4 us (31%)
  Pallas kernels  32.6 us (29%)
  local copies, waits for them, and re-layouts  5.95 us (5%)
  other arithmetic  1.96 us (2%)
    ppermute x9, waiting for transfers between devices, send(): return lax.ppermute(value, BOTH, moves)  21.1 us
    ppermute x9, starting transfers between devices, send(): return lax.ppermute(value, BOTH, moves)  15.3 us
    all_to_all x1, starting transfers between devices, on_device(): lax.all_to_all(outgoing, BOTH, split_axis=0, concat_axis=0, tiled=True)  11.1 us
    pallas_call x1, Pallas kernels, normed_projection(): pl.pallas_call(body, grid=(layers,), in_specs=[pl.BlockSpec((tok, depth),...  10.1 us
    pallas_call x2, Pallas kernels, look_up(): pl.pallas_call(body, grid=(half,), in_specs=[pl.BlockSpec((1, lines, lane...  9.29 us
    all_to_all x1, waiting for transfers between devices, on_device(): lax.all_to_all(sorted_rows, 'grp', split_axis=0, concat_axis=0, tiled=True)  7.33 us
    pallas_call x1, Pallas kernels, rows_side_by_side(): pl.pallas_call(body, grid=(layers,), in_specs=[pl.BlockSpec((1, rows, wid...  6.73 us
    all_to_all x1, waiting for transfers between devices, on_device(): lax.all_to_all(gated, 'grp', split_axis=0, concat_axis=0, tiled=True)  5.84 us
  transfers between devices with their start and end apart: 12, of which 8 were waited for; matrix products, arithmetic and copies ran while one was open for 4% of the time, Pallas kernels for 27%

profile of v3, /device:TPU:0, one launch (start us, length us, event | category | flops | bytes accessed | tf_op | source)
XLA Modules:
  0.0 110.7 jit_solution(964725273623752868)
XLA Ops:
  3.5 11.1 %all-to-all-start = ((s32[128,1,288]{2,1,0:T(1,128)}), s32[128,1,288]{2,1,0:T(1,128)S(1)}, u32[]{:S(2)}, u32[]{:S(2)}) async-start(s32[128,1,288]{2,1,0:T(1,128)} %copy.25), calls=%async_computation | async-start | bytes 393216 | tf_op jit(solution)/shard_map/all_to_all | solution.py:268
  14.6 10.1 %shard_map.68.n_ref = f32[8,256,256]{2,1,0:T(8,128)} custom-call(bf16[256,2560]{1,0:T(8,128)(2,1)} %h_ref.1, bf16[2560,2048]{1,0:T(8,128)(2,1)} %w_ref.1, f32[1,256]{1,0:T(1,128)} %bitcast.27), custom_call_target="tpu_custom_call" | custom-call | flops 2684354560 | bytes 13893632 | tf_op jit(solution)/shard_map/pallas_call | solution.py:181
  25.0 4.8 %all-to-all-start.1 = ((bf16[8,1024,256]{2,1,0:T(8,128)(2,1)}), bf16[8,1024,256]{2,1,0:T(8,128)(2,1)}, u32[]{:S(2)}, u32[]{:S(2)}) async-start(bf16[8,1024,256]{2,1,0:T(8,128)(2,1)} %bitcast.18), calls=%async_computation.1 | async-start | bytes 8388608 | tf_op jit(solution)/shard_map/all_to_all | solution.py:274
  31.2 4.6 %shard_map.71 = (bf16[4,2,8,16,256]{4,3,2,1,0:T(8,128)(2,1)}, bf16[4,2,8,16,256]{4,3,2,1,0:T(8,128)(2,1)}) custom-call(s32[4,8,128]{2,1,0:T(8,128)} %reshape.51.w_ref, bf16[8192,256]{1,0:T(8,128)(2,1)} %bitcast.19), custom_call_target="tpu_custom_call" | custom-call | bytes 65536 | tf_op jit(solution)/shard_map/pallas_call | solution.py:85
  35.8 4.6 %shard_map.69 = (bf16[2,2,8,16,256]{4,3,2,1,0:T(8,128)(2,1)}, bf16[2,2,8,16,256]{4,3,2,1,0:T(8,128)(2,1)}, bf16[2,2,8,16,256]{4,3,2,1,0:T(8,128)(2,1)}, bf16[2,2,8,16,256]{4,3,2,1,0:T(8,128)(2,1)}) custom-call(s32[4,8,128]{2,1,0:T(8,128)} %reshape.51.w_ref, bf16[8192,256]{1,0:T(8,128)(2,1)} %bitcast.20), custom_call_target="tpu_custom_call" | custom-call | bytes 65536 | tf_op jit(solution)/shard_map/pallas_call | solution.py:85
  40.5 3.8 %collective-permute-start.4 = (bf16[4,2,8,16,256]{4,3,2,1,0:T(8,128)(2,1)S(1)}, bf16[4,2,8,16,256]{4,3,2,1,0:T(8,128)(2,1)S(1)}, u32[]{:S(2)}, u32[]{:S(2)}) collective-permute-start(bf16[4,2,8,16,256]{4,3,2,1,0:T(8,128)(2,1)S(1)} %copy-done.4), channel_id=1, source_target_pairs={{0,18},{1,19},{2,16},{3,17},{16,2},{17,3},{18,0},{19,1},{4,22},{5,... | collective-permute-start | bytes 1572872 | tf_op jit(solution)/shard_map/ppermute | solution.py:29
  44.3 1.5 %collective-permute-start = (bf16[2,2,8,16,256]{4,3,2,1,0:T(8,128)(2,1)}, bf16[2,2,8,16,256]{4,3,2,1,0:T(8,128)(2,1)S(1)}, u32[]{:S(2)}, u32[]{:S(2)}) collective-permute-start(bf16[2,2,8,16,256]{4,3,2,1,0:T(8,128)(2,1)} %get-tuple-element.19), channel_id=1, source_target_pairs={{0,4},{1,5},{2,6},{3,7},{16,20},{17,21},{18,22},{19,23},{4,8},{5,9... | collective-permute-start | bytes 786440 | tf_op jit(solution)/shard_map/ppermute | solution.py:29
  45.8 2.7 %collective-permute-start.1 = (bf16[2,2,8,16,256]{4,3,2,1,0:T(8,128)(2,1)}, bf16[2,2,8,16,256]{4,3,2,1,0:T(8,128)(2,1)S(1)}, u32[]{:S(2)}, u32[]{:S(2)}) collective-permute-start(bf16[2,2,8,16,256]{4,3,2,1,0:T(8,128)(2,1)} %get-tuple-element.20), channel_id=1, source_target_pairs={{0,8},{1,9},{2,10},{3,11},{16,24},{17,25},{18,26},{19,27},{4,12},{... | collective-permute-start | bytes 786440 | tf_op jit(solution)/shard_map/ppermute | solution.py:29
  48.5 1.4 %collective-permute-start.2 = (bf16[2,2,8,16,256]{4,3,2,1,0:T(8,128)(2,1)}, bf16[2,2,8,16,256]{4,3,2,1,0:T(8,128)(2,1)S(1)}, u32[]{:S(2)}, u32[]{:S(2)}) collective-permute-start(bf16[2,2,8,16,256]{4,3,2,1,0:T(8,128)(2,1)} %get-tuple-element.21), channel_id=1, source_target_pairs={{0,12},{1,13},{2,14},{3,15},{16,28},{17,29},{18,30},{19,31},{4,0},... | collective-permute-start | bytes 786440 | tf_op jit(solution)/shard_map/ppermute | solution.py:29
  50.0 4.1 %collective-permute-done.refs_1_ = bf16[2,2,8,16,256]{4,3,2,1,0:T(8,128)(2,1)S(1)} collective-permute-done((bf16[2,2,8,16,256]{4,3,2,1,0:T(8,128)(2,1)}, bf16[2,2,8,16,256]{4,3,2,1,0:T(8,128)(2,1)S(1)}, u32[]{:S(2)}, u32[]{:S(2)}) %collective-permute-start) | collective-permute-done | bytes 262176 | tf_op jit(solution)/shard_map/ppermute | solution.py:29
  54.0 5.8 %collective-permute-done.1.refs_2_ = bf16[2,2,8,16,256]{4,3,2,1,0:T(8,128)(2,1)S(1)} collective-permute-done((bf16[2,2,8,16,256]{4,3,2,1,0:T(8,128)(2,1)}, bf16[2,2,8,16,256]{4,3,2,1,0:T(8,128)(2,1)S(1)}, u32[]{:S(2)}, u32[]{:S(2)}) %collective-permute-start.1) | collective-permute-done | bytes 262176 | tf_op jit(solution)/shard_map/ppermute | solution.py:29
  61.3 1.4 %collective-permute-start.5 = (bf16[2,2,8,16,256]{4,3,2,1,0:T(8,128)(2,1)S(1)}, bf16[2,2,8,16,256]{4,3,2,1,0:T(8,128)(2,1)S(1)}, u32[]{:S(2)}, u32[]{:S(2)}) collective-permute-start(bf16[2,2,8,16,256]{4,3,2,1,0:T(8,128)(2,1)S(1)} %get-tuple-element.24), channel_id=1, source_target_pairs={{0,4},{1,5},{2,6},{3,7},{16,20},{17,21},{18,22},{19,23},{4,8},{5,9... | collective-permute-start | bytes 786440 | tf_op jit(solution)/shard_map/ppermute | solution.py:29
  62.8 2.4 %collective-permute-start.6 = (bf16[2,2,8,16,256]{4,3,2,1,0:T(8,128)(2,1)S(1)}, bf16[2,2,8,16,256]{4,3,2,1,0:T(8,128)(2,1)S(1)}, u32[]{:S(2)}, u32[]{:S(2)}) collective-permute-start(bf16[2,2,8,16,256]{4,3,2,1,0:T(8,128)(2,1)S(1)} %get-tuple-element.25), channel_id=1, source_target_pairs={{0,8},{1,9},{2,10},{3,11},{16,24},{17,25},{18,26},{19,27},{4,12},{... | collective-permute-start | bytes 786440 | tf_op jit(solution)/shard_map/ppermute | solution.py:29
  65.2 1.5 %collective-permute-start.7 = (bf16[2,2,8,16,256]{4,3,2,1,0:T(8,128)(2,1)S(1)}, bf16[2,2,8,16,256]{4,3,2,1,0:T(8,128)(2,1)S(1)}, u32[]{:S(2)}, u32[]{:S(2)}) collective-permute-start(bf16[2,2,8,16,256]{4,3,2,1,0:T(8,128)(2,1)S(1)} %get-tuple-element.26), channel_id=1, source_target_pairs={{0,12},{1,13},{2,14},{3,15},{16,28},{17,29},{18,30},{19,31},{4,0},... | collective-permute-start | bytes 786440 | tf_op jit(solution)/shard_map/ppermute | solution.py:29
  66.7 3.3 %collective-permute-done.5.refs_7_ = bf16[2,2,8,16,256]{4,3,2,1,0:T(8,128)(2,1)S(1)} collective-permute-done((bf16[2,2,8,16,256]{4,3,2,1,0:T(8,128)(2,1)S(1)}, bf16[2,2,8,16,256]{4,3,2,1,0:T(8,128)(2,1)S(1)}, u32[]{:S(2)}, u32[]{:S(2)}) %collective-permute-start.5) | collective-permute-done | bytes 262176 | tf_op jit(solution)/shard_map/ppermute | solution.py:29
  70.0 6.8 %collective-permute-done.6.refs_8_ = bf16[2,2,8,16,256]{4,3,2,1,0:T(8,128)(2,1)S(1)} collective-permute-done((bf16[2,2,8,16,256]{4,3,2,1,0:T(8,128)(2,1)S(1)}, bf16[2,2,8,16,256]{4,3,2,1,0:T(8,128)(2,1)S(1)}, u32[]{:S(2)}, u32[]{:S(2)}) %collective-permute-start.6) | collective-permute-done | bytes 262176 | tf_op jit(solution)/shard_map/ppermute | solution.py:29
  76.8 1.0 shard_map.73
  79.7 1.1 %collective-permute-done.8.refs_10_ = bf16[16,8,16,256]{3,2,1,0:T(8,128)(2,1)} collective-permute-done((bf16[16,8,16,256]{3,2,1,0:T(8,128)(2,1)}, bf16[16,8,16,256]{3,2,1,0:T(8,128)(2,1)}, u32[]{:S(2)}, u32[]{:S(2)}) %collective-permute-start.8) | collective-permute-done | bytes 1048608 | tf_op jit(solution)/shard_map/ppermute | solution.py:29
  80.8 3.0 %shard_map.74 = bf16[8,256,256]{2,1,0:T(8,128)(2,1)} custom-call(s32[8,256]{1,0:T(8,128)S(1)} %bitcast.17, bf16[2,2,8,16,256]{4,3,2,1,0:T(8,128)(2,1)S(1)} %copy-done.3, bf16[2,2,8,16,256]{4,3,2,1,0:T(8,128)(2,1)S(1)} %collective-permute-done.refs_1_, bf16[2,2,8,16,256]{4,3,2,1,0:T(8,128)(2,1)S(1)} %collective-permute-done.1.refs_2_, ...), custom_call_target="tpu_custom_call" | custom-call | bytes 65536 | tf_op jit(solution)/shard_map/pallas_call | solution.py:106
  83.8 5.8 %all-to-all-done.1.x_ref = bf16[8,1024,256]{2,1,0:T(8,128)(2,1)} async-done(((bf16[8,1024,256]{2,1,0:T(8,128)(2,1)}), bf16[8,1024,256]{2,1,0:T(8,128)(2,1)}, u32[]{:S(2)}, u32[]{:S(2)}) %all-to-all-start.1) | async-done | bytes 4194336 | tf_op jit(solution)/shard_map/all_to_all | solution.py:274
  89.7 3.7 %all-to-all-start.2 = ((bf16[8,256,256]{2,1,0:T(8,128)(2,1)}), bf16[8,256,256]{2,1,0:T(8,128)(2,1)S(1)}, u32[]{:S(2)}, u32[]{:S(2)}) async-start(bf16[8,256,256]{2,1,0:T(8,128)(2,1)} %shard_map.74), calls=%async_computation.2 | async-start | bytes 2097152 | tf_op jit(solution)/shard_map/all_to_all | solution.py:296
  94.2 6.7 %shard_map.75 = bf16[1024,2048]{1,0:T(8,128)(2,1)} custom-call(bf16[8,1024,256]{2,1,0:T(8,128)(2,1)} %all-to-all-done.1.x_ref), custom_call_target="tpu_custom_call" | custom-call | bytes 8388608 | tf_op jit(solution)/shard_map/pallas_call | solution.py:38
  100.9 7.3 %all-to-all-done.2.r_ref = bf16[8,256,256]{2,1,0:T(8,128)(2,1)S(1)} async-done(((bf16[8,256,256]{2,1,0:T(8,128)(2,1)}), bf16[8,256,256]{2,1,0:T(8,128)(2,1)S(1)}, u32[]{:S(2)}, u32[]{:S(2)}) %all-to-all-start.2) | async-done | bytes 1048608 | tf_op jit(solution)/shard_map/all_to_all | solution.py:296
  108.3 2.4 %shard_map.76 = bf16[256,8,256]{2,1,0:T(8,128)(2,1)} custom-call(s32[256,1]{1,0:T(8,128)S(1)} %copy.30.s_ref, bf16[8,256,256]{2,1,0:T(8,128)(2,1)S(1)} %all-to-all-done.2.r_ref, f32[8,256,256]{2,1,0:T(8,128)S(1)} %copy-done), custom_call_target="tpu_custom_call" | custom-call | flops 3145728 | bytes 4194304 | tf_op jit(solution)/shard_map/pallas_call | solution.py:212
  (44 shorter events, 8.6 us)
Async XLA Ops:
  3.5 21.4 %all-to-all-start = ((s32[128,1,288]{2,1,0:T(1,128)}), s32[128,1,288]{2,1,0:T(1,128)S(1)}, u32[]{:S(2)}, u32[]{:S(2)}) async-start(s32[128,1,288]{2,1,0:T(1,128)} %copy.25), calls=%async_computation | async-start | bytes 393216 | tf_op jit(solution)/shard_map/all_to_all | solution.py:268
  25.0 64.7 %all-to-all-start.1 = ((bf16[8,1024,256]{2,1,0:T(8,128)(2,1)}), bf16[8,1024,256]{2,1,0:T(8,128)(2,1)}, u32[]{:S(2)}, u32[]{:S(2)}) async-start(bf16[8,1024,256]{2,1,0:T(8,128)(2,1)} %bitcast.18), calls=%async_computation.1 | async-start | bytes 8388608 | tf_op jit(solution)/shard_map/all_to_all | solution.py:274
  35.8 4.7 %copy-start.4 = (bf16[4,2,8,16,256]{4,3,2,1,0:T(8,128)(2,1)S(1)}, bf16[4,2,8,16,256]{4,3,2,1,0:T(8,128)(2,1)}, u32[]{:S(2)}) copy-start(bf16[4,2,8,16,256]{4,3,2,1,0:T(8,128)(2,1)} %get-tuple-element.23) | copy-start | bytes 1572868
  35.8 25.4 %copy-start.1 = (bf16[4,2,8,16,256]{4,3,2,1,0:T(8,128)(2,1)S(1)}, bf16[4,2,8,16,256]{4,3,2,1,0:T(8,128)(2,1)}, u32[]{:S(2)}) copy-start(bf16[4,2,8,16,256]{4,3,2,1,0:T(8,128)(2,1)} %get-tuple-element.22.n_ref.refs_5_) | copy-start | bytes 1572868
  40.5 20.8 %collective-permute-start.4 = (bf16[4,2,8,16,256]{4,3,2,1,0:T(8,128)(2,1)S(1)}, bf16[4,2,8,16,256]{4,3,2,1,0:T(8,128)(2,1)S(1)}, u32[]{:S(2)}, u32[]{:S(2)}) collective-permute-start(bf16[4,2,8,16,256]{4,3,2,1,0:T(8,128)(2,1)S(1)} %copy-done.4), channel_id=1, source_target_pairs={{0,18},{1,19},{2,16},{3,17},{16,2},{17,3},{18,0},{19,1},{4,22},{5,... | collective-permute-start | bytes 1572872 | tf_op jit(solution)/shard_map/ppermute | solution.py:29
  44.3 9.7 %collective-permute-start = (bf16[2,2,8,16,256]{4,3,2,1,0:T(8,128)(2,1)}, bf16[2,2,8,16,256]{4,3,2,1,0:T(8,128)(2,1)S(1)}, u32[]{:S(2)}, u32[]{:S(2)}) collective-permute-start(bf16[2,2,8,16,256]{4,3,2,1,0:T(8,128)(2,1)} %get-tuple-element.19), channel_id=1, source_target_pairs={{0,4},{1,5},{2,6},{3,7},{16,20},{17,21},{18,22},{19,23},{4,8},{5,9... | collective-permute-start | bytes 786440 | tf_op jit(solution)/shard_map/ppermute | solution.py:29
  45.8 14.0 %collective-permute-start.1 = (bf16[2,2,8,16,256]{4,3,2,1,0:T(8,128)(2,1)}, bf16[2,2,8,16,256]{4,3,2,1,0:T(8,128)(2,1)S(1)}, u32[]{:S(2)}, u32[]{:S(2)}) collective-permute-start(bf16[2,2,8,16,256]{4,3,2,1,0:T(8,128)(2,1)} %get-tuple-element.20), channel_id=1, source_target_pairs={{0,8},{1,9},{2,10},{3,11},{16,24},{17,25},{18,26},{19,27},{4,12},{... | collective-permute-start | bytes 786440 | tf_op jit(solution)/shard_map/ppermute | solution.py:29
  48.5 11.3 %collective-permute-start.2 = (bf16[2,2,8,16,256]{4,3,2,1,0:T(8,128)(2,1)}, bf16[2,2,8,16,256]{4,3,2,1,0:T(8,128)(2,1)S(1)}, u32[]{:S(2)}, u32[]{:S(2)}) collective-permute-start(bf16[2,2,8,16,256]{4,3,2,1,0:T(8,128)(2,1)} %get-tuple-element.21), channel_id=1, source_target_pairs={{0,12},{1,13},{2,14},{3,15},{16,28},{17,29},{18,30},{19,31},{4,0},... | collective-permute-start | bytes 786440 | tf_op jit(solution)/shard_map/ppermute | solution.py:29
  59.8 1.0 copy-start.2
  60.8 20.1 %copy-start.3 = (bf16[2,2,8,16,256]{4,3,2,1,0:T(8,128)(2,1)S(1)}, bf16[2,2,8,16,256]{4,3,2,1,0:T(8,128)(2,1)}, u32[]{:S(2)}) copy-start(bf16[2,2,8,16,256]{4,3,2,1,0:T(8,128)(2,1)} %get-tuple-element.18.refs_0_) | copy-start | bytes 786436
  60.8 16.0 %collective-permute-start.3 = (bf16[4,2,8,16,256]{4,3,2,1,0:T(8,128)(2,1)S(1)}, bf16[4,2,8,16,256]{4,3,2,1,0:T(8,128)(2,1)S(1)}, u32[]{:S(2)}, u32[]{:S(2)}) collective-permute-start(bf16[4,2,8,16,256]{4,3,2,1,0:T(8,128)(2,1)S(1)} %shard_map.70), channel_id=1, source_target_pairs={{0,18},{1,19},{2,16},{3,17},{16,2},{17,3},{18,0},{19,1},{4,22},{5,... | collective-permute-start | bytes 1572872 | tf_op jit(solution)/shard_map/ppermute | solution.py:29
  61.3 8.7 %collective-permute-start.5 = (bf16[2,2,8,16,256]{4,3,2,1,0:T(8,128)(2,1)S(1)}, bf16[2,2,8,16,256]{4,3,2,1,0:T(8,128)(2,1)S(1)}, u32[]{:S(2)}, u32[]{:S(2)}) collective-permute-start(bf16[2,2,8,16,256]{4,3,2,1,0:T(8,128)(2,1)S(1)} %get-tuple-element.24), channel_id=1, source_target_pairs={{0,4},{1,5},{2,6},{3,7},{16,20},{17,21},{18,22},{19,23},{4,8},{5,9... | collective-permute-start | bytes 786440 | tf_op jit(solution)/shard_map/ppermute | solution.py:29
  62.8 14.0 %collective-permute-start.6 = (bf16[2,2,8,16,256]{4,3,2,1,0:T(8,128)(2,1)S(1)}, bf16[2,2,8,16,256]{4,3,2,1,0:T(8,128)(2,1)S(1)}, u32[]{:S(2)}, u32[]{:S(2)}) collective-permute-start(bf16[2,2,8,16,256]{4,3,2,1,0:T(8,128)(2,1)S(1)} %get-tuple-element.25), channel_id=1, source_target_pairs={{0,8},{1,9},{2,10},{3,11},{16,24},{17,25},{18,26},{19,27},{4,12},{... | collective-permute-start | bytes 786440 | tf_op jit(solution)/shard_map/ppermute | solution.py:29
  65.2 11.6 %collective-permute-start.7 = (bf16[2,2,8,16,256]{4,3,2,1,0:T(8,128)(2,1)S(1)}, bf16[2,2,8,16,256]{4,3,2,1,0:T(8,128)(2,1)S(1)}, u32[]{:S(2)}, u32[]{:S(2)}) collective-permute-start(bf16[2,2,8,16,256]{4,3,2,1,0:T(8,128)(2,1)S(1)} %get-tuple-element.26), channel_id=1, source_target_pairs={{0,12},{1,13},{2,14},{3,15},{16,28},{17,29},{18,30},{19,31},{4,0},... | collective-permute-start | bytes 786440 | tf_op jit(solution)/shard_map/ppermute | solution.py:29
  77.8 3.0 %collective-permute-start.8 = (bf16[16,8,16,256]{3,2,1,0:T(8,128)(2,1)}, bf16[16,8,16,256]{3,2,1,0:T(8,128)(2,1)}, u32[]{:S(2)}, u32[]{:S(2)}) collective-permute-start(bf16[16,8,16,256]{3,2,1,0:T(8,128)(2,1)} %shard_map.73), channel_id=1, source_target_pairs={{0,1},{1,0},{2,3},{3,2},{16,17},{17,16},{18,19},{19,18},{4,5},{5,4... | collective-permute-start | bytes 3145736 | tf_op jit(solution)/shard_map/ppermute | solution.py:29
  89.7 18.6 %all-to-all-start.2 = ((bf16[8,256,256]{2,1,0:T(8,128)(2,1)}), bf16[8,256,256]{2,1,0:T(8,128)(2,1)S(1)}, u32[]{:S(2)}, u32[]{:S(2)}) async-start(bf16[8,256,256]{2,1,0:T(8,128)(2,1)} %shard_map.74), calls=%async_computation.2 | async-start | bytes 2097152 | tf_op jit(solution)/shard_map/all_to_all | solution.py:296
  94.2 14.1 %copy-start = (f32[8,256,256]{2,1,0:T(8,128)S(1)}, f32[8,256,256]{2,1,0:T(8,128)}, u32[]{:S(2)}) copy-start(f32[8,256,256]{2,1,0:T(8,128)} %shard_map.68.n_ref) | copy-start | bytes 6291460

commit v4 on v3

v4 whole, which is shorter than its diff:
```python
import functools
import math

import jax
import jax.numpy as jnp
from jax import lax
from jax.experimental import pallas as pl
from jax.experimental.pallas import tpu as pltpu
from jax.sharding import PartitionSpec as P

CAP = 4
LANES = 128
BOTH = ("grp", "dev")


def flat_index(y, zl, x, zh, c, n_x):
    return (y * 2 + zl) * (n_x * 4) + x * 4 + zh * 2 + c


def send(value, n_y, n_x, dx=0, flip=0, core=0):
    moves = []
    for y in range(n_y):
        for x in range(n_x):
            for rest in range(8):
                zl, zh, c = rest // 4, rest // 2 % 2, rest % 2
                here = flat_index(y, zl, x, zh, c, n_x)
                there = flat_index(y, zl ^ flip, (x + dx) % n_x, zh ^ flip, c ^ core, n_x)
                moves.append((here, there))
    return lax.ppermute(value, BOTH, moves)


def column_of(line):
    lanes = line.shape[1]
    return jnp.transpose(jnp.broadcast_to(line, (lanes, lanes)))


def onehot_of(line, depth):
    col = column_of(line)
    lane = lax.broadcasted_iota(jnp.int32, col.shape, 1)
    return jnp.concatenate(
        [(col == lane + k * LANES).astype(jnp.bfloat16) for k in range(depth // LANES)], axis=1
    )


def look_up(shard, wanted, n_x, n_grp, x_first):
    blocks, lines, lanes = wanted.shape
    rows, width = shard.shape
    depth = rows // blocks
    half = blocks // 2
    duo = n_grp // 2
    outs = (n_x, 2) if x_first else (2, n_x)
    from_line, from_row = (0, half) if x_first else (half, 0)

    def body(w_ref, t_ref, *o_refs):
        for b in range(half):
            onehot = jnp.concatenate(
                [onehot_of(w_ref[from_line + b, r : r + 1, :], depth) for r in range(lines)],
                axis=0,
            )
            first = (from_row + b) * depth
            got = jnp.dot(
                onehot, t_ref[first : first + depth], preferred_element_type=jnp.float32
            )
            got = got.reshape(n_x, 2, 2, duo, 2 * CAP, width).astype(jnp.bfloat16)
            for k in range(n_x):
                for s in range(2):
                    if x_first:
                        o_refs[k][s, :, :, b] = got[k, s]
                    else:
                        o_refs[s][k, :, :, b] = got[k, s]

    shape = (outs[1], 2, duo, half, 2 * CAP, width)
    return near_call(body, [shape] * outs[0], [wanted, shard])


def near_call(body, outs, operands):
    vmem = pl.BlockSpec(memory_space=pltpu.VMEM)
    return pl.pallas_call(
        body,
        in_specs=[vmem] * len(operands),
        out_specs=[vmem] * len(outs),
        out_shape=[jax.ShapeDtypeStruct(shape, jnp.bfloat16) for shape in outs],
        compiler_params=pltpu.CompilerParams(vmem_limit_bytes=16 << 20),
        cost_estimate=pl.CostEstimate(flops=0, bytes_accessed=1 << 16, transcendentals=0),
    )(*operands)


def flip_parts(a_x):
    def body(*refs):
        for k, ref in enumerate(refs[:-1]):
            refs[-1][k] = ref[1]

    return near_call(body, [(len(a_x), *a_x[0].shape[1:])], a_x)[0]


def x_parts(near, b_far):
    n_x = near.shape[0]

    def body(n_ref, f_ref, *o_refs):
        for k, o_ref in enumerate(o_refs):
            o_ref[0] = n_ref[k + 1]
            o_ref[1] = f_ref[k + 1]

    return near_call(body, [(2, *near.shape[1:])] * (n_x - 1), [near, b_far])


def rows_by_core(refs, n_x, core, pick):
    a_refs, far_ref, near_ref, b_far_ref = refs[:n_x], refs[n_x], refs[n_x + 1], refs[n_x + 2]
    b_refs = refs[n_x + 3 : 2 * n_x + 2]
    rows = [r[(0, core) + pick] for r in a_refs]
    rows += [far_ref[(k, core) + pick] for k in range(n_x)]
    for s, ref in ((0, near_ref), (1, b_far_ref)):
        rows += [ref[(0, core) + pick]] + [r[(s, core) + pick] for r in b_refs]
    return rows


def core_parts(parts, n_x):
    def body(*refs):
        for i, rows in enumerate(rows_by_core(refs[:-1], n_x, 1, ())):
            refs[-1][i] = rows

    return near_call(body, [(4 * n_x, *parts[0].shape[2:])], parts)[0]


def in_token_order(places, parts, other, n_x):
    n_grp, tok = places.shape
    pieces, duo, blocks, run, width = other.shape
    count = 2 * pieces * blocks * run
    together = n_grp // duo

    def body(p_ref, *refs):
        o_ref, other_ref = refs[-1], refs[-2]
        for u in range(duo):
            rows = rows_by_core(refs[:-2], n_x, 0, (u,))
            rows += [other_ref[i, u] for i in range(pieces)]
            rows = jnp.concatenate([r.reshape(blocks * run, width) for r in rows], axis=0)
            for g in range(u * together, (u + 1) * together):
                onehot = jnp.concatenate(
                    [
                        onehot_of(p_ref[g : g + 1, t : t + LANES], count)
                        for t in range(0, tok, LANES)
                    ],
                    axis=0,
                )
                got = jnp.dot(onehot, rows, preferred_element_type=jnp.float32)
                o_ref[g] = got.astype(jnp.bfloat16)

    return near_call(body, [(n_grp, tok, width)], [places, *parts, other])[0]


def serve_and_project(stacked, hidden, w_proj, norm_gain):
    layers, rows, width = stacked.shape
    tok, depth = hidden.shape
    columns = w_proj.shape[1]
    steps = 5
    part = depth // steps

    def body(m_ref, h_hbm, w_ref, g_ref, s_ref, o_ref, *scratch):
        held, h_ref, weights, acc_ref, m_sem, s_sem, w_sem, h_sem = scratch
        loads, reads, writes = [], [], []
        states = pltpu.make_async_copy(h_hbm, h_ref, h_sem)
        states.start()
        for q in range(steps):
            rows_q = w_ref.at[q * part : (q + 1) * part]
            loads.append(pltpu.make_async_copy(rows_q, weights.at[q], w_sem.at[q]))
            loads[q].start()
        for l in range(layers):
            reads.append(pltpu.make_async_copy(m_ref.at[l], held.at[l], m_sem.at[l]))
            reads[l].start()
            block = s_ref.at[:, l * width : (l + 1) * width]
            writes.append(pltpu.make_async_copy(held.at[l], block, s_sem.at[l]))
        states.wait()
        for q in range(steps):
            loads[q].wait()
            term = jnp.dot(
                h_ref[:, q * part : (q + 1) * part],
                weights[q],
                preferred_element_type=jnp.float32,
            )
            if q:
                acc_ref[...] += term
            else:
                acc_ref[...] = term
        for l in range(layers):
            reads[l].wait()
            writes[l].start()
        for l in range(layers):
            proj = acc_ref[:, l * width : (l + 1) * width]
            mean_sq = jnp.mean(proj * proj, axis=-1, keepdims=True)
            o_ref[l] = proj / jnp.sqrt(mean_sq + 1e-06) * g_ref[...]
        for l in range(layers):
            writes[l].wait()

    hbm = pl.BlockSpec(memory_space=pltpu.HBM)
    vmem = pl.BlockSpec(memory_space=pltpu.VMEM)
    return pl.pallas_call(
        body,
        in_specs=[hbm, hbm, hbm, vmem],
        out_specs=[hbm, vmem],
        out_shape=[
            jax.ShapeDtypeStruct((rows, layers * width), stacked.dtype),
            jax.ShapeDtypeStruct((layers, tok, width), jnp.float32),
        ],
        scratch_shapes=[
            pltpu.VMEM((layers, rows, width), stacked.dtype),
            pltpu.VMEM((tok, depth), hidden.dtype),
            pltpu.VMEM((steps, part, columns), w_proj.dtype),
            pltpu.VMEM((tok, columns), jnp.float32),
            pltpu.SemaphoreType.DMA((layers,)),
            pltpu.SemaphoreType.DMA((layers,)),
            pltpu.SemaphoreType.DMA((steps,)),
            pltpu.SemaphoreType.DMA,
        ],
        compiler_params=pltpu.CompilerParams(vmem_limit_bytes=46 << 20),
        cost_estimate=pl.CostEstimate(
            flops=2 * tok * depth * columns,
            bytes_accessed=2 * depth * (tok + columns) + 4 * stacked.size,
            transcendentals=0,
        ),
    )(stacked, hidden, w_proj, norm_gain.reshape(1, width))


def add_embedding(crossed, pieces, normed):
    layers, tok, width = pieces.shape

    def body(s_ref, r_ref, *refs):
        n_refs, o_ref, acc_ref = refs[:-2], refs[-2], refs[-1]
        each = layers // len(n_refs)
        swap = s_ref[...] > 0
        for l in range(layers):
            emb = jnp.where(
                swap, r_ref[l ^ 1].astype(jnp.float32), r_ref[l].astype(jnp.float32)
            )
            acc_ref[:, l, :] = (n_refs[l // each][l % each] + math.sqrt(width) * emb) / math.sqrt(2.0)
        o_ref[...] = acc_ref[...].astype(jnp.bfloat16)

    vmem = pl.BlockSpec(memory_space=pltpu.VMEM)
    return pl.pallas_call(
        body,
        in_specs=[vmem] * (2 + len(normed)),
        out_specs=vmem,
        out_shape=jax.ShapeDtypeStruct((tok, layers, width), jnp.bfloat16),
        scratch_shapes=[pltpu.VMEM((tok, layers, width), jnp.float32)],
        compiler_params=pltpu.CompilerParams(vmem_limit_bytes=16 << 20),
        cost_estimate=pl.CostEstimate(
            flops=6 * tok * layers * width,
            bytes_accessed=8 * layers * width * tok,
            transcendentals=0,
        ),
    )(crossed.reshape(tok, 1), pieces, *normed)


def on_device(table, token_ids, hidden, w_proj, norm_gain):
    n_grp = lax.axis_size("grp")
    n_dev = lax.axis_size("dev")
    n_y, n_x = n_grp // 2, n_dev // 4
    peers = n_grp * n_dev
    d_index = lax.axis_index("dev")
    my_x, my_zh, my_c = d_index // 4, d_index // 2 % 2, d_index % 2
    _, shard_rows, width = table.shape
    layers = w_proj.shape[1] // width
    row_count = shard_rows // n_grp
    tok_count = token_ids.shape[0]
    slots = peers * CAP
    shard = table.reshape(shard_rows, width)
    hop = functools.partial(send, n_y=n_y, n_x=n_x)

    ids = lax.all_to_all(
        jnp.broadcast_to(token_ids[None, None], (n_grp, 1, tok_count)),
        "grp",
        split_axis=0,
        concat_axis=0,
        tiled=True,
    )
    gated, ids = lax.optimization_barrier((table.reshape(n_grp, row_count, width), ids))
    moved = lax.all_to_all(gated, "grp", split_axis=0, concat_axis=0, tiled=True)

    def crossed_of(holder):
        return (holder // 2 % 2) ^ my_zh

    ids = ids.reshape(n_grp, tok_count)
    block = ids // row_count
    positions = jnp.arange(tok_count, dtype=jnp.int32)
    same = (block[:, :, None] == block[:, None, :]) & (positions[None, :] < positions[:, None])
    rank = jnp.sum(same.astype(jnp.int32), axis=2)
    holder = block // n_grp
    k = (my_x - holder // 4 + n_x) % n_x
    in_shard = block % n_grp
    half_run = n_grp // 2 * CAP
    places = ((holder % 2) ^ my_c) * 2 + 1 - in_shard // (n_grp // 2)
    places = (places * 2 + crossed_of(holder)) * n_x + k
    spot = places * half_run + in_shard % (n_grp // 2) * CAP + rank
    odd = (jnp.arange(n_grp, dtype=jnp.int32) % 2)[:, None]
    places = (places * (n_grp // 2) + in_shard % (n_grp // 2)) * 2 * CAP + odd * CAP + rank
    hit = (spot[:, None, :] == jnp.arange(slots, dtype=jnp.int32)[None, :, None]).astype(
        jnp.int32
    )
    local = ids % row_count
    asked = jnp.sum(hit * (local + 1)[:, None, :], axis=2) - 1
    asked = asked.reshape(n_grp, 2, 2, 2, n_x, n_grp // 2, CAP).transpose(1, 3, 4, 2, 5, 0, 6)
    asked = asked.reshape(2, 2, n_x, n_grp, n_grp * CAP)
    asked = jnp.stack([asked[0], hop(asked[1], core=1)])
    asked = jnp.stack(
        [asked[:, :, 0]] + [hop(asked[:, :, q], dx=n_x - q) for q in range(1, n_x)]
    )
    asked = jnp.stack([asked[:, :, 0], hop(asked[:, :, 1], flip=1)], axis=1)
    wanted = asked.transpose(3, 0, 1, 2, 4).reshape(n_grp, n_x, 4 * n_grp * CAP)

    near, far = look_up(shard, wanted, n_x, n_grp, False)
    a_x = look_up(shard, wanted, n_x, n_grp, True)
    a_x = [a_x[0]] + [hop(a_x[q], dx=q) for q in range(1, n_x)]
    b_far = hop(far, flip=1)
    a_far = hop(flip_parts(a_x), flip=1)
    b_x = [hop(part, dx=q + 1) for q, part in enumerate(x_parts(near, b_far))]
    parts = [*a_x, a_far, near, b_far, *b_x]
    other = hop(core_parts(parts, n_x), core=1)
    sorted_rows = in_token_order(places, parts, other, n_x)
    moved, sorted_rows, hidden = lax.optimization_barrier((moved, sorted_rows, hidden))

    pieces = lax.all_to_all(sorted_rows, "grp", split_axis=0, concat_axis=0, tiled=True)
    served, normed = serve_and_project(moved, hidden, w_proj, norm_gain)
    served = served.reshape(1, 1, row_count, layers * width)
    crossed = crossed_of(token_ids // shard_rows)
    layer_inputs = add_embedding(crossed, pieces, [normed])
    return (served, layer_inputs)


def solution(mesh):
    in_specs = (P("grp", "dev", None), P(("grp", "dev")), P(("grp", "dev"), None), P(), P())
    out_specs = (P("dev", "grp", None, None), P(("grp", "dev"), None, None))
    return jax.shard_map(
        on_device, mesh=mesh, in_specs=in_specs, out_specs=out_specs, check_vma=False
    )
```

time: 111 us -> 102 us (0.919)
  Pallas kernels: 32.6 us -> 15.5 us
  waiting for transfers between devices: 34.4 us -> 42.3 us
    pallas_call x5 -> x2, Pallas kernels: 28.5 us -> 10.5 us  [the longest x1 8.12 us: serve_and_project(): pl.pallas_call(body, in_specs=[hbm, hbm, hbm, vmem], out_specs=[hbm, vmem...]
    ppermute x9 -> x14, waiting for transfers between devices: 21.1 us -> 29.3 us  [send(): return lax.ppermute(value, BOTH, moves)]
    all_to_all x1, waiting for transfers between devices: 0.13 us -> 6.11 us  [on_device(): lax.all_to_all(jnp.broadcast_to(token_ids[None, None], (n_grp, 1, tok_cou...]
    all_to_all x1, waiting for transfers between devices: 5.84 us -> 0.01 us  [on_device(): lax.all_to_all(gated, 'grp', split_axis=0, concat_axis=0, tiled=True)]
    ppermute x9 -> x14, starting transfers between devices: 15.3 us -> 20.9 us  [send(): return lax.ppermute(value, BOTH, moves)]
    all_to_all x1, starting transfers between devices: 11.1 us -> 5.91 us  [on_device(): lax.all_to_all(jnp.broadcast_to(token_ids[None, None], (n_grp, 1, tok_cou...]
    unnamed x11 -> x8, local copies, waits for them, and re-layouts: 0.97 us -> 3.51 us
    broadcast_in_dim x1, local copies, waits for them, and re-layouts: 0.01 us -> 1.28 us  [on_device(): jnp.broadcast_to(token_ids[None, None], (n_grp, 1, tok_count))]
  transfers between devices with their start and end apart: 12 -> 17, of which waited for: 8 -> 11; matrix products, arithmetic and copies ran while one was open for 4% -> 3% of each run, Pallas kernels for 27% -> 13%
where the time goes in v4:
time: 102 us
  waiting for transfers between devices  42.3 us (41%)
  starting transfers between devices  35.4 us (35%)
  Pallas kernels  15.5 us (15%)
  local copies, waits for them, and re-layouts  6.38 us (6%)
  other arithmetic  1.62 us (2%)
    ppermute x14, waiting for transfers between devices, send(): return lax.ppermute(value, BOTH, moves)  29.3 us
    ppermute x14, starting transfers between devices, send(): return lax.ppermute(value, BOTH, moves)  20.9 us
    pallas_call x1, Pallas kernels, serve_and_project(): pl.pallas_call(body, in_specs=[hbm, hbm, hbm, vmem], out_specs=[hbm, vmem...  8.12 us
    all_to_all x1, waiting for transfers between devices, on_device(): lax.all_to_all(sorted_rows, 'grp', split_axis=0, concat_axis=0, tiled=True)  6.87 us
    all_to_all x1, waiting for transfers between devices, on_device(): lax.all_to_all(jnp.broadcast_to(token_ids[None, None], (n_grp, 1, tok_cou...  6.11 us
    all_to_all x1, starting transfers between devices, on_device(): lax.all_to_all(jnp.broadcast_to(token_ids[None, None], (n_grp, 1, tok_cou...  5.91 us
    pallas_call x6, Pallas kernels, near_call(): pl.pallas_call(body, in_specs=[vmem] * len(operands), out_specs=[vmem] *...  5.01 us
    all_to_all x1, starting transfers between devices, on_device(): lax.all_to_all(gated, 'grp', split_axis=0, concat_axis=0, tiled=True)  4.57 us
  transfers between devices with their start and end apart: 17, of which 11 were waited for; matrix products, arithmetic and copies ran while one was open for 3% of the time, Pallas kernels for 13%

profile of v4, /device:TPU:0, one launch (start us, length us, event | category | flops | bytes accessed | tf_op | source)
XLA Modules:
  0.0 102.0 jit_solution(9509758605134202747)
XLA Ops:
  1.9 5.9 %all-to-all-start = ((s32[8,1,256]{2,1,0:T(1,128)}), s32[8,1,256]{2,1,0:T(1,128)S(1)}, u32[]{:S(2)}, u32[]{:S(2)}) async-start(s32[8,1,256]{2,1,0:T(1,128)} %broadcast_in_dim.2), calls=%async_computation | async-start | bytes 16384 | tf_op jit(solution)/shard_map/all_to_all | solution.py:268
  7.9 6.1 %all-to-all-done = s32[8,1,256]{2,1,0:T(1,128)S(1)} async-done(((s32[8,1,256]{2,1,0:T(1,128)}), s32[8,1,256]{2,1,0:T(1,128)S(1)}, u32[]{:S(2)}, u32[]{:S(2)}) %all-to-all-start) | async-done | bytes 8224 | tf_op jit(solution)/shard_map/all_to_all | solution.py:268
  14.0 4.6 %all-to-all-start.1 = ((bf16[8,1024,256]{2,1,0:T(8,128)(2,1)}), bf16[8,1024,256]{2,1,0:T(8,128)(2,1)}, u32[]{:S(2)}, u32[]{:S(2)}) async-start(bf16[8,1024,256]{2,1,0:T(8,128)(2,1)} %bitcast.65), calls=%async_computation.1 | async-start | bytes 8388608 | tf_op jit(solution)/shard_map/all_to_all | solution.py:276
  22.1 2.8 %collective-permute-start.1 = (s32[2,2,8,32]{3,2,1,0:T(8,128)S(1)}, s32[2,2,8,32]{3,2,1,0:T(8,128)S(1)}, u32[]{:S(2)}, u32[]{:S(2)}) collective-permute-start(s32[2,2,8,32]{3,2,1,0:T(8,128)S(1)} %get-tuple-element.39), channel_id=1, source_target_pairs={{0,12},{1,13},{2,14},{3,15},{16,28},{17,29},{18,30},{19,31},{4,0},... | collective-permute-start | bytes 12296 | tf_op jit(solution)/shard_map/ppermute | solution.py:29
  26.6 3.6 %collective-permute-done.2 = s32[2,2,8,32]{3,2,1,0:T(8,128)S(1)} collective-permute-done((s32[2,2,8,32]{3,2,1,0:T(8,128)S(1)}, s32[2,2,8,32]{3,2,1,0:T(8,128)S(1)}, u32[]{:S(2)}, u32[]{:S(2)}) %collective-permute-start.2) | collective-permute-done | bytes 4128 | tf_op jit(solution)/shard_map/ppermute | solution.py:29
  30.7 4.1 %collective-permute-start.4 = (s32[4,2,8,32]{3,2,1,0:T(8,128)S(1)}, s32[4,2,8,32]{3,2,1,0:T(8,128)S(1)}, u32[]{:S(2)}, u32[]{:S(2)}) collective-permute-start(s32[4,2,8,32]{3,2,1,0:T(8,128)S(1)} %get-tuple-element.37), channel_id=1, source_target_pairs={{0,18},{1,19},{2,16},{3,17},{16,2},{17,3},{18,0},{19,1},{4,22},{5,... | collective-permute-start | bytes 24584 | tf_op jit(solution)/shard_map/ppermute | solution.py:29
  34.8 1.9 %collective-permute-done.4 = s32[4,2,8,32]{3,2,1,0:T(8,128)S(1)} collective-permute-done((s32[4,2,8,32]{3,2,1,0:T(8,128)S(1)}, s32[4,2,8,32]{3,2,1,0:T(8,128)S(1)}, u32[]{:S(2)}, u32[]{:S(2)}) %collective-permute-start.4) | collective-permute-done | bytes 8224 | tf_op jit(solution)/shard_map/ppermute | solution.py:29
  36.9 2.2 %copy-done = bf16[1,8192,256]{2,1,0:T(8,128)(2,1)S(1)} copy-done((bf16[1,8192,256]{2,1,0:T(8,128)(2,1)S(1)}, bf16[1,8192,256]{2,1,0:T(8,128)(2,1)}, u32[]{:S(2)}) %copy-start) | copy-done | bytes 4194328
  39.1 1.3 %shard_map.70 = (bf16[4,2,4,4,8,256]{5,4,3,2,1,0:T(8,128)(2,1)S(1)}, bf16[4,2,4,4,8,256]{5,4,3,2,1,0:T(8,128)(2,1)S(1)}) custom-call(s32[8,4,128]{2,1,0:T(4,128)S(1)} %reshape.90.w_ref, bf16[8192,256]{1,0:T(8,128)(2,1)S(1)} %bitcast.66), custom_call_target="tpu_custom_call" | custom-call | bytes 65536 | tf_op jit(solution)/shard_map/pallas_call | solution.py:78
  40.4 1.3 %shard_map.68 = (bf16[2,2,4,4,8,256]{5,4,3,2,1,0:T(8,128)(2,1)S(1)}, bf16[2,2,4,4,8,256]{5,4,3,2,1,0:T(8,128)(2,1)S(1)}, bf16[2,2,4,4,8,256]{5,4,3,2,1,0:T(8,128)(2,1)S(1)}, bf16[2,2,4,4,8,256]{5,4,3,2,1,0:T(8,128)(2,1)S(1)}) custom-call(s32[8,4,128]{2,1,0:T(4,128)S(1)} %reshape.90.w_ref, bf16[8192,256]{1,0:T(8,128)(2,1)S(1)} %bitcast.67), custom_call_target="tpu_custom_call" | custom-call | bytes 65536 | tf_op jit(solution)/shard_map/pallas_call | solution.py:78
  41.7 3.3 %collective-permute-start.9 = (bf16[4,2,4,4,8,256]{5,4,3,2,1,0:T(8,128)(2,1)S(1)}, bf16[4,2,4,4,8,256]{5,4,3,2,1,0:T(8,128)(2,1)S(1)}, u32[]{:S(2)}, u32[]{:S(2)}) collective-permute-start(bf16[4,2,4,4,8,256]{5,4,3,2,1,0:T(8,128)(2,1)S(1)} %get-tuple-element.25), channel_id=1, source_target_pairs={{0,18},{1,19},{2,16},{3,17},{16,2},{17,3},{18,0},{19,1},{4,22},{5,... | collective-permute-start | bytes 1572872 | tf_op jit(solution)/shard_map/ppermute | solution.py:29
  45.0 1.8 %collective-permute-start.6 = (bf16[2,2,4,4,8,256]{5,4,3,2,1,0:T(8,128)(2,1)S(1)}, bf16[2,2,4,4,8,256]{5,4,3,2,1,0:T(8,128)(2,1)S(1)}, u32[]{:S(2)}, u32[]{:S(2)}) collective-permute-start(bf16[2,2,4,4,8,256]{5,4,3,2,1,0:T(8,128)(2,1)S(1)} %get-tuple-element.22), channel_id=1, source_target_pairs={{0,8},{1,9},{2,10},{3,11},{16,24},{17,25},{18,26},{19,27},{4,12},{... | collective-permute-start | bytes 786440 | tf_op jit(solution)/shard_map/ppermute | solution.py:29
  46.8 2.4 %collective-permute-start.7 = (bf16[2,2,4,4,8,256]{5,4,3,2,1,0:T(8,128)(2,1)S(1)}, bf16[2,2,4,4,8,256]{5,4,3,2,1,0:T(8,128)(2,1)S(1)}, u32[]{:S(2)}, u32[]{:S(2)}) collective-permute-start(bf16[2,2,4,4,8,256]{5,4,3,2,1,0:T(8,128)(2,1)S(1)} %get-tuple-element.23), channel_id=1, source_target_pairs={{0,12},{1,13},{2,14},{3,15},{16,28},{17,29},{18,30},{19,31},{4,0},... | collective-permute-start | bytes 786440 | tf_op jit(solution)/shard_map/ppermute | solution.py:29
  49.1 8.7 %collective-permute-done.5.refs_1_ = bf16[2,2,4,4,8,256]{5,4,3,2,1,0:T(8,128)(2,1)S(1)} collective-permute-done((bf16[2,2,4,4,8,256]{5,4,3,2,1,0:T(8,128)(2,1)S(1)}, bf16[2,2,4,4,8,256]{5,4,3,2,1,0:T(8,128)(2,1)S(1)}, u32[]{:S(2)}, u32[]{:S(2)}) %collective-permute-start.5) | collective-permute-done | bytes 262176 | tf_op jit(solution)/shard_map/ppermute | solution.py:29
  59.9 3.2 %collective-permute-start.11 = (bf16[2,2,4,4,8,256]{5,4,3,2,1,0:T(8,128)(2,1)S(1)}, bf16[2,2,4,4,8,256]{5,4,3,2,1,0:T(8,128)(2,1)S(1)}, u32[]{:S(2)}, u32[]{:S(2)}) collective-permute-start(bf16[2,2,4,4,8,256]{5,4,3,2,1,0:T(8,128)(2,1)S(1)} %get-tuple-element.27), channel_id=1, source_target_pairs={{0,8},{1,9},{2,10},{3,11},{16,24},{17,25},{18,26},{19,27},{4,12},{... | collective-permute-start | bytes 786440 | tf_op jit(solution)/shard_map/ppermute | solution.py:29
  63.2 4.8 %collective-permute-done.10.refs_7_ = bf16[2,2,4,4,8,256]{5,4,3,2,1,0:T(8,128)(2,1)S(1)} collective-permute-done((bf16[2,2,4,4,8,256]{5,4,3,2,1,0:T(8,128)(2,1)S(1)}, bf16[2,2,4,4,8,256]{5,4,3,2,1,0:T(8,128)(2,1)S(1)}, u32[]{:S(2)}, u32[]{:S(2)}) %collective-permute-start.10) | collective-permute-done | bytes 262176 | tf_op jit(solution)/shard_map/ppermute | solution.py:29
  68.0 6.0 %collective-permute-done.11.refs_8_ = bf16[2,2,4,4,8,256]{5,4,3,2,1,0:T(8,128)(2,1)S(1)} collective-permute-done((bf16[2,2,4,4,8,256]{5,4,3,2,1,0:T(8,128)(2,1)S(1)}, bf16[2,2,4,4,8,256]{5,4,3,2,1,0:T(8,128)(2,1)S(1)}, u32[]{:S(2)}, u32[]{:S(2)}) %collective-permute-start.11) | collective-permute-done | bytes 262176 | tf_op jit(solution)/shard_map/ppermute | solution.py:29
  74.3 2.6 %collective-permute-done.13.refs_10_ = bf16[16,4,4,8,256]{4,3,2,1,0:T(8,128)(2,1)S(1)} collective-permute-done((bf16[16,4,4,8,256]{4,3,2,1,0:T(8,128)(2,1)S(1)}, bf16[16,4,4,8,256]{4,3,2,1,0:T(8,128)(2,1)S(1)}, u32[]{:S(2)}, u32[]{:S(2)}) %collective-permute-start.13) | collective-permute-done | bytes 1048608 | tf_op jit(solution)/shard_map/ppermute | solution.py:29
  76.9 2.3 %shard_map.73 = bf16[8,256,256]{2,1,0:T(8,128)(2,1)} custom-call(s32[8,256]{1,0:T(8,128)S(1)} %fusion.20.p_ref, bf16[2,2,4,4,8,256]{5,4,3,2,1,0:T(8,128)(2,1)S(1)} %get-tuple-element.20.refs_0_, bf16[2,2,4,4,8,256]{5,4,3,2,1,0:T(8,128)(2,1)S(1)} %collective-permute-done.5.refs_1_, bf16[2,2,4,4,8,256]{5,4,3,2,1,0:T(8,128)(2,1)S(1)} %collective-permute-done.6.refs_2_, ...), custom_call_target="tpu_custom_call" | custom-call | bytes 65536 | tf_op jit(solution)/shard_map/pallas_call | solution.py:78
  79.1 4.0 %all-to-all-start.2 = ((bf16[8,256,256]{2,1,0:T(8,128)(2,1)}), bf16[8,256,256]{2,1,0:T(8,128)(2,1)S(1)}, u32[]{:S(2)}, u32[]{:S(2)}) async-start(bf16[8,256,256]{2,1,0:T(8,128)(2,1)} %shard_map.73), calls=%async_computation.2 | async-start | bytes 2097152 | tf_op jit(solution)/shard_map/all_to_all | solution.py:320
  83.3 1.3 %copy-done.1 = bf16[256,2560]{1,0:T(8,128)(2,1)S(1)} copy-done((bf16[256,2560]{1,0:T(8,128)(2,1)S(1)}, bf16[256,2560]{1,0:T(8,128)(2,1)}, u32[]{:S(2)}) %copy-start.1) | copy-done | bytes 1310744
  84.6 8.1 %shard_map.74 = (bf16[1024,2048]{1,0:T(8,128)(2,1)}, f32[8,256,256]{2,1,0:T(8,128)S(1)}) custom-call(bf16[8,1024,256]{2,1,0:T(8,128)(2,1)} %all-to-all-done.1.m_ref, bf16[256,2560]{1,0:T(8,128)(2,1)S(1)} %copy-done.1, bf16[2560,2048]{1,0:T(8,128)(2,1)} %w_ref.1, f32[1,256]{1,0:T(1,128)S(1)} %bitcast.68), custom_call_target="tpu_custom_call" | custom-call | flops 2684354560 | bytes 20185088 | tf_op jit(solution)/shard_map/pallas_call | solution.py:196
  92.8 6.9 %all-to-all-done.2.r_ref = bf16[8,256,256]{2,1,0:T(8,128)(2,1)S(1)} async-done(((bf16[8,256,256]{2,1,0:T(8,128)(2,1)}), bf16[8,256,256]{2,1,0:T(8,128)(2,1)S(1)}, u32[]{:S(2)}, u32[]{:S(2)}) %all-to-all-start.2) | async-done | bytes 1048608 | tf_op jit(solution)/shard_map/all_to_all | solution.py:320
  99.6 2.4 %shard_map.75 = bf16[256,8,256]{2,1,0:T(8,128)(2,1)} custom-call(s32[256,1]{1,0:T(8,128)S(1)} %copy.43.s_ref, bf16[8,256,256]{2,1,0:T(8,128)(2,1)S(1)} %all-to-all-done.2.r_ref, f32[8,256,256]{2,1,0:T(8,128)S(1)} %get-tuple-element.33.refs_0_), custom_call_target="tpu_custom_call" | custom-call | flops 3145728 | bytes 4194304 | tf_op jit(solution)/shard_map/pallas_call | solution.py:238
  (50 shorter events, 9.7 us)
Async XLA Ops:
  1.9 12.1 %all-to-all-start = ((s32[8,1,256]{2,1,0:T(1,128)}), s32[8,1,256]{2,1,0:T(1,128)S(1)}, u32[]{:S(2)}, u32[]{:S(2)}) async-start(s32[8,1,256]{2,1,0:T(1,128)} %broadcast_in_dim.2), calls=%async_computation | async-start | bytes 16384 | tf_op jit(solution)/shard_map/all_to_all | solution.py:268
  14.0 65.1 %all-to-all-start.1 = ((bf16[8,1024,256]{2,1,0:T(8,128)(2,1)}), bf16[8,1024,256]{2,1,0:T(8,128)(2,1)}, u32[]{:S(2)}, u32[]{:S(2)}) async-start(bf16[8,1024,256]{2,1,0:T(8,128)(2,1)} %bitcast.65), calls=%async_computation.1 | async-start | bytes 8388608 | tf_op jit(solution)/shard_map/all_to_all | solution.py:276
  20.8 1.3 %collective-permute-start = (s32[2,4,8,32]{3,2,1,0:T(8,128)S(1)}, s32[2,4,8,32]{3,2,1,0:T(8,128)S(1)}, u32[]{:S(2)}, u32[]{:S(2)}) collective-permute-start(s32[2,4,8,32]{3,2,1,0:T(8,128)S(1)} %squeeze.15), channel_id=1, source_target_pairs={{0,1},{1,0},{2,3},{3,2},{16,17},{17,16},{18,19},{19,18},{4,5},{5,4... | collective-permute-start | bytes 24584 | tf_op jit(solution)/shard_map/ppermute | solution.py:29
  22.1 4.5 %collective-permute-start.1 = (s32[2,2,8,32]{3,2,1,0:T(8,128)S(1)}, s32[2,2,8,32]{3,2,1,0:T(8,128)S(1)}, u32[]{:S(2)}, u32[]{:S(2)}) collective-permute-start(s32[2,2,8,32]{3,2,1,0:T(8,128)S(1)} %get-tuple-element.39), channel_id=1, source_target_pairs={{0,12},{1,13},{2,14},{3,15},{16,28},{17,29},{18,30},{19,31},{4,0},... | collective-permute-start | bytes 12296 | tf_op jit(solution)/shard_map/ppermute | solution.py:29
  24.9 5.2 %collective-permute-start.2 = (s32[2,2,8,32]{3,2,1,0:T(8,128)S(1)}, s32[2,2,8,32]{3,2,1,0:T(8,128)S(1)}, u32[]{:S(2)}, u32[]{:S(2)}) collective-permute-start(s32[2,2,8,32]{3,2,1,0:T(8,128)S(1)} %get-tuple-element.41), channel_id=1, source_target_pairs={{0,8},{1,9},{2,10},{3,11},{16,24},{17,25},{18,26},{19,27},{4,12},{... | collective-permute-start | bytes 12296 | tf_op jit(solution)/shard_map/ppermute | solution.py:29
  25.7 4.9 %collective-permute-start.3 = (s32[2,2,8,32]{3,2,1,0:T(8,128)S(1)}, s32[2,2,8,32]{3,2,1,0:T(8,128)S(1)}, u32[]{:S(2)}, u32[]{:S(2)}) collective-permute-start(s32[2,2,8,32]{3,2,1,0:T(8,128)S(1)} %get-tuple-element.40), channel_id=1, source_target_pairs={{0,4},{1,5},{2,6},{3,7},{16,20},{17,21},{18,22},{19,23},{4,8},{5,9... | collective-permute-start | bytes 12296 | tf_op jit(solution)/shard_map/ppermute | solution.py:29
  30.7 6.0 %collective-permute-start.4 = (s32[4,2,8,32]{3,2,1,0:T(8,128)S(1)}, s32[4,2,8,32]{3,2,1,0:T(8,128)S(1)}, u32[]{:S(2)}, u32[]{:S(2)}) collective-permute-start(s32[4,2,8,32]{3,2,1,0:T(8,128)S(1)} %get-tuple-element.37), channel_id=1, source_target_pairs={{0,18},{1,19},{2,16},{3,17},{16,2},{17,3},{18,0},{19,1},{4,22},{5,... | collective-permute-start | bytes 24584 | tf_op jit(solution)/shard_map/ppermute | solution.py:29
  36.9 2.2 %copy-start = (bf16[1,8192,256]{2,1,0:T(8,128)(2,1)S(1)}, bf16[1,8192,256]{2,1,0:T(8,128)(2,1)}, u32[]{:S(2)}) copy-start(bf16[1,8192,256]{2,1,0:T(8,128)(2,1)} %param.5) | copy-start | bytes 12582916
  41.7 17.3 %collective-permute-start.9 = (bf16[4,2,4,4,8,256]{5,4,3,2,1,0:T(8,128)(2,1)S(1)}, bf16[4,2,4,4,8,256]{5,4,3,2,1,0:T(8,128)(2,1)S(1)}, u32[]{:S(2)}, u32[]{:S(2)}) collective-permute-start(bf16[4,2,4,4,8,256]{5,4,3,2,1,0:T(8,128)(2,1)S(1)} %get-tuple-element.25), channel_id=1, source_target_pairs={{0,18},{1,19},{2,16},{3,17},{16,2},{17,3},{18,0},{19,1},{4,22},{5,... | collective-permute-start | bytes 1572872 | tf_op jit(solution)/shard_map/ppermute | solution.py:29
  45.0 12.9 %collective-permute-start.5 = (bf16[2,2,4,4,8,256]{5,4,3,2,1,0:T(8,128)(2,1)S(1)}, bf16[2,2,4,4,8,256]{5,4,3,2,1,0:T(8,128)(2,1)S(1)}, u32[]{:S(2)}, u32[]{:S(2)}) collective-permute-start(bf16[2,2,4,4,8,256]{5,4,3,2,1,0:T(8,128)(2,1)S(1)} %get-tuple-element.21), channel_id=1, source_target_pairs={{0,4},{1,5},{2,6},{3,7},{16,20},{17,21},{18,22},{19,23},{4,8},{5,9... | collective-permute-start | bytes 786440 | tf_op jit(solution)/shard_map/ppermute | solution.py:29
  45.0 12.9 %collective-permute-start.6 = (bf16[2,2,4,4,8,256]{5,4,3,2,1,0:T(8,128)(2,1)S(1)}, bf16[2,2,4,4,8,256]{5,4,3,2,1,0:T(8,128)(2,1)S(1)}, u32[]{:S(2)}, u32[]{:S(2)}) collective-permute-start(bf16[2,2,4,4,8,256]{5,4,3,2,1,0:T(8,128)(2,1)S(1)} %get-tuple-element.22), channel_id=1, source_target_pairs={{0,8},{1,9},{2,10},{3,11},{16,24},{17,25},{18,26},{19,27},{4,12},{... | collective-permute-start | bytes 786440 | tf_op jit(solution)/shard_map/ppermute | solution.py:29
  46.8 11.7 %collective-permute-start.7 = (bf16[2,2,4,4,8,256]{5,4,3,2,1,0:T(8,128)(2,1)S(1)}, bf16[2,2,4,4,8,256]{5,4,3,2,1,0:T(8,128)(2,1)S(1)}, u32[]{:S(2)}, u32[]{:S(2)}) collective-permute-start(bf16[2,2,4,4,8,256]{5,4,3,2,1,0:T(8,128)(2,1)S(1)} %get-tuple-element.23), channel_id=1, source_target_pairs={{0,12},{1,13},{2,14},{3,15},{16,28},{17,29},{18,30},{19,31},{4,0},... | collective-permute-start | bytes 786440 | tf_op jit(solution)/shard_map/ppermute | solution.py:29
  58.5 15.5 %collective-permute-start.8 = (bf16[4,2,4,4,8,256]{5,4,3,2,1,0:T(8,128)(2,1)S(1)}, bf16[4,2,4,4,8,256]{5,4,3,2,1,0:T(8,128)(2,1)S(1)}, u32[]{:S(2)}, u32[]{:S(2)}) collective-permute-start(bf16[4,2,4,4,8,256]{5,4,3,2,1,0:T(8,128)(2,1)S(1)} %shard_map.69), channel_id=1, source_target_pairs={{0,18},{1,19},{2,16},{3,17},{16,2},{17,3},{18,0},{19,1},{4,22},{5,... | collective-permute-start | bytes 1572872 | tf_op jit(solution)/shard_map/ppermute | solution.py:29
  59.0 9.0 %collective-permute-start.10 = (bf16[2,2,4,4,8,256]{5,4,3,2,1,0:T(8,128)(2,1)S(1)}, bf16[2,2,4,4,8,256]{5,4,3,2,1,0:T(8,128)(2,1)S(1)}, u32[]{:S(2)}, u32[]{:S(2)}) collective-permute-start(bf16[2,2,4,4,8,256]{5,4,3,2,1,0:T(8,128)(2,1)S(1)} %get-tuple-element.26), channel_id=1, source_target_pairs={{0,4},{1,5},{2,6},{3,7},{16,20},{17,21},{18,22},{19,23},{4,8},{5,9... | collective-permute-start | bytes 786440 | tf_op jit(solution)/shard_map/ppermute | solution.py:29
  59.9 14.1 %collective-permute-start.11 = (bf16[2,2,4,4,8,256]{5,4,3,2,1,0:T(8,128)(2,1)S(1)}, bf16[2,2,4,4,8,256]{5,4,3,2,1,0:T(8,128)(2,1)S(1)}, u32[]{:S(2)}, u32[]{:S(2)}) collective-permute-start(bf16[2,2,4,4,8,256]{5,4,3,2,1,0:T(8,128)(2,1)S(1)} %get-tuple-element.27), channel_id=1, source_target_pairs={{0,8},{1,9},{2,10},{3,11},{16,24},{17,25},{18,26},{19,27},{4,12},{... | collective-permute-start | bytes 786440 | tf_op jit(solution)/shard_map/ppermute | solution.py:29
  63.1 10.9 %collective-permute-start.12 = (bf16[2,2,4,4,8,256]{5,4,3,2,1,0:T(8,128)(2,1)S(1)}, bf16[2,2,4,4,8,256]{5,4,3,2,1,0:T(8,128)(2,1)S(1)}, u32[]{:S(2)}, u32[]{:S(2)}) collective-permute-start(bf16[2,2,4,4,8,256]{5,4,3,2,1,0:T(8,128)(2,1)S(1)} %get-tuple-element.28), channel_id=1, source_target_pairs={{0,12},{1,13},{2,14},{3,15},{16,28},{17,29},{18,30},{19,31},{4,0},... | collective-permute-start | bytes 786440 | tf_op jit(solution)/shard_map/ppermute | solution.py:29
  74.1 9.0 %copy-start.3 = (s32[256]{0:T(256)S(1)}, s32[256]{0:T(256)}, u32[]{:S(2)}) copy-start(s32[256]{0:T(256)} %param.6) | copy-start | bytes 3076
  74.1 9.2 %copy-start.2 = (f32[256]{0:T(256)S(1)}, f32[256]{0:T(256)}, u32[]{:S(2)}) copy-start(f32[256]{0:T(256)} %param.9) | copy-start | bytes 3076
  74.1 2.7 %collective-permute-start.13 = (bf16[16,4,4,8,256]{4,3,2,1,0:T(8,128)(2,1)S(1)}, bf16[16,4,4,8,256]{4,3,2,1,0:T(8,128)(2,1)S(1)}, u32[]{:S(2)}, u32[]{:S(2)}) collective-permute-start(bf16[16,4,4,8,256]{4,3,2,1,0:T(8,128)(2,1)S(1)} %shard_map.72), channel_id=1, source_target_pairs={{0,1},{1,0},{2,3},{3,2},{16,17},{17,16},{18,19},{19,18},{4,5},{5,4... | collective-permute-start | bytes 3145736 | tf_op jit(solution)/shard_map/ppermute | solution.py:29
  79.1 20.5 %all-to-all-start.2 = ((bf16[8,256,256]{2,1,0:T(8,128)(2,1)}), bf16[8,256,256]{2,1,0:T(8,128)(2,1)S(1)}, u32[]{:S(2)}, u32[]{:S(2)}) async-start(bf16[8,256,256]{2,1,0:T(8,128)(2,1)} %shard_map.73), calls=%async_computation.2 | async-start | bytes 2097152 | tf_op jit(solution)/shard_map/all_to_all | solution.py:320
  83.3 1.3 %copy-start.1 = (bf16[256,2560]{1,0:T(8,128)(2,1)S(1)}, bf16[256,2560]{1,0:T(8,128)(2,1)}, u32[]{:S(2)}) copy-start(bf16[256,2560]{1,0:T(8,128)(2,1)} %h_hbm) | copy-start | bytes 3932164

commit v5 on v4

--- a/solution.py
+++ b/solution.py
@@ -222,32 +222,45 @@
 
 def add_embedding(crossed, pieces, normed):
     layers, tok, width = pieces.shape
-
-    def body(s_ref, r_ref, *refs):
-        n_refs, o_ref, acc_ref = refs[:-2], refs[-2], refs[-1]
-        each = layers // len(n_refs)
-        swap = s_ref[...] > 0
-        for l in range(layers):
-            emb = jnp.where(
-                swap, r_ref[l ^ 1].astype(jnp.float32), r_ref[l].astype(jnp.float32)
-            )
-            acc_ref[:, l, :] = (n_refs[l // each][l % each] + math.sqrt(width) * emb) / math.sqrt(2.0)
-        o_ref[...] = acc_ref[...].astype(jnp.bfloat16)
+    blocks = 4
+    part = tok // blocks
+
+    def body(s_ref, r_ref, n_ref, o_ref, acc_ref, out_ref, sem):
+        copies = []
+        for q in range(blocks):
+            here = slice(q * part, (q + 1) * part)
+            swap = s_ref[here] > 0
+            for l in range(layers):
+                emb = jnp.where(
+                    swap,
+                    r_ref[l ^ 1, here].astype(jnp.float32),
+                    r_ref[l, here].astype(jnp.float32),
+                )
+                acc_ref[:, l, :] = (n_ref[l, here] + math.sqrt(width) * emb) / math.sqrt(2.0)
+            out_ref[here] = acc_ref[...].astype(jnp.bfloat16)
+            copies.append(pltpu.make_async_copy(out_ref.at[here], o_ref.at[here], sem.at[q]))
+            copies[q].start()
+        for copy in copies:
+            copy.wait()
 
     vmem = pl.BlockSpec(memory_space=pltpu.VMEM)
     return pl.pallas_call(
         body,
-        in_specs=[vmem] * (2 + len(normed)),
-        out_specs=vmem,
+        in_specs=[vmem] * 3,
+        out_specs=pl.BlockSpec(memory_space=pltpu.HBM),
         out_shape=jax.ShapeDtypeStruct((tok, layers, width), jnp.bfloat16),
-        scratch_shapes=[pltpu.VMEM((tok, layers, width), jnp.float32)],
+        scratch_shapes=[
+            pltpu.VMEM((part, layers, width), jnp.float32),
+            pltpu.VMEM((tok, layers, width), jnp.bfloat16),
+            pltpu.SemaphoreType.DMA((blocks,)),
+        ],
         compiler_params=pltpu.CompilerParams(vmem_limit_bytes=16 << 20),
         cost_estimate=pl.CostEstimate(
             flops=6 * tok * layers * width,
             bytes_accessed=8 * layers * width * tok,
             transcendentals=0,
         ),
-    )(crossed.reshape(tok, 1), pieces, *normed)
+    )(crossed.reshape(tok, 1), pieces, normed)
 
 
 def on_device(table, token_ids, hidden, w_proj, norm_gain):
@@ -265,11 +278,22 @@
     shard = table.reshape(shard_rows, width)
     hop = functools.partial(send, n_y=n_y, n_x=n_x)
 
+    columns = []
+    for x in range(n_x):
+        for c in range(2):
+            columns.append(
+                [
+                    flat_index(g // 2, g % 2, x, zh, c, n_x)
+                    for zh in range(2)
+                    for g in range(n_grp)
+                ]
+            )
     ids = lax.all_to_all(
-        jnp.broadcast_to(token_ids[None, None], (n_grp, 1, tok_count)),
-        "grp",
+        jnp.broadcast_to(token_ids[None, None], (2 * n_grp, 1, tok_count)),
+        BOTH,
         split_axis=0,
         concat_axis=0,
+        axis_index_groups=columns,
         tiled=True,
     )
     gated, ids = lax.optimization_barrier((table.reshape(n_grp, row_count, width), ids))
@@ -278,33 +302,36 @@
     def crossed_of(holder):
         return (holder // 2 % 2) ^ my_zh
 
-    ids = ids.reshape(n_grp, tok_count)
+    ids = ids.reshape(2, n_grp, tok_count)
+    ids = jnp.where(my_zh == 1, ids[::-1], ids)
     block = ids // row_count
     positions = jnp.arange(tok_count, dtype=jnp.int32)
-    same = (block[:, :, None] == block[:, None, :]) & (positions[None, :] < positions[:, None])
-    rank = jnp.sum(same.astype(jnp.int32), axis=2)
+    same = (block[..., :, None] == block[..., None, :]) & (
+        positions[None, :] < positions[:, None]
+    )
+    rank = jnp.sum(same.astype(jnp.int32), axis=3)
     holder = block // n_grp
     k = (my_x - holder // 4 + n_x) % n_x
     in_shard = block % n_grp
-    half_run = n_grp // 2 * CAP
-    places = ((holder % 2) ^ my_c) * 2 + 1 - in_shard // (n_grp // 2)
-    places = (places * 2 + crossed_of(holder)) * n_x + k
-    spot = places * half_run + in_shard % (n_grp // 2) * CAP + rank
+    four = n_grp // 2
+    part = ((holder % 2) ^ my_c) * 2 + 1 - in_shard // four
+    spot = ((part * n_x + k) * four + in_shard % four) * CAP + rank
+    spot = jnp.where(crossed_of(holder) == 0, spot, -1)
     odd = (jnp.arange(n_grp, dtype=jnp.int32) % 2)[:, None]
-    places = (places * (n_grp // 2) + in_shard % (n_grp // 2)) * 2 * CAP + odd * CAP + rank
-    hit = (spot[:, None, :] == jnp.arange(slots, dtype=jnp.int32)[None, :, None]).astype(
-        jnp.int32
-    )
+    places = ((part * 2 + crossed_of(holder)) * n_x + k) * four + in_shard % four
+    places = places[0] * 2 * CAP + odd * CAP + rank[0]
+    hit = (
+        spot[:, :, None, :] == jnp.arange(slots // 2, dtype=jnp.int32)[None, None, :, None]
+    ).astype(jnp.int32)
     local = ids % row_count
-    asked = jnp.sum(hit * (local + 1)[:, None, :], axis=2) - 1
-    asked = asked.reshape(n_grp, 2, 2, 2, n_x, n_grp // 2, CAP).transpose(1, 3, 4, 2, 5, 0, 6)
+    asked = jnp.sum(hit * (local + 1)[:, :, None, :], axis=3) - 1
+    asked = asked.reshape(2, n_grp, 2, 2, n_x, four, CAP).transpose(2, 0, 4, 3, 5, 1, 6)
     asked = asked.reshape(2, 2, n_x, n_grp, n_grp * CAP)
     asked = jnp.stack([asked[0], hop(asked[1], core=1)])
     asked = jnp.stack(
         [asked[:, :, 0]] + [hop(asked[:, :, q], dx=n_x - q) for q in range(1, n_x)]
     )
-    asked = jnp.stack([asked[:, :, 0], hop(asked[:, :, 1], flip=1)], axis=1)
-    wanted = asked.transpose(3, 0, 1, 2, 4).reshape(n_grp, n_x, 4 * n_grp * CAP)
+    wanted = asked.transpose(3, 0, 2, 1, 4).reshape(n_grp, n_x, 4 * n_grp * CAP)
 
     near, far = look_up(shard, wanted, n_x, n_grp, False)
     a_x = look_up(shard, wanted, n_x, n_grp, True)
@@ -321,7 +348,7 @@
     served, normed = serve_and_project(moved, hidden, w_proj, norm_gain)
     served = served.reshape(1, 1, row_count, layers * width)
     crossed = crossed_of(token_ids // shard_rows)
-    layer_inputs = add_embedding(crossed, pieces, [normed])
+    layer_inputs = add_embedding(crossed, pieces, normed)
     return (served, layer_inputs)
 
 

time: 102 us -> 100 us (0.980)
  blocking collectives: 0 us -> 15.5 us
  starting transfers between devices: 35.4 us -> 25.9 us
  waiting for transfers between devices: 42.3 us -> 34 us
    all_to_all x0 -> x1, blocking collectives: none -> 15.5 us  [on_device(): lax.all_to_all(jnp.broadcast_to(token_ids[None, None], (2 * n_grp, 1, tok...]
    all_to_all x1 -> x0, waiting for transfers between devices: 6.11 us -> none  [on_device(): lax.all_to_all(jnp.broadcast_to(token_ids[None, None], (n_grp, 1, tok_cou...]
    all_to_all x1 -> x0, starting transfers between devices: 5.91 us -> none  [on_device(): lax.all_to_all(jnp.broadcast_to(token_ids[None, None], (n_grp, 1, tok_cou...]
    ppermute x14 -> x13, starting transfers between devices: 20.9 us -> 17.6 us  [send(): return lax.ppermute(value, BOTH, moves)]
    all_to_all x1, waiting for transfers between devices: 0.01 us -> 2.89 us  [on_device(): lax.all_to_all(gated, 'grp', split_axis=0, concat_axis=0, tiled=True)]
    ppermute x14 -> x13, waiting for transfers between devices: 29.3 us -> 26.7 us  [send(): return lax.ppermute(value, BOTH, moves)]
    all_to_all x1, waiting for transfers between devices: 6.87 us -> 4.44 us  [on_device(): lax.all_to_all(sorted_rows, 'grp', split_axis=0, concat_axis=0, tiled=True)]
    unnamed x8 -> x9, local copies, waits for them, and re-layouts: 3.51 us -> 3.52 us
  transfers between devices with their start and end apart: 17 -> 15, of which waited for: 11 -> 9; matrix products, arithmetic and copies ran while one was open for 3% -> 4% of each run, Pallas kernels for 13% -> 13%
where the time goes in v5:
time: 100 us; the launch traced here: 99.7 us
  waiting for transfers between devices  34 us (34%)
  starting transfers between devices  25.9 us (26%)
  blocking collectives  15.5 us (16%)
  Pallas kernels  15 us (15%)
  local copies, waits for them, and re-layouts  5.78 us (6%)
  other arithmetic  2.33 us (2%)
  between operations  1.06 us (1%)
    ppermute x13, waiting for transfers between devices, send(): return lax.ppermute(value, BOTH, moves)  26.7 us
    ppermute x13, starting transfers between devices, send(): return lax.ppermute(value, BOTH, moves)  17.6 us
    all_to_all x1, blocking collectives, on_device(): lax.all_to_all(jnp.broadcast_to(token_ids[None, None], (2 * n_grp, 1, tok...  15.5 us
    pallas_call x1, Pallas kernels, serve_and_project(): pl.pallas_call(body, in_specs=[hbm, hbm, hbm, vmem], out_specs=[hbm, vmem...  8.12 us
    pallas_call x6, Pallas kernels, near_call(): pl.pallas_call(body, in_specs=[vmem] * len(operands), out_specs=[vmem] *...  5.01 us
    all_to_all x1, starting transfers between devices, on_device(): lax.all_to_all(gated, 'grp', split_axis=0, concat_axis=0, tiled=True)  4.56 us
    all_to_all x1, waiting for transfers between devices, on_device(): lax.all_to_all(sorted_rows, 'grp', split_axis=0, concat_axis=0, tiled=True)  4.44 us
    all_to_all x1, starting transfers between devices, on_device(): lax.all_to_all(sorted_rows, 'grp', split_axis=0, concat_axis=0, tiled=True)  3.74 us
  transfers between devices with their start and end apart: 15, of which 9 were waited for; matrix products, arithmetic and copies ran while one was open for 4% of the time, Pallas kernels for 13%

profile of v5, /device:TPU:0, one launch (start us, length us, event | category | flops | bytes accessed | tf_op | source)
XLA Modules:
  0.0 99.7 jit_solution(16460351875327375556)
XLA Ops:
  1.3 15.5 %all_to_all.15 = s32[16,1,256]{2,1,0:T(1,128)S(1)} all-to-all(s32[16,1,256]{2,1,0:T(1,128)S(1)} %broadcast_in_dim.3), channel_id=1, replica_groups={{0,16,32,48,64,80,96,112,2,18,34,50,66,82,98,114},{1,17,33,49,65,81,97,..., dimensions={0} | all-to-all | bytes 32768 | tf_op jit(solution)/shard_map/all_to_all | solution.py:291
  16.8 4.6 %all-to-all-start.1 = ((bf16[8,1024,256]{2,1,0:T(8,128)(2,1)}), bf16[8,1024,256]{2,1,0:T(8,128)(2,1)}, u32[]{:S(2)}, u32[]{:S(2)}) async-start(bf16[8,1024,256]{2,1,0:T(8,128)(2,1)} %bitcast.45), calls=%async_computation.1 | async-start | bytes 8388608 | tf_op jit(solution)/shard_map/all_to_all | solution.py:300
  21.5 1.3 %convert_reduce_fusion = s32[2,8,256]{2,1,0:T(8,128)S(1)} fusion(s32[2,8,256]{2,1,0:T(8,128)S(1)} %get-tuple-element.39, pred[256,256]{1,0:T(8,128)(4,1)S(1)} %iota_compare_fusion.1), kind=kLoop, calls=%fused_computation.2 | loop fusion | flops 4190208 | bytes 98304 | tf_op jit(solution)/shard_map/reduce_sum | solution.py:312
  25.7 3.1 %collective-permute-start.2 = (s32[2,2,8,32]{3,2,1,0:T(8,128)S(1)}, s32[2,2,8,32]{3,2,1,0:T(8,128)S(1)}, u32[]{:S(2)}, u32[]{:S(2)}) collective-permute-start(s32[2,2,8,32]{3,2,1,0:T(8,128)S(1)} %get-tuple-element.45), channel_id=1, source_target_pairs={{0,8},{1,9},{2,10},{3,11},{16,24},{17,25},{18,26},{19,27},{4,12},{... | collective-permute-start | bytes 12296 | tf_op jit(solution)/shard_map/ppermute | solution.py:29
  29.4 2.6 %collective-permute-start.1 = (s32[2,2,8,32]{3,2,1,0:T(8,128)S(1)}, s32[2,2,8,32]{3,2,1,0:T(8,128)S(1)}, u32[]{:S(2)}, u32[]{:S(2)}) collective-permute-start(s32[2,2,8,32]{3,2,1,0:T(8,128)S(1)} %get-tuple-element.43), channel_id=1, source_target_pairs={{0,12},{1,13},{2,14},{3,15},{16,28},{17,29},{18,30},{19,31},{4,0},... | collective-permute-start | bytes 12296 | tf_op jit(solution)/shard_map/ppermute | solution.py:29
  32.1 1.7 %collective-permute-done.3 = s32[2,2,8,32]{3,2,1,0:T(8,128)S(1)} collective-permute-done((s32[2,2,8,32]{3,2,1,0:T(8,128)S(1)}, s32[2,2,8,32]{3,2,1,0:T(8,128)S(1)}, u32[]{:S(2)}, u32[]{:S(2)}) %collective-permute-start.3) | collective-permute-done | bytes 4128 | tf_op jit(solution)/shard_map/ppermute | solution.py:29
  34.0 2.2 %copy-done = bf16[1,8192,256]{2,1,0:T(8,128)(2,1)S(1)} copy-done((bf16[1,8192,256]{2,1,0:T(8,128)(2,1)S(1)}, bf16[1,8192,256]{2,1,0:T(8,128)(2,1)}, u32[]{:S(2)}) %copy-start) | copy-done | bytes 4194328
  37.5 1.3 %shard_map.68 = (bf16[2,2,4,4,8,256]{5,4,3,2,1,0:T(8,128)(2,1)S(1)}, bf16[2,2,4,4,8,256]{5,4,3,2,1,0:T(8,128)(2,1)S(1)}, bf16[2,2,4,4,8,256]{5,4,3,2,1,0:T(8,128)(2,1)S(1)}, bf16[2,2,4,4,8,256]{5,4,3,2,1,0:T(8,128)(2,1)S(1)}) custom-call(s32[8,4,128]{2,1,0:T(4,128)S(1)} %reshape.67.w_ref, bf16[8192,256]{1,0:T(8,128)(2,1)S(1)} %bitcast.47), custom_call_target="tpu_custom_call" | custom-call | bytes 65536 | tf_op jit(solution)/shard_map/pallas_call | solution.py:78
  38.8 1.7 %collective-permute-start.8 = (bf16[4,2,4,4,8,256]{5,4,3,2,1,0:T(8,128)(2,1)S(1)}, bf16[4,2,4,4,8,256]{5,4,3,2,1,0:T(8,128)(2,1)S(1)}, u32[]{:S(2)}, u32[]{:S(2)}) collective-permute-start(bf16[4,2,4,4,8,256]{5,4,3,2,1,0:T(8,128)(2,1)S(1)} %get-tuple-element.25), channel_id=1, source_target_pairs={{0,18},{1,19},{2,16},{3,17},{16,2},{17,3},{18,0},{19,1},{4,22},{5,... | collective-permute-start | bytes 1572872 | tf_op jit(solution)/shard_map/ppermute | solution.py:29
  40.5 4.7 %collective-permute-start.5 = (bf16[2,2,4,4,8,256]{5,4,3,2,1,0:T(8,128)(2,1)S(1)}, bf16[2,2,4,4,8,256]{5,4,3,2,1,0:T(8,128)(2,1)S(1)}, u32[]{:S(2)}, u32[]{:S(2)}) collective-permute-start(bf16[2,2,4,4,8,256]{5,4,3,2,1,0:T(8,128)(2,1)S(1)} %get-tuple-element.22), channel_id=1, source_target_pairs={{0,8},{1,9},{2,10},{3,11},{16,24},{17,25},{18,26},{19,27},{4,12},{... | collective-permute-start | bytes 786440 | tf_op jit(solution)/shard_map/ppermute | solution.py:29
  45.2 4.8 %collective-permute-done.4.refs_1_ = bf16[2,2,4,4,8,256]{5,4,3,2,1,0:T(8,128)(2,1)S(1)} collective-permute-done((bf16[2,2,4,4,8,256]{5,4,3,2,1,0:T(8,128)(2,1)S(1)}, bf16[2,2,4,4,8,256]{5,4,3,2,1,0:T(8,128)(2,1)S(1)}, u32[]{:S(2)}, u32[]{:S(2)}) %collective-permute-start.4) | collective-permute-done | bytes 262176 | tf_op jit(solution)/shard_map/ppermute | solution.py:29
  50.0 5.5 %collective-permute-done.5.refs_2_ = bf16[2,2,4,4,8,256]{5,4,3,2,1,0:T(8,128)(2,1)S(1)} collective-permute-done((bf16[2,2,4,4,8,256]{5,4,3,2,1,0:T(8,128)(2,1)S(1)}, bf16[2,2,4,4,8,256]{5,4,3,2,1,0:T(8,128)(2,1)S(1)}, u32[]{:S(2)}, u32[]{:S(2)}) %collective-permute-start.5) | collective-permute-done | bytes 262176 | tf_op jit(solution)/shard_map/ppermute | solution.py:29
  55.6 1.7 %collective-permute-start.7 = (bf16[4,2,4,4,8,256]{5,4,3,2,1,0:T(8,128)(2,1)S(1)}, bf16[4,2,4,4,8,256]{5,4,3,2,1,0:T(8,128)(2,1)S(1)}, u32[]{:S(2)}, u32[]{:S(2)}) collective-permute-start(bf16[4,2,4,4,8,256]{5,4,3,2,1,0:T(8,128)(2,1)S(1)} %shard_map.69), channel_id=1, source_target_pairs={{0,18},{1,19},{2,16},{3,17},{16,2},{17,3},{18,0},{19,1},{4,22},{5,... | collective-permute-start | bytes 1572872 | tf_op jit(solution)/shard_map/ppermute | solution.py:29
  58.3 2.0 %collective-permute-start.11 = (bf16[2,2,4,4,8,256]{5,4,3,2,1,0:T(8,128)(2,1)S(1)}, bf16[2,2,4,4,8,256]{5,4,3,2,1,0:T(8,128)(2,1)S(1)}, u32[]{:S(2)}, u32[]{:S(2)}) collective-permute-start(bf16[2,2,4,4,8,256]{5,4,3,2,1,0:T(8,128)(2,1)S(1)} %get-tuple-element.28), channel_id=1, source_target_pairs={{0,12},{1,13},{2,14},{3,15},{16,28},{17,29},{18,30},{19,31},{4,0},... | collective-permute-start | bytes 786440 | tf_op jit(solution)/shard_map/ppermute | solution.py:29
  60.3 7.7 %collective-permute-done.10.refs_8_ = bf16[2,2,4,4,8,256]{5,4,3,2,1,0:T(8,128)(2,1)S(1)} collective-permute-done((bf16[2,2,4,4,8,256]{5,4,3,2,1,0:T(8,128)(2,1)S(1)}, bf16[2,2,4,4,8,256]{5,4,3,2,1,0:T(8,128)(2,1)S(1)}, u32[]{:S(2)}, u32[]{:S(2)}) %collective-permute-start.10) | collective-permute-done | bytes 262176 | tf_op jit(solution)/shard_map/ppermute | solution.py:29
  68.0 3.8 %collective-permute-done.11.refs_9_ = bf16[2,2,4,4,8,256]{5,4,3,2,1,0:T(8,128)(2,1)S(1)} collective-permute-done((bf16[2,2,4,4,8,256]{5,4,3,2,1,0:T(8,128)(2,1)S(1)}, bf16[2,2,4,4,8,256]{5,4,3,2,1,0:T(8,128)(2,1)S(1)}, u32[]{:S(2)}, u32[]{:S(2)}) %collective-permute-start.11) | collective-permute-done | bytes 262176 | tf_op jit(solution)/shard_map/ppermute | solution.py:29
  72.1 2.6 %collective-permute-done.12.refs_10_ = bf16[16,4,4,8,256]{4,3,2,1,0:T(8,128)(2,1)S(1)} collective-permute-done((bf16[16,4,4,8,256]{4,3,2,1,0:T(8,128)(2,1)S(1)}, bf16[16,4,4,8,256]{4,3,2,1,0:T(8,128)(2,1)S(1)}, u32[]{:S(2)}, u32[]{:S(2)}) %collective-permute-start.12) | collective-permute-done | bytes 1048608 | tf_op jit(solution)/shard_map/ppermute | solution.py:29
  74.6 2.3 %shard_map.73 = bf16[8,256,256]{2,1,0:T(8,128)(2,1)} custom-call(s32[8,256]{1,0:T(8,128)S(1)} %fusion.26.p_ref, bf16[2,2,4,4,8,256]{5,4,3,2,1,0:T(8,128)(2,1)S(1)} %get-tuple-element.20.refs_0_, bf16[2,2,4,4,8,256]{5,4,3,2,1,0:T(8,128)(2,1)S(1)} %collective-permute-done.4.refs_1_, bf16[2,2,4,4,8,256]{5,4,3,2,1,0:T(8,128)(2,1)S(1)} %collective-permute-done.5.refs_2_, ...), custom_call_target="tpu_custom_call" | custom-call | bytes 65536 | tf_op jit(solution)/shard_map/pallas_call | solution.py:78
  76.9 2.9 %all-to-all-done.1.m_ref = bf16[8,1024,256]{2,1,0:T(8,128)(2,1)} async-done(((bf16[8,1024,256]{2,1,0:T(8,128)(2,1)}), bf16[8,1024,256]{2,1,0:T(8,128)(2,1)}, u32[]{:S(2)}, u32[]{:S(2)}) %all-to-all-start.1) | async-done | bytes 4194336 | tf_op jit(solution)/shard_map/all_to_all | solution.py:300
  79.8 3.7 %all-to-all-start.2 = ((bf16[8,256,256]{2,1,0:T(8,128)(2,1)}), bf16[8,256,256]{2,1,0:T(8,128)(2,1)S(1)}, u32[]{:S(2)}, u32[]{:S(2)}) async-start(bf16[8,256,256]{2,1,0:T(8,128)(2,1)} %shard_map.73), calls=%async_computation.2 | async-start | bytes 2097152 | tf_op jit(solution)/shard_map/all_to_all | solution.py:347
  83.7 1.3 %copy-done.1 = bf16[256,2560]{1,0:T(8,128)(2,1)S(1)} copy-done((bf16[256,2560]{1,0:T(8,128)(2,1)S(1)}, bf16[256,2560]{1,0:T(8,128)(2,1)}, u32[]{:S(2)}) %copy-start.1) | copy-done | bytes 1310744
  85.0 8.1 %shard_map.74 = (bf16[1024,2048]{1,0:T(8,128)(2,1)}, f32[8,256,256]{2,1,0:T(8,128)S(1)}) custom-call(bf16[8,1024,256]{2,1,0:T(8,128)(2,1)} %all-to-all-done.1.m_ref, bf16[256,2560]{1,0:T(8,128)(2,1)S(1)} %copy-done.1, bf16[2560,2048]{1,0:T(8,128)(2,1)} %w_ref.1, f32[1,256]{1,0:T(1,128)S(1)} %bitcast.48), custom_call_target="tpu_custom_call" | custom-call | flops 2684354560 | bytes 20185088 | tf_op jit(solution)/shard_map/pallas_call | solution.py:196
  93.2 4.4 %all-to-all-done.2.r_ref = bf16[8,256,256]{2,1,0:T(8,128)(2,1)S(1)} async-done(((bf16[8,256,256]{2,1,0:T(8,128)(2,1)}), bf16[8,256,256]{2,1,0:T(8,128)(2,1)S(1)}, u32[]{:S(2)}, u32[]{:S(2)}) %all-to-all-start.2) | async-done | bytes 1048608 | tf_op jit(solution)/shard_map/all_to_all | solution.py:347
  97.6 1.9 %shard_map.75 = bf16[256,8,256]{2,1,0:T(8,128)(2,1)} custom-call(s32[256,1]{1,0:T(8,128)S(1)} %copy.33.s_ref, bf16[8,256,256]{2,1,0:T(8,128)(2,1)S(1)} %all-to-all-done.2.r_ref, f32[8,256,256]{2,1,0:T(8,128)S(1)} %get-tuple-element.33.n_ref), custom_call_target="tpu_custom_call" | custom-call | flops 3145728 | bytes 4194304 | tf_op jit(solution)/shard_map/pallas_call | solution.py:247
  (45 shorter events, 7.1 us)
Async XLA Ops:
  16.8 62.9 %all-to-all-start.1 = ((bf16[8,1024,256]{2,1,0:T(8,128)(2,1)}), bf16[8,1024,256]{2,1,0:T(8,128)(2,1)}, u32[]{:S(2)}, u32[]{:S(2)}) async-start(bf16[8,1024,256]{2,1,0:T(8,128)(2,1)} %bitcast.45), calls=%async_computation.1 | async-start | bytes 8388608 | tf_op jit(solution)/shard_map/all_to_all | solution.py:300
  24.4 1.3 %collective-permute-start = (s32[2,4,8,32]{3,2,1,0:T(8,128)S(1)}, s32[2,4,8,32]{3,2,1,0:T(8,128)S(1)}, u32[]{:S(2)}, u32[]{:S(2)}) collective-permute-start(s32[2,4,8,32]{3,2,1,0:T(8,128)S(1)} %squeeze.17), channel_id=1, source_target_pairs={{0,1},{1,0},{2,3},{3,2},{16,17},{17,16},{18,19},{19,18},{4,5},{5,4... | collective-permute-start | bytes 24584 | tf_op jit(solution)/shard_map/ppermute | solution.py:29
  25.7 6.3 %collective-permute-start.2 = (s32[2,2,8,32]{3,2,1,0:T(8,128)S(1)}, s32[2,2,8,32]{3,2,1,0:T(8,128)S(1)}, u32[]{:S(2)}, u32[]{:S(2)}) collective-permute-start(s32[2,2,8,32]{3,2,1,0:T(8,128)S(1)} %get-tuple-element.45), channel_id=1, source_target_pairs={{0,8},{1,9},{2,10},{3,11},{16,24},{17,25},{18,26},{19,27},{4,12},{... | collective-permute-start | bytes 12296 | tf_op jit(solution)/shard_map/ppermute | solution.py:29
  28.9 4.9 %collective-permute-start.3 = (s32[2,2,8,32]{3,2,1,0:T(8,128)S(1)}, s32[2,2,8,32]{3,2,1,0:T(8,128)S(1)}, u32[]{:S(2)}, u32[]{:S(2)}) collective-permute-start(s32[2,2,8,32]{3,2,1,0:T(8,128)S(1)} %get-tuple-element.44), channel_id=1, source_target_pairs={{0,4},{1,5},{2,6},{3,7},{16,20},{17,21},{18,22},{19,23},{4,8},{5,9... | collective-permute-start | bytes 12296 | tf_op jit(solution)/shard_map/ppermute | solution.py:29
  29.4 4.4 %collective-permute-start.1 = (s32[2,2,8,32]{3,2,1,0:T(8,128)S(1)}, s32[2,2,8,32]{3,2,1,0:T(8,128)S(1)}, u32[]{:S(2)}, u32[]{:S(2)}) collective-permute-start(s32[2,2,8,32]{3,2,1,0:T(8,128)S(1)} %get-tuple-element.43), channel_id=1, source_target_pairs={{0,12},{1,13},{2,14},{3,15},{16,28},{17,29},{18,30},{19,31},{4,0},... | collective-permute-start | bytes 12296 | tf_op jit(solution)/shard_map/ppermute | solution.py:29
  34.0 2.2 %copy-start = (bf16[1,8192,256]{2,1,0:T(8,128)(2,1)S(1)}, bf16[1,8192,256]{2,1,0:T(8,128)(2,1)}, u32[]{:S(2)}) copy-start(bf16[1,8192,256]{2,1,0:T(8,128)(2,1)} %param.5) | copy-start | bytes 12582916
  38.8 18.5 %collective-permute-start.8 = (bf16[4,2,4,4,8,256]{5,4,3,2,1,0:T(8,128)(2,1)S(1)}, bf16[4,2,4,4,8,256]{5,4,3,2,1,0:T(8,128)(2,1)S(1)}, u32[]{:S(2)}, u32[]{:S(2)}) collective-permute-start(bf16[4,2,4,4,8,256]{5,4,3,2,1,0:T(8,128)(2,1)S(1)} %get-tuple-element.25), channel_id=1, source_target_pairs={{0,18},{1,19},{2,16},{3,17},{16,2},{17,3},{18,0},{19,1},{4,22},{5,... | collective-permute-start | bytes 1572872 | tf_op jit(solution)/shard_map/ppermute | solution.py:29
  40.5 9.5 %collective-permute-start.4 = (bf16[2,2,4,4,8,256]{5,4,3,2,1,0:T(8,128)(2,1)S(1)}, bf16[2,2,4,4,8,256]{5,4,3,2,1,0:T(8,128)(2,1)S(1)}, u32[]{:S(2)}, u32[]{:S(2)}) collective-permute-start(bf16[2,2,4,4,8,256]{5,4,3,2,1,0:T(8,128)(2,1)S(1)} %get-tuple-element.21), channel_id=1, source_target_pairs={{0,4},{1,5},{2,6},{3,7},{16,20},{17,21},{18,22},{19,23},{4,8},{5,9... | collective-permute-start | bytes 786440 | tf_op jit(solution)/shard_map/ppermute | solution.py:29
  40.5 15.1 %collective-permute-start.5 = (bf16[2,2,4,4,8,256]{5,4,3,2,1,0:T(8,128)(2,1)S(1)}, bf16[2,2,4,4,8,256]{5,4,3,2,1,0:T(8,128)(2,1)S(1)}, u32[]{:S(2)}, u32[]{:S(2)}) collective-permute-start(bf16[2,2,4,4,8,256]{5,4,3,2,1,0:T(8,128)(2,1)S(1)} %get-tuple-element.22), channel_id=1, source_target_pairs={{0,8},{1,9},{2,10},{3,11},{16,24},{17,25},{18,26},{19,27},{4,12},{... | collective-permute-start | bytes 786440 | tf_op jit(solution)/shard_map/ppermute | solution.py:29
  45.2 10.4 %collective-permute-start.6 = (bf16[2,2,4,4,8,256]{5,4,3,2,1,0:T(8,128)(2,1)S(1)}, bf16[2,2,4,4,8,256]{5,4,3,2,1,0:T(8,128)(2,1)S(1)}, u32[]{:S(2)}, u32[]{:S(2)}) collective-permute-start(bf16[2,2,4,4,8,256]{5,4,3,2,1,0:T(8,128)(2,1)S(1)} %get-tuple-element.23), channel_id=1, source_target_pairs={{0,12},{1,13},{2,14},{3,15},{16,28},{17,29},{18,30},{19,31},{4,0},... | collective-permute-start | bytes 786440 | tf_op jit(solution)/shard_map/ppermute | solution.py:29
  55.6 16.2 %collective-permute-start.7 = (bf16[4,2,4,4,8,256]{5,4,3,2,1,0:T(8,128)(2,1)S(1)}, bf16[4,2,4,4,8,256]{5,4,3,2,1,0:T(8,128)(2,1)S(1)}, u32[]{:S(2)}, u32[]{:S(2)}) collective-permute-start(bf16[4,2,4,4,8,256]{5,4,3,2,1,0:T(8,128)(2,1)S(1)} %shard_map.69), channel_id=1, source_target_pairs={{0,18},{1,19},{2,16},{3,17},{16,2},{17,3},{18,0},{19,1},{4,22},{5,... | collective-permute-start | bytes 1572872 | tf_op jit(solution)/shard_map/ppermute | solution.py:29
  57.3 10.7 %collective-permute-start.10 = (bf16[2,2,4,4,8,256]{5,4,3,2,1,0:T(8,128)(2,1)S(1)}, bf16[2,2,4,4,8,256]{5,4,3,2,1,0:T(8,128)(2,1)S(1)}, u32[]{:S(2)}, u32[]{:S(2)}) collective-permute-start(bf16[2,2,4,4,8,256]{5,4,3,2,1,0:T(8,128)(2,1)S(1)} %get-tuple-element.27), channel_id=1, source_target_pairs={{0,8},{1,9},{2,10},{3,11},{16,24},{17,25},{18,26},{19,27},{4,12},{... | collective-permute-start | bytes 786440 | tf_op jit(solution)/shard_map/ppermute | solution.py:29
  58.3 13.5 %collective-permute-start.11 = (bf16[2,2,4,4,8,256]{5,4,3,2,1,0:T(8,128)(2,1)S(1)}, bf16[2,2,4,4,8,256]{5,4,3,2,1,0:T(8,128)(2,1)S(1)}, u32[]{:S(2)}, u32[]{:S(2)}) collective-permute-start(bf16[2,2,4,4,8,256]{5,4,3,2,1,0:T(8,128)(2,1)S(1)} %get-tuple-element.28), channel_id=1, source_target_pairs={{0,12},{1,13},{2,14},{3,15},{16,28},{17,29},{18,30},{19,31},{4,0},... | collective-permute-start | bytes 786440 | tf_op jit(solution)/shard_map/ppermute | solution.py:29
  60.3 11.5 %collective-permute-start.9 = (bf16[2,2,4,4,8,256]{5,4,3,2,1,0:T(8,128)(2,1)S(1)}, bf16[2,2,4,4,8,256]{5,4,3,2,1,0:T(8,128)(2,1)S(1)}, u32[]{:S(2)}, u32[]{:S(2)}) collective-permute-start(bf16[2,2,4,4,8,256]{5,4,3,2,1,0:T(8,128)(2,1)S(1)} %get-tuple-element.26), channel_id=1, source_target_pairs={{0,4},{1,5},{2,6},{3,7},{16,20},{17,21},{18,22},{19,23},{4,8},{5,9... | collective-permute-start | bytes 786440 | tf_op jit(solution)/shard_map/ppermute | solution.py:29
  71.9 11.7 %copy-start.3 = (s32[256]{0:T(256)S(1)}, s32[256]{0:T(256)}, u32[]{:S(2)}) copy-start(s32[256]{0:T(256)} %param.6) | copy-start | bytes 3076
  71.9 11.8 %copy-start.2 = (f32[256]{0:T(256)S(1)}, f32[256]{0:T(256)}, u32[]{:S(2)}) copy-start(f32[256]{0:T(256)} %param.9) | copy-start | bytes 3076
  71.9 2.7 %collective-permute-start.12 = (bf16[16,4,4,8,256]{4,3,2,1,0:T(8,128)(2,1)S(1)}, bf16[16,4,4,8,256]{4,3,2,1,0:T(8,128)(2,1)S(1)}, u32[]{:S(2)}, u32[]{:S(2)}) collective-permute-start(bf16[16,4,4,8,256]{4,3,2,1,0:T(8,128)(2,1)S(1)} %shard_map.72), channel_id=1, source_target_pairs={{0,1},{1,0},{2,3},{3,2},{16,17},{17,16},{18,19},{19,18},{4,5},{5,4... | collective-permute-start | bytes 3145736 | tf_op jit(solution)/shard_map/ppermute | solution.py:29
  79.8 17.8 %all-to-all-start.2 = ((bf16[8,256,256]{2,1,0:T(8,128)(2,1)}), bf16[8,256,256]{2,1,0:T(8,128)(2,1)S(1)}, u32[]{:S(2)}, u32[]{:S(2)}) async-start(bf16[8,256,256]{2,1,0:T(8,128)(2,1)} %shard_map.73), calls=%async_computation.2 | async-start | bytes 2097152 | tf_op jit(solution)/shard_map/all_to_all | solution.py:347
  83.7 1.3 %copy-start.1 = (bf16[256,2560]{1,0:T(8,128)(2,1)S(1)}, bf16[256,2560]{1,0:T(8,128)(2,1)}, u32[]{:S(2)}) copy-start(bf16[256,2560]{1,0:T(8,128)(2,1)} %h_hbm) | copy-start | bytes 3932164

commit v6 on v5

--- a/solution.py
+++ b/solution.py
@@ -187,7 +187,8 @@
         for l in range(layers):
             proj = acc_ref[:, l * width : (l + 1) * width]
             mean_sq = jnp.mean(proj * proj, axis=-1, keepdims=True)
-            o_ref[l] = proj / jnp.sqrt(mean_sq + 1e-06) * g_ref[...]
+            normed = proj / jnp.sqrt(mean_sq + 1e-06) * g_ref[...]
+            o_ref[l] = normed / math.sqrt(2.0)
         for l in range(layers):
             writes[l].wait()
 
@@ -236,7 +237,7 @@
                     r_ref[l ^ 1, here].astype(jnp.float32),
                     r_ref[l, here].astype(jnp.float32),
                 )
-                acc_ref[:, l, :] = (n_ref[l, here] + math.sqrt(width) * emb) / math.sqrt(2.0)
+                acc_ref[:, l, :] = n_ref[l, here] + math.sqrt(width / 2.0) * emb
             out_ref[here] = acc_ref[...].astype(jnp.bfloat16)
             copies.append(pltpu.make_async_copy(out_ref.at[here], o_ref.at[here], sem.at[q]))
             copies[q].start()

time: 100 us -> 100 us (level)
  no operation moved by 1% of the time
where the time goes in v6:
time: 100 us; the launch traced here: 99.6 us
  waiting for transfers between devices  34 us (34%)
  starting transfers between devices  25.9 us (26%)
  blocking collectives  15.5 us (16%)
  Pallas kernels  15 us (15%)
  local copies, waits for them, and re-layouts  5.78 us (6%)
  other arithmetic  2.33 us (2%)
  between operations  1.06 us (1%)
    ppermute x13, waiting for transfers between devices, send(): return lax.ppermute(value, BOTH, moves)  26.7 us
    ppermute x13, starting transfers between devices, send(): return lax.ppermute(value, BOTH, moves)  17.6 us
    all_to_all x1, blocking collectives, on_device(): lax.all_to_all(jnp.broadcast_to(token_ids[None, None], (2 * n_grp, 1, tok...  15.5 us
    pallas_call x1, Pallas kernels, serve_and_project(): pl.pallas_call(body, in_specs=[hbm, hbm, hbm, vmem], out_specs=[hbm, vmem...  8.12 us
    pallas_call x6, Pallas kernels, near_call(): pl.pallas_call(body, in_specs=[vmem] * len(operands), out_specs=[vmem] *...  5.01 us
    all_to_all x1, starting transfers between devices, on_device(): lax.all_to_all(gated, 'grp', split_axis=0, concat_axis=0, tiled=True)  4.56 us
    all_to_all x1, waiting for transfers between devices, on_device(): lax.all_to_all(sorted_rows, 'grp', split_axis=0, concat_axis=0, tiled=True)  4.44 us
    all_to_all x1, starting transfers between devices, on_device(): lax.all_to_all(sorted_rows, 'grp', split_axis=0, concat_axis=0, tiled=True)  3.74 us
  transfers between devices with their start and end apart: 15, of which 9 were waited for; matrix products, arithmetic and copies ran while one was open for 4% of the time, Pallas kernels for 13%

profile of v6, /device:TPU:0, one launch (start us, length us, event | category | flops | bytes accessed | tf_op | source)
XLA Modules:
  0.0 99.6 jit_solution(6299845953780270457)
XLA Ops:
  1.3 15.5 %all_to_all.15 = s32[16,1,256]{2,1,0:T(1,128)S(1)} all-to-all(s32[16,1,256]{2,1,0:T(1,128)S(1)} %broadcast_in_dim.3), channel_id=1, replica_groups={{0,16,32,48,64,80,96,112,2,18,34,50,66,82,98,114},{1,17,33,49,65,81,97,..., dimensions={0} | all-to-all | bytes 32768 | tf_op jit(solution)/shard_map/all_to_all | solution.py:292
  16.8 4.6 %all-to-all-start.1 = ((bf16[8,1024,256]{2,1,0:T(8,128)(2,1)}), bf16[8,1024,256]{2,1,0:T(8,128)(2,1)}, u32[]{:S(2)}, u32[]{:S(2)}) async-start(bf16[8,1024,256]{2,1,0:T(8,128)(2,1)} %bitcast.45), calls=%async_computation.1 | async-start | bytes 8388608 | tf_op jit(solution)/shard_map/all_to_all | solution.py:301
  21.5 1.3 %convert_reduce_fusion = s32[2,8,256]{2,1,0:T(8,128)S(1)} fusion(s32[2,8,256]{2,1,0:T(8,128)S(1)} %get-tuple-element.39, pred[256,256]{1,0:T(8,128)(4,1)S(1)} %iota_compare_fusion.1), kind=kLoop, calls=%fused_computation.2 | loop fusion | flops 4190208 | bytes 98304 | tf_op jit(solution)/shard_map/reduce_sum | solution.py:313
  25.7 3.1 %collective-permute-start.2 = (s32[2,2,8,32]{3,2,1,0:T(8,128)S(1)}, s32[2,2,8,32]{3,2,1,0:T(8,128)S(1)}, u32[]{:S(2)}, u32[]{:S(2)}) collective-permute-start(s32[2,2,8,32]{3,2,1,0:T(8,128)S(1)} %get-tuple-element.45), channel_id=1, source_target_pairs={{0,8},{1,9},{2,10},{3,11},{16,24},{17,25},{18,26},{19,27},{4,12},{... | collective-permute-start | bytes 12296 | tf_op jit(solution)/shard_map/ppermute | solution.py:29
  29.4 2.6 %collective-permute-start.1 = (s32[2,2,8,32]{3,2,1,0:T(8,128)S(1)}, s32[2,2,8,32]{3,2,1,0:T(8,128)S(1)}, u32[]{:S(2)}, u32[]{:S(2)}) collective-permute-start(s32[2,2,8,32]{3,2,1,0:T(8,128)S(1)} %get-tuple-element.43), channel_id=1, source_target_pairs={{0,12},{1,13},{2,14},{3,15},{16,28},{17,29},{18,30},{19,31},{4,0},... | collective-permute-start | bytes 12296 | tf_op jit(solution)/shard_map/ppermute | solution.py:29
  32.1 1.7 %collective-permute-done.3 = s32[2,2,8,32]{3,2,1,0:T(8,128)S(1)} collective-permute-done((s32[2,2,8,32]{3,2,1,0:T(8,128)S(1)}, s32[2,2,8,32]{3,2,1,0:T(8,128)S(1)}, u32[]{:S(2)}, u32[]{:S(2)}) %collective-permute-start.3) | collective-permute-done | bytes 4128 | tf_op jit(solution)/shard_map/ppermute | solution.py:29
  34.0 2.2 %copy-done = bf16[1,8192,256]{2,1,0:T(8,128)(2,1)S(1)} copy-done((bf16[1,8192,256]{2,1,0:T(8,128)(2,1)S(1)}, bf16[1,8192,256]{2,1,0:T(8,128)(2,1)}, u32[]{:S(2)}) %copy-start) | copy-done | bytes 4194328
  37.5 1.3 %shard_map.68 = (bf16[2,2,4,4,8,256]{5,4,3,2,1,0:T(8,128)(2,1)S(1)}, bf16[2,2,4,4,8,256]{5,4,3,2,1,0:T(8,128)(2,1)S(1)}, bf16[2,2,4,4,8,256]{5,4,3,2,1,0:T(8,128)(2,1)S(1)}, bf16[2,2,4,4,8,256]{5,4,3,2,1,0:T(8,128)(2,1)S(1)}) custom-call(s32[8,4,128]{2,1,0:T(4,128)S(1)} %reshape.67.w_ref, bf16[8192,256]{1,0:T(8,128)(2,1)S(1)} %bitcast.47), custom_call_target="tpu_custom_call" | custom-call | bytes 65536 | tf_op jit(solution)/shard_map/pallas_call | solution.py:78
  38.8 1.7 %collective-permute-start.8 = (bf16[4,2,4,4,8,256]{5,4,3,2,1,0:T(8,128)(2,1)S(1)}, bf16[4,2,4,4,8,256]{5,4,3,2,1,0:T(8,128)(2,1)S(1)}, u32[]{:S(2)}, u32[]{:S(2)}) collective-permute-start(bf16[4,2,4,4,8,256]{5,4,3,2,1,0:T(8,128)(2,1)S(1)} %get-tuple-element.25), channel_id=1, source_target_pairs={{0,18},{1,19},{2,16},{3,17},{16,2},{17,3},{18,0},{19,1},{4,22},{5,... | collective-permute-start | bytes 1572872 | tf_op jit(solution)/shard_map/ppermute | solution.py:29
  40.5 4.7 %collective-permute-start.5 = (bf16[2,2,4,4,8,256]{5,4,3,2,1,0:T(8,128)(2,1)S(1)}, bf16[2,2,4,4,8,256]{5,4,3,2,1,0:T(8,128)(2,1)S(1)}, u32[]{:S(2)}, u32[]{:S(2)}) collective-permute-start(bf16[2,2,4,4,8,256]{5,4,3,2,1,0:T(8,128)(2,1)S(1)} %get-tuple-element.22), channel_id=1, source_target_pairs={{0,8},{1,9},{2,10},{3,11},{16,24},{17,25},{18,26},{19,27},{4,12},{... | collective-permute-start | bytes 786440 | tf_op jit(solution)/shard_map/ppermute | solution.py:29
  45.2 4.8 %collective-permute-done.4.refs_1_ = bf16[2,2,4,4,8,256]{5,4,3,2,1,0:T(8,128)(2,1)S(1)} collective-permute-done((bf16[2,2,4,4,8,256]{5,4,3,2,1,0:T(8,128)(2,1)S(1)}, bf16[2,2,4,4,8,256]{5,4,3,2,1,0:T(8,128)(2,1)S(1)}, u32[]{:S(2)}, u32[]{:S(2)}) %collective-permute-start.4) | collective-permute-done | bytes 262176 | tf_op jit(solution)/shard_map/ppermute | solution.py:29
  50.0 5.5 %collective-permute-done.5.refs_2_ = bf16[2,2,4,4,8,256]{5,4,3,2,1,0:T(8,128)(2,1)S(1)} collective-permute-done((bf16[2,2,4,4,8,256]{5,4,3,2,1,0:T(8,128)(2,1)S(1)}, bf16[2,2,4,4,8,256]{5,4,3,2,1,0:T(8,128)(2,1)S(1)}, u32[]{:S(2)}, u32[]{:S(2)}) %collective-permute-start.5) | collective-permute-done | bytes 262176 | tf_op jit(solution)/shard_map/ppermute | solution.py:29
  55.6 1.7 %collective-permute-start.7 = (bf16[4,2,4,4,8,256]{5,4,3,2,1,0:T(8,128)(2,1)S(1)}, bf16[4,2,4,4,8,256]{5,4,3,2,1,0:T(8,128)(2,1)S(1)}, u32[]{:S(2)}, u32[]{:S(2)}) collective-permute-start(bf16[4,2,4,4,8,256]{5,4,3,2,1,0:T(8,128)(2,1)S(1)} %shard_map.69), channel_id=1, source_target_pairs={{0,18},{1,19},{2,16},{3,17},{16,2},{17,3},{18,0},{19,1},{4,22},{5,... | collective-permute-start | bytes 1572872 | tf_op jit(solution)/shard_map/ppermute | solution.py:29
  58.3 2.0 %collective-permute-start.11 = (bf16[2,2,4,4,8,256]{5,4,3,2,1,0:T(8,128)(2,1)S(1)}, bf16[2,2,4,4,8,256]{5,4,3,2,1,0:T(8,128)(2,1)S(1)}, u32[]{:S(2)}, u32[]{:S(2)}) collective-permute-start(bf16[2,2,4,4,8,256]{5,4,3,2,1,0:T(8,128)(2,1)S(1)} %get-tuple-element.28), channel_id=1, source_target_pairs={{0,12},{1,13},{2,14},{3,15},{16,28},{17,29},{18,30},{19,31},{4,0},... | collective-permute-start | bytes 786440 | tf_op jit(solution)/shard_map/ppermute | solution.py:29
  60.3 7.7 %collective-permute-done.10.refs_8_ = bf16[2,2,4,4,8,256]{5,4,3,2,1,0:T(8,128)(2,1)S(1)} collective-permute-done((bf16[2,2,4,4,8,256]{5,4,3,2,1,0:T(8,128)(2,1)S(1)}, bf16[2,2,4,4,8,256]{5,4,3,2,1,0:T(8,128)(2,1)S(1)}, u32[]{:S(2)}, u32[]{:S(2)}) %collective-permute-start.10) | collective-permute-done | bytes 262176 | tf_op jit(solution)/shard_map/ppermute | solution.py:29
  68.0 3.8 %collective-permute-done.11.refs_9_ = bf16[2,2,4,4,8,256]{5,4,3,2,1,0:T(8,128)(2,1)S(1)} collective-permute-done((bf16[2,2,4,4,8,256]{5,4,3,2,1,0:T(8,128)(2,1)S(1)}, bf16[2,2,4,4,8,256]{5,4,3,2,1,0:T(8,128)(2,1)S(1)}, u32[]{:S(2)}, u32[]{:S(2)}) %collective-permute-start.11) | collective-permute-done | bytes 262176 | tf_op jit(solution)/shard_map/ppermute | solution.py:29
  72.1 2.6 %collective-permute-done.12.refs_10_ = bf16[16,4,4,8,256]{4,3,2,1,0:T(8,128)(2,1)S(1)} collective-permute-done((bf16[16,4,4,8,256]{4,3,2,1,0:T(8,128)(2,1)S(1)}, bf16[16,4,4,8,256]{4,3,2,1,0:T(8,128)(2,1)S(1)}, u32[]{:S(2)}, u32[]{:S(2)}) %collective-permute-start.12) | collective-permute-done | bytes 1048608 | tf_op jit(solution)/shard_map/ppermute | solution.py:29
  74.6 2.3 %shard_map.73 = bf16[8,256,256]{2,1,0:T(8,128)(2,1)} custom-call(s32[8,256]{1,0:T(8,128)S(1)} %fusion.26.p_ref, bf16[2,2,4,4,8,256]{5,4,3,2,1,0:T(8,128)(2,1)S(1)} %get-tuple-element.20.refs_0_, bf16[2,2,4,4,8,256]{5,4,3,2,1,0:T(8,128)(2,1)S(1)} %collective-permute-done.4.refs_1_, bf16[2,2,4,4,8,256]{5,4,3,2,1,0:T(8,128)(2,1)S(1)} %collective-permute-done.5.refs_2_, ...), custom_call_target="tpu_custom_call" | custom-call | bytes 65536 | tf_op jit(solution)/shard_map/pallas_call | solution.py:78
  76.9 2.9 %all-to-all-done.1.m_ref = bf16[8,1024,256]{2,1,0:T(8,128)(2,1)} async-done(((bf16[8,1024,256]{2,1,0:T(8,128)(2,1)}), bf16[8,1024,256]{2,1,0:T(8,128)(2,1)}, u32[]{:S(2)}, u32[]{:S(2)}) %all-to-all-start.1) | async-done | bytes 4194336 | tf_op jit(solution)/shard_map/all_to_all | solution.py:301
  79.8 3.7 %all-to-all-start.2 = ((bf16[8,256,256]{2,1,0:T(8,128)(2,1)}), bf16[8,256,256]{2,1,0:T(8,128)(2,1)S(1)}, u32[]{:S(2)}, u32[]{:S(2)}) async-start(bf16[8,256,256]{2,1,0:T(8,128)(2,1)} %shard_map.73), calls=%async_computation.2 | async-start | bytes 2097152 | tf_op jit(solution)/shard_map/all_to_all | solution.py:348
  83.7 1.3 %copy-done.1 = bf16[256,2560]{1,0:T(8,128)(2,1)S(1)} copy-done((bf16[256,2560]{1,0:T(8,128)(2,1)S(1)}, bf16[256,2560]{1,0:T(8,128)(2,1)}, u32[]{:S(2)}) %copy-start.1) | copy-done | bytes 1310744
  85.0 8.1 %shard_map.74 = (bf16[1024,2048]{1,0:T(8,128)(2,1)}, f32[8,256,256]{2,1,0:T(8,128)S(1)}) custom-call(bf16[8,1024,256]{2,1,0:T(8,128)(2,1)} %all-to-all-done.1.m_ref, bf16[256,2560]{1,0:T(8,128)(2,1)S(1)} %copy-done.1, bf16[2560,2048]{1,0:T(8,128)(2,1)} %w_ref.1, f32[1,256]{1,0:T(1,128)S(1)} %bitcast.48), custom_call_target="tpu_custom_call" | custom-call | flops 2684354560 | bytes 20185088 | tf_op jit(solution)/shard_map/pallas_call | solution.py:197
  93.2 4.4 %all-to-all-done.2.r_ref = bf16[8,256,256]{2,1,0:T(8,128)(2,1)S(1)} async-done(((bf16[8,256,256]{2,1,0:T(8,128)(2,1)}), bf16[8,256,256]{2,1,0:T(8,128)(2,1)S(1)}, u32[]{:S(2)}, u32[]{:S(2)}) %all-to-all-start.2) | async-done | bytes 1048608 | tf_op jit(solution)/shard_map/all_to_all | solution.py:348
  97.6 1.9 %shard_map.75 = bf16[256,8,256]{2,1,0:T(8,128)(2,1)} custom-call(s32[256,1]{1,0:T(8,128)S(1)} %copy.33.s_ref, bf16[8,256,256]{2,1,0:T(8,128)(2,1)S(1)} %all-to-all-done.2.r_ref, f32[8,256,256]{2,1,0:T(8,128)S(1)} %get-tuple-element.33.n_ref), custom_call_target="tpu_custom_call" | custom-call | flops 3145728 | bytes 4194304 | tf_op jit(solution)/shard_map/pallas_call | solution.py:248
  (45 shorter events, 7.1 us)
Async XLA Ops:
  16.8 62.9 %all-to-all-start.1 = ((bf16[8,1024,256]{2,1,0:T(8,128)(2,1)}), bf16[8,1024,256]{2,1,0:T(8,128)(2,1)}, u32[]{:S(2)}, u32[]{:S(2)}) async-start(bf16[8,1024,256]{2,1,0:T(8,128)(2,1)} %bitcast.45), calls=%async_computation.1 | async-start | bytes 8388608 | tf_op jit(solution)/shard_map/all_to_all | solution.py:301
  24.4 1.3 %collective-permute-start = (s32[2,4,8,32]{3,2,1,0:T(8,128)S(1)}, s32[2,4,8,32]{3,2,1,0:T(8,128)S(1)}, u32[]{:S(2)}, u32[]{:S(2)}) collective-permute-start(s32[2,4,8,32]{3,2,1,0:T(8,128)S(1)} %squeeze.17), channel_id=1, source_target_pairs={{0,1},{1,0},{2,3},{3,2},{16,17},{17,16},{18,19},{19,18},{4,5},{5,4... | collective-permute-start | bytes 24584 | tf_op jit(solution)/shard_map/ppermute | solution.py:29
  25.7 6.3 %collective-permute-start.2 = (s32[2,2,8,32]{3,2,1,0:T(8,128)S(1)}, s32[2,2,8,32]{3,2,1,0:T(8,128)S(1)}, u32[]{:S(2)}, u32[]{:S(2)}) collective-permute-start(s32[2,2,8,32]{3,2,1,0:T(8,128)S(1)} %get-tuple-element.45), channel_id=1, source_target_pairs={{0,8},{1,9},{2,10},{3,11},{16,24},{17,25},{18,26},{19,27},{4,12},{... | collective-permute-start | bytes 12296 | tf_op jit(solution)/shard_map/ppermute | solution.py:29
  28.9 4.9 %collective-permute-start.3 = (s32[2,2,8,32]{3,2,1,0:T(8,128)S(1)}, s32[2,2,8,32]{3,2,1,0:T(8,128)S(1)}, u32[]{:S(2)}, u32[]{:S(2)}) collective-permute-start(s32[2,2,8,32]{3,2,1,0:T(8,128)S(1)} %get-tuple-element.44), channel_id=1, source_target_pairs={{0,4},{1,5},{2,6},{3,7},{16,20},{17,21},{18,22},{19,23},{4,8},{5,9... | collective-permute-start | bytes 12296 | tf_op jit(solution)/shard_map/ppermute | solution.py:29
  29.4 4.4 %collective-permute-start.1 = (s32[2,2,8,32]{3,2,1,0:T(8,128)S(1)}, s32[2,2,8,32]{3,2,1,0:T(8,128)S(1)}, u32[]{:S(2)}, u32[]{:S(2)}) collective-permute-start(s32[2,2,8,32]{3,2,1,0:T(8,128)S(1)} %get-tuple-element.43), channel_id=1, source_target_pairs={{0,12},{1,13},{2,14},{3,15},{16,28},{17,29},{18,30},{19,31},{4,0},... | collective-permute-start | bytes 12296 | tf_op jit(solution)/shard_map/ppermute | solution.py:29
  34.0 2.2 %copy-start = (bf16[1,8192,256]{2,1,0:T(8,128)(2,1)S(1)}, bf16[1,8192,256]{2,1,0:T(8,128)(2,1)}, u32[]{:S(2)}) copy-start(bf16[1,8192,256]{2,1,0:T(8,128)(2,1)} %param.5) | copy-start | bytes 12582916
  38.8 18.5 %collective-permute-start.8 = (bf16[4,2,4,4,8,256]{5,4,3,2,1,0:T(8,128)(2,1)S(1)}, bf16[4,2,4,4,8,256]{5,4,3,2,1,0:T(8,128)(2,1)S(1)}, u32[]{:S(2)}, u32[]{:S(2)}) collective-permute-start(bf16[4,2,4,4,8,256]{5,4,3,2,1,0:T(8,128)(2,1)S(1)} %get-tuple-element.25), channel_id=1, source_target_pairs={{0,18},{1,19},{2,16},{3,17},{16,2},{17,3},{18,0},{19,1},{4,22},{5,... | collective-permute-start | bytes 1572872 | tf_op jit(solution)/shard_map/ppermute | solution.py:29
  40.5 9.5 %collective-permute-start.4 = (bf16[2,2,4,4,8,256]{5,4,3,2,1,0:T(8,128)(2,1)S(1)}, bf16[2,2,4,4,8,256]{5,4,3,2,1,0:T(8,128)(2,1)S(1)}, u32[]{:S(2)}, u32[]{:S(2)}) collective-permute-start(bf16[2,2,4,4,8,256]{5,4,3,2,1,0:T(8,128)(2,1)S(1)} %get-tuple-element.21), channel_id=1, source_target_pairs={{0,4},{1,5},{2,6},{3,7},{16,20},{17,21},{18,22},{19,23},{4,8},{5,9... | collective-permute-start | bytes 786440 | tf_op jit(solution)/shard_map/ppermute | solution.py:29
  40.5 15.1 %collective-permute-start.5 = (bf16[2,2,4,4,8,256]{5,4,3,2,1,0:T(8,128)(2,1)S(1)}, bf16[2,2,4,4,8,256]{5,4,3,2,1,0:T(8,128)(2,1)S(1)}, u32[]{:S(2)}, u32[]{:S(2)}) collective-permute-start(bf16[2,2,4,4,8,256]{5,4,3,2,1,0:T(8,128)(2,1)S(1)} %get-tuple-element.22), channel_id=1, source_target_pairs={{0,8},{1,9},{2,10},{3,11},{16,24},{17,25},{18,26},{19,27},{4,12},{... | collective-permute-start | bytes 786440 | tf_op jit(solution)/shard_map/ppermute | solution.py:29
  45.2 10.4 %collective-permute-start.6 = (bf16[2,2,4,4,8,256]{5,4,3,2,1,0:T(8,128)(2,1)S(1)}, bf16[2,2,4,4,8,256]{5,4,3,2,1,0:T(8,128)(2,1)S(1)}, u32[]{:S(2)}, u32[]{:S(2)}) collective-permute-start(bf16[2,2,4,4,8,256]{5,4,3,2,1,0:T(8,128)(2,1)S(1)} %get-tuple-element.23), channel_id=1, source_target_pairs={{0,12},{1,13},{2,14},{3,15},{16,28},{17,29},{18,30},{19,31},{4,0},... | collective-permute-start | bytes 786440 | tf_op jit(solution)/shard_map/ppermute | solution.py:29
  55.6 16.2 %collective-permute-start.7 = (bf16[4,2,4,4,8,256]{5,4,3,2,1,0:T(8,128)(2,1)S(1)}, bf16[4,2,4,4,8,256]{5,4,3,2,1,0:T(8,128)(2,1)S(1)}, u32[]{:S(2)}, u32[]{:S(2)}) collective-permute-start(bf16[4,2,4,4,8,256]{5,4,3,2,1,0:T(8,128)(2,1)S(1)} %shard_map.69), channel_id=1, source_target_pairs={{0,18},{1,19},{2,16},{3,17},{16,2},{17,3},{18,0},{19,1},{4,22},{5,... | collective-permute-start | bytes 1572872 | tf_op jit(solution)/shard_map/ppermute | solution.py:29
  57.3 10.7 %collective-permute-start.10 = (bf16[2,2,4,4,8,256]{5,4,3,2,1,0:T(8,128)(2,1)S(1)}, bf16[2,2,4,4,8,256]{5,4,3,2,1,0:T(8,128)(2,1)S(1)}, u32[]{:S(2)}, u32[]{:S(2)}) collective-permute-start(bf16[2,2,4,4,8,256]{5,4,3,2,1,0:T(8,128)(2,1)S(1)} %get-tuple-element.27), channel_id=1, source_target_pairs={{0,8},{1,9},{2,10},{3,11},{16,24},{17,25},{18,26},{19,27},{4,12},{... | collective-permute-start | bytes 786440 | tf_op jit(solution)/shard_map/ppermute | solution.py:29
  58.3 13.5 %collective-permute-start.11 = (bf16[2,2,4,4,8,256]{5,4,3,2,1,0:T(8,128)(2,1)S(1)}, bf16[2,2,4,4,8,256]{5,4,3,2,1,0:T(8,128)(2,1)S(1)}, u32[]{:S(2)}, u32[]{:S(2)}) collective-permute-start(bf16[2,2,4,4,8,256]{5,4,3,2,1,0:T(8,128)(2,1)S(1)} %get-tuple-element.28), channel_id=1, source_target_pairs={{0,12},{1,13},{2,14},{3,15},{16,28},{17,29},{18,30},{19,31},{4,0},... | collective-permute-start | bytes 786440 | tf_op jit(solution)/shard_map/ppermute | solution.py:29
  60.3 11.5 %collective-permute-start.9 = (bf16[2,2,4,4,8,256]{5,4,3,2,1,0:T(8,128)(2,1)S(1)}, bf16[2,2,4,4,8,256]{5,4,3,2,1,0:T(8,128)(2,1)S(1)}, u32[]{:S(2)}, u32[]{:S(2)}) collective-permute-start(bf16[2,2,4,4,8,256]{5,4,3,2,1,0:T(8,128)(2,1)S(1)} %get-tuple-element.26), channel_id=1, source_target_pairs={{0,4},{1,5},{2,6},{3,7},{16,20},{17,21},{18,22},{19,23},{4,8},{5,9... | collective-permute-start | bytes 786440 | tf_op jit(solution)/shard_map/ppermute | solution.py:29
  71.9 11.7 %copy-start.3 = (s32[256]{0:T(256)S(1)}, s32[256]{0:T(256)}, u32[]{:S(2)}) copy-start(s32[256]{0:T(256)} %param.6) | copy-start | bytes 3076
  71.9 11.8 %copy-start.2 = (f32[256]{0:T(256)S(1)}, f32[256]{0:T(256)}, u32[]{:S(2)}) copy-start(f32[256]{0:T(256)} %param.9) | copy-start | bytes 3076
  71.9 2.7 %collective-permute-start.12 = (bf16[16,4,4,8,256]{4,3,2,1,0:T(8,128)(2,1)S(1)}, bf16[16,4,4,8,256]{4,3,2,1,0:T(8,128)(2,1)S(1)}, u32[]{:S(2)}, u32[]{:S(2)}) collective-permute-start(bf16[16,4,4,8,256]{4,3,2,1,0:T(8,128)(2,1)S(1)} %shard_map.72), channel_id=1, source_target_pairs={{0,1},{1,0},{2,3},{3,2},{16,17},{17,16},{18,19},{19,18},{4,5},{5,4... | collective-permute-start | bytes 3145736 | tf_op jit(solution)/shard_map/ppermute | solution.py:29
  79.8 17.8 %all-to-all-start.2 = ((bf16[8,256,256]{2,1,0:T(8,128)(2,1)}), bf16[8,256,256]{2,1,0:T(8,128)(2,1)S(1)}, u32[]{:S(2)}, u32[]{:S(2)}) async-start(bf16[8,256,256]{2,1,0:T(8,128)(2,1)} %shard_map.73), calls=%async_computation.2 | async-start | bytes 2097152 | tf_op jit(solution)/shard_map/all_to_all | solution.py:348
  83.7 1.3 %copy-start.1 = (bf16[256,2560]{1,0:T(8,128)(2,1)S(1)}, bf16[256,2560]{1,0:T(8,128)(2,1)}, u32[]{:S(2)}) copy-start(bf16[256,2560]{1,0:T(8,128)(2,1)} %h_hbm) | copy-start | bytes 3932164

commit v7 on v6

--- a/solution.py
+++ b/solution.py
@@ -148,27 +148,55 @@
     return near_call(body, [(n_grp, tok, width)], [places, *parts, other])[0]
 
 
-def serve_and_project(stacked, hidden, w_proj, norm_gain):
+def serve(stacked):
     layers, rows, width = stacked.shape
+
+    def body(m_ref, s_ref, held, m_sem, s_sem):
+        reads, writes = [], []
+        for l in range(layers):
+            reads.append(pltpu.make_async_copy(m_ref.at[l], held.at[l], m_sem.at[l]))
+            reads[l].start()
+            block = s_ref.at[:, l * width : (l + 1) * width]
+            writes.append(pltpu.make_async_copy(held.at[l], block, s_sem.at[l]))
+        for l in range(layers):
+            reads[l].wait()
+            writes[l].start()
+        for write in writes:
+            write.wait()
+
+    hbm = pl.BlockSpec(memory_space=pltpu.HBM)
+    return pl.pallas_call(
+        body,
+        in_specs=[hbm],
+        out_specs=hbm,
+        out_shape=jax.ShapeDtypeStruct((rows, layers * width), stacked.dtype),
+        scratch_shapes=[
+            pltpu.VMEM((layers, rows, width), stacked.dtype),
+            pltpu.SemaphoreType.DMA((layers,)),
+            pltpu.SemaphoreType.DMA((layers,)),
+        ],
+        compiler_params=pltpu.CompilerParams(vmem_limit_bytes=16 << 20),
+        cost_estimate=pl.CostEstimate(
+            flops=0, bytes_accessed=4 * stacked.size, transcendentals=0
+        ),
+    )(stacked)
+
+
+def normed_projection(hidden, w_proj, norm_gain, layers):
     tok, depth = hidden.shape
     columns = w_proj.shape[1]
+    width = columns // layers
     steps = 5
     part = depth // steps
 
-    def body(m_ref, h_hbm, w_ref, g_ref, s_ref, o_ref, *scratch):
-        held, h_ref, weights, acc_ref, m_sem, s_sem, w_sem, h_sem = scratch
-        loads, reads, writes = [], [], []
+    def body(h_hbm, w_ref, g_ref, o_ref, h_ref, weights, acc_ref, w_sem, h_sem):
+        loads = []
         states = pltpu.make_async_copy(h_hbm, h_ref, h_sem)
         states.start()
         for q in range(steps):
             rows_q = w_ref.at[q * part : (q + 1) * part]
             loads.append(pltpu.make_async_copy(rows_q, weights.at[q], w_sem.at[q]))
             loads[q].start()
-        for l in range(layers):
-            reads.append(pltpu.make_async_copy(m_ref.at[l], held.at[l], m_sem.at[l]))
-            reads[l].start()
-            block = s_ref.at[:, l * width : (l + 1) * width]
-            writes.append(pltpu.make_async_copy(held.at[l], block, s_sem.at[l]))
         states.wait()
         for q in range(steps):
             loads[q].wait()
@@ -182,43 +210,32 @@
             else:
                 acc_ref[...] = term
         for l in range(layers):
-            reads[l].wait()
-            writes[l].start()
-        for l in range(layers):
             proj = acc_ref[:, l * width : (l + 1) * width]
             mean_sq = jnp.mean(proj * proj, axis=-1, keepdims=True)
             normed = proj / jnp.sqrt(mean_sq + 1e-06) * g_ref[...]
             o_ref[l] = normed / math.sqrt(2.0)
-        for l in range(layers):
-            writes[l].wait()
 
     hbm = pl.BlockSpec(memory_space=pltpu.HBM)
     vmem = pl.BlockSpec(memory_space=pltpu.VMEM)
     return pl.pallas_call(
         body,
-        in_specs=[hbm, hbm, hbm, vmem],
-        out_specs=[hbm, vmem],
-        out_shape=[
-            jax.ShapeDtypeStruct((rows, layers * width), stacked.dtype),
-            jax.ShapeDtypeStruct((layers, tok, width), jnp.float32),
-        ],
+        in_specs=[hbm, hbm, vmem],
+        out_specs=vmem,
+        out_shape=jax.ShapeDtypeStruct((layers, tok, width), jnp.float32),
         scratch_shapes=[
-            pltpu.VMEM((layers, rows, width), stacked.dtype),
             pltpu.VMEM((tok, depth), hidden.dtype),
             pltpu.VMEM((steps, part, columns), w_proj.dtype),
             pltpu.VMEM((tok, columns), jnp.float32),
-            pltpu.SemaphoreType.DMA((layers,)),
-            pltpu.SemaphoreType.DMA((layers,)),
             pltpu.SemaphoreType.DMA((steps,)),
             pltpu.SemaphoreType.DMA,
         ],
-        compiler_params=pltpu.CompilerParams(vmem_limit_bytes=46 << 20),
+        compiler_params=pltpu.CompilerParams(vmem_limit_bytes=56 << 20),
         cost_estimate=pl.CostEstimate(
             flops=2 * tok * depth * columns,
-            bytes_accessed=2 * depth * (tok + columns) + 4 * stacked.size,
+            bytes_accessed=2 * depth * (tok + columns) + 4 * tok * columns,
             transcendentals=0,
         ),
-    )(stacked, hidden, w_proj, norm_gain.reshape(1, width))
+    )(hidden, w_proj, norm_gain.reshape(1, width))
 
 
 def add_embedding(crossed, pieces, normed):
@@ -297,7 +314,10 @@
         axis_index_groups=columns,
         tiled=True,
     )
-    gated, ids = lax.optimization_barrier((table.reshape(n_grp, row_count, width), ids))
+    normed = normed_projection(hidden, w_proj, norm_gain, layers)
+    gated, ids, normed = lax.optimization_barrier(
+        (table.reshape(n_grp, row_count, width), ids, normed)
+    )
     moved = lax.all_to_all(gated, "grp", split_axis=0, concat_axis=0, tiled=True)
 
     def crossed_of(holder):
@@ -343,11 +363,10 @@
     parts = [*a_x, a_far, near, b_far, *b_x]
     other = hop(core_parts(parts, n_x), core=1)
     sorted_rows = in_token_order(places, parts, other, n_x)
-    moved, sorted_rows, hidden = lax.optimization_barrier((moved, sorted_rows, hidden))
+    moved, sorted_rows = lax.optimization_barrier((moved, sorted_rows))
 
     pieces = lax.all_to_all(sorted_rows, "grp", split_axis=0, concat_axis=0, tiled=True)
-    served, normed = serve_and_project(moved, hidden, w_proj, norm_gain)
-    served = served.reshape(1, 1, row_count, layers * width)
+    served = serve(moved).reshape(1, 1, row_count, layers * width)
     crossed = crossed_of(token_ids // shard_rows)
     layer_inputs = add_embedding(crossed, pieces, normed)
     return (served, layer_inputs)

time: 100 us -> 105 us (1.050)
  blocking collectives: 15.5 us -> 0 us
  waiting for transfers between devices: 34 us -> 42.2 us
  starting transfers between devices: 25.9 us -> 33.7 us
  Pallas kernels: 15 us -> 19.9 us
    all_to_all x1 -> x0, blocking collectives: 15.5 us -> none  [on_device(): lax.all_to_all(jnp.broadcast_to(token_ids[None, None], (2 * n_grp, 1, tok...]
    all_to_all x0 -> x1, starting transfers between devices: none -> 8.13 us  [on_device(): lax.all_to_all(jnp.broadcast_to(token_ids[None, None], (2 * n_grp, 1, tok...]
    all_to_all x1, waiting for transfers between devices: 4.44 us -> 10.6 us  [on_device(): lax.all_to_all(sorted_rows, 'grp', split_axis=0, concat_axis=0, tiled=True)]
    pallas_call x1 -> x2, Pallas kernels: 8.12 us -> 13.1 us  [the longest x1 9.35 us: normed_projection(): pl.pallas_call(body, in_specs=[hbm, hbm, vmem], out_specs=vmem, out_shape...]
    ppermute x13, waiting for transfers between devices: 26.7 us -> 28.8 us  [send(): return lax.ppermute(value, BOTH, moves)]
    unnamed x9 -> x7, local copies, waits for them, and re-layouts: 3.52 us -> 2.2 us
    ppermute x13, starting transfers between devices: 17.6 us -> 16.4 us  [send(): return lax.ppermute(value, BOTH, moves)]
    all_to_all x1, starting transfers between devices: 4.56 us -> 5.62 us  [on_device(): lax.all_to_all(gated, 'grp', split_axis=0, concat_axis=0, tiled=True)]
  transfers between devices with their start and end apart: 15 -> 16, of which waited for: 9 -> 10; matrix products, arithmetic and copies ran while one was open for 4% -> 4% of each run, Pallas kernels for 13% -> 17%
where the time goes in v7:
time: 105 us; the launch traced here: 104 us
  waiting for transfers between devices  42.2 us (40%)
  starting transfers between devices  33.7 us (32%)
  Pallas kernels  19.9 us (19%)
  local copies, waits for them, and re-layouts  5.07 us (5%)
  other arithmetic  2.33 us (2%)
    ppermute x13, waiting for transfers between devices, send(): return lax.ppermute(value, BOTH, moves)  28.8 us
    ppermute x13, starting transfers between devices, send(): return lax.ppermute(value, BOTH, moves)  16.4 us
    all_to_all x1, waiting for transfers between devices, on_device(): lax.all_to_all(sorted_rows, 'grp', split_axis=0, concat_axis=0, tiled=True)  10.6 us
    pallas_call x1, Pallas kernels, normed_projection(): pl.pallas_call(body, in_specs=[hbm, hbm, vmem], out_specs=vmem, out_shape...  9.35 us
    all_to_all x1, starting transfers between devices, on_device(): lax.all_to_all(jnp.broadcast_to(token_ids[None, None], (2 * n_grp, 1, tok...  8.13 us
    all_to_all x1, starting transfers between devices, on_device(): lax.all_to_all(gated, 'grp', split_axis=0, concat_axis=0, tiled=True)  5.62 us
    pallas_call x6, Pallas kernels, near_call(): pl.pallas_call(body, in_specs=[vmem] * len(operands), out_specs=[vmem] *...  5.01 us
    pallas_call x1, Pallas kernels, serve(): pl.pallas_call(body, in_specs=[hbm], out_specs=hbm, out_shape=jax.ShapeDt...  3.72 us
  transfers between devices with their start and end apart: 16, of which 10 were waited for; matrix products, arithmetic and copies ran while one was open for 4% of the time, Pallas kernels for 17%

profile of v7, /device:TPU:0, one launch (start us, length us, event | category | flops | bytes accessed | tf_op | source)
XLA Modules:
  0.0 104.2 jit_solution(11371465233295450286)
XLA Ops:
  0.6 1.3 %broadcast_in_dim.3 = s32[16,1,256]{2,1,0:T(1,128)} broadcast(s32[256]{0:T(256)} %param.6), dimensions={2} | broadcast | bytes 17408 | tf_op jit(solution)/shard_map/broadcast_in_dim | solution.py:310
  1.9 8.1 %all-to-all-start = ((s32[16,1,256]{2,1,0:T(1,128)}), s32[16,1,256]{2,1,0:T(1,128)S(1)}, u32[]{:S(2)}, u32[]{:S(2)}) async-start(s32[16,1,256]{2,1,0:T(1,128)} %broadcast_in_dim.3), calls=%async_computation | async-start | bytes 32768 | tf_op jit(solution)/shard_map/all_to_all | solution.py:309
  10.1 9.4 %shard_map.68.n_ref = f32[8,256,256]{2,1,0:T(8,128)} custom-call(bf16[256,2560]{1,0:T(8,128)(2,1)} %h_hbm.1, bf16[2560,2048]{1,0:T(8,128)(2,1)} %w_ref.1, f32[1,256]{1,0:T(1,128)} %bitcast.56), custom_call_target="tpu_custom_call" | custom-call | flops 2684354560 | bytes 13893632 | tf_op jit(solution)/shard_map/pallas_call | solution.py:220
  19.4 5.6 %all-to-all-start.1 = ((bf16[8,1024,256]{2,1,0:T(8,128)(2,1)}), bf16[8,1024,256]{2,1,0:T(8,128)(2,1)}, u32[]{:S(2)}, u32[]{:S(2)}) async-start(bf16[8,1024,256]{2,1,0:T(8,128)(2,1)} %bitcast.45), calls=%async_computation.1 | async-start | bytes 8388608 | tf_op jit(solution)/shard_map/all_to_all | solution.py:321
  25.1 1.3 %convert_reduce_fusion = s32[2,8,256]{2,1,0:T(8,128)S(1)} fusion(s32[2,8,256]{2,1,0:T(8,128)S(1)} %get-tuple-element.35, pred[256,256]{1,0:T(8,128)(4,1)S(1)} %iota_compare_fusion.1), kind=kLoop, calls=%fused_computation.2 | loop fusion | flops 4190208 | bytes 98304 | tf_op jit(solution)/shard_map/reduce_sum | solution.py:333
  29.3 2.8 %collective-permute-start.1 = (s32[2,2,8,32]{3,2,1,0:T(8,128)S(1)}, s32[2,2,8,32]{3,2,1,0:T(8,128)S(1)}, u32[]{:S(2)}, u32[]{:S(2)}) collective-permute-start(s32[2,2,8,32]{3,2,1,0:T(8,128)S(1)} %get-tuple-element.39), channel_id=1, source_target_pairs={{0,12},{1,13},{2,14},{3,15},{16,28},{17,29},{18,30},{19,31},{4,0},... | collective-permute-start | bytes 12296 | tf_op jit(solution)/shard_map/ppermute | solution.py:29
  33.9 3.6 %collective-permute-done.2 = s32[2,2,8,32]{3,2,1,0:T(8,128)S(1)} collective-permute-done((s32[2,2,8,32]{3,2,1,0:T(8,128)S(1)}, s32[2,2,8,32]{3,2,1,0:T(8,128)S(1)}, u32[]{:S(2)}, u32[]{:S(2)}) %collective-permute-start.2) | collective-permute-done | bytes 4128 | tf_op jit(solution)/shard_map/ppermute | solution.py:29
  38.1 2.2 %copy-done = bf16[1,8192,256]{2,1,0:T(8,128)(2,1)S(1)} copy-done((bf16[1,8192,256]{2,1,0:T(8,128)(2,1)S(1)}, bf16[1,8192,256]{2,1,0:T(8,128)(2,1)}, u32[]{:S(2)}) %copy-start) | copy-done | bytes 4194328
  41.6 1.3 %shard_map.69 = (bf16[2,2,4,4,8,256]{5,4,3,2,1,0:T(8,128)(2,1)S(1)}, bf16[2,2,4,4,8,256]{5,4,3,2,1,0:T(8,128)(2,1)S(1)}, bf16[2,2,4,4,8,256]{5,4,3,2,1,0:T(8,128)(2,1)S(1)}, bf16[2,2,4,4,8,256]{5,4,3,2,1,0:T(8,128)(2,1)S(1)}) custom-call(s32[8,4,128]{2,1,0:T(4,128)S(1)} %reshape.68.w_ref, bf16[8192,256]{1,0:T(8,128)(2,1)S(1)} %bitcast.47), custom_call_target="tpu_custom_call" | custom-call | bytes 65536 | tf_op jit(solution)/shard_map/pallas_call | solution.py:78
  42.9 3.3 %collective-permute-start.8 = (bf16[4,2,4,4,8,256]{5,4,3,2,1,0:T(8,128)(2,1)S(1)}, bf16[4,2,4,4,8,256]{5,4,3,2,1,0:T(8,128)(2,1)S(1)}, u32[]{:S(2)}, u32[]{:S(2)}) collective-permute-start(bf16[4,2,4,4,8,256]{5,4,3,2,1,0:T(8,128)(2,1)S(1)} %get-tuple-element.23), channel_id=1, source_target_pairs={{0,18},{1,19},{2,16},{3,17},{16,2},{17,3},{18,0},{19,1},{4,22},{5,... | collective-permute-start | bytes 1572872 | tf_op jit(solution)/shard_map/ppermute | solution.py:29
  46.2 1.8 %collective-permute-start.5 = (bf16[2,2,4,4,8,256]{5,4,3,2,1,0:T(8,128)(2,1)S(1)}, bf16[2,2,4,4,8,256]{5,4,3,2,1,0:T(8,128)(2,1)S(1)}, u32[]{:S(2)}, u32[]{:S(2)}) collective-permute-start(bf16[2,2,4,4,8,256]{5,4,3,2,1,0:T(8,128)(2,1)S(1)} %get-tuple-element.20), channel_id=1, source_target_pairs={{0,8},{1,9},{2,10},{3,11},{16,24},{17,25},{18,26},{19,27},{4,12},{... | collective-permute-start | bytes 786440 | tf_op jit(solution)/shard_map/ppermute | solution.py:29
  48.0 2.4 %collective-permute-start.6 = (bf16[2,2,4,4,8,256]{5,4,3,2,1,0:T(8,128)(2,1)S(1)}, bf16[2,2,4,4,8,256]{5,4,3,2,1,0:T(8,128)(2,1)S(1)}, u32[]{:S(2)}, u32[]{:S(2)}) collective-permute-start(bf16[2,2,4,4,8,256]{5,4,3,2,1,0:T(8,128)(2,1)S(1)} %get-tuple-element.21), channel_id=1, source_target_pairs={{0,12},{1,13},{2,14},{3,15},{16,28},{17,29},{18,30},{19,31},{4,0},... | collective-permute-start | bytes 786440 | tf_op jit(solution)/shard_map/ppermute | solution.py:29
  50.3 9.5 %collective-permute-done.4.refs_1_ = bf16[2,2,4,4,8,256]{5,4,3,2,1,0:T(8,128)(2,1)S(1)} collective-permute-done((bf16[2,2,4,4,8,256]{5,4,3,2,1,0:T(8,128)(2,1)S(1)}, bf16[2,2,4,4,8,256]{5,4,3,2,1,0:T(8,128)(2,1)S(1)}, u32[]{:S(2)}, u32[]{:S(2)}) %collective-permute-start.4) | collective-permute-done | bytes 262176 | tf_op jit(solution)/shard_map/ppermute | solution.py:29
  61.0 1.6 %collective-permute-start.10 = (bf16[2,2,4,4,8,256]{5,4,3,2,1,0:T(8,128)(2,1)S(1)}, bf16[2,2,4,4,8,256]{5,4,3,2,1,0:T(8,128)(2,1)S(1)}, u32[]{:S(2)}, u32[]{:S(2)}) collective-permute-start(bf16[2,2,4,4,8,256]{5,4,3,2,1,0:T(8,128)(2,1)S(1)} %get-tuple-element.25), channel_id=1, source_target_pairs={{0,8},{1,9},{2,10},{3,11},{16,24},{17,25},{18,26},{19,27},{4,12},{... | collective-permute-start | bytes 786440 | tf_op jit(solution)/shard_map/ppermute | solution.py:29
  62.6 2.0 %collective-permute-start.11 = (bf16[2,2,4,4,8,256]{5,4,3,2,1,0:T(8,128)(2,1)S(1)}, bf16[2,2,4,4,8,256]{5,4,3,2,1,0:T(8,128)(2,1)S(1)}, u32[]{:S(2)}, u32[]{:S(2)}) collective-permute-start(bf16[2,2,4,4,8,256]{5,4,3,2,1,0:T(8,128)(2,1)S(1)} %get-tuple-element.26), channel_id=1, source_target_pairs={{0,12},{1,13},{2,14},{3,15},{16,28},{17,29},{18,30},{19,31},{4,0},... | collective-permute-start | bytes 786440 | tf_op jit(solution)/shard_map/ppermute | solution.py:29
  64.6 7.2 %collective-permute-done.10.refs_8_ = bf16[2,2,4,4,8,256]{5,4,3,2,1,0:T(8,128)(2,1)S(1)} collective-permute-done((bf16[2,2,4,4,8,256]{5,4,3,2,1,0:T(8,128)(2,1)S(1)}, bf16[2,2,4,4,8,256]{5,4,3,2,1,0:T(8,128)(2,1)S(1)}, u32[]{:S(2)}, u32[]{:S(2)}) %collective-permute-start.10) | collective-permute-done | bytes 262176 | tf_op jit(solution)/shard_map/ppermute | solution.py:29
  71.8 4.3 %collective-permute-done.11.refs_9_ = bf16[2,2,4,4,8,256]{5,4,3,2,1,0:T(8,128)(2,1)S(1)} collective-permute-done((bf16[2,2,4,4,8,256]{5,4,3,2,1,0:T(8,128)(2,1)S(1)}, bf16[2,2,4,4,8,256]{5,4,3,2,1,0:T(8,128)(2,1)S(1)}, u32[]{:S(2)}, u32[]{:S(2)}) %collective-permute-start.11) | collective-permute-done | bytes 262176 | tf_op jit(solution)/shard_map/ppermute | solution.py:29
  76.6 2.6 %collective-permute-done.12.refs_10_ = bf16[16,4,4,8,256]{4,3,2,1,0:T(8,128)(2,1)S(1)} collective-permute-done((bf16[16,4,4,8,256]{4,3,2,1,0:T(8,128)(2,1)S(1)}, bf16[16,4,4,8,256]{4,3,2,1,0:T(8,128)(2,1)S(1)}, u32[]{:S(2)}, u32[]{:S(2)}) %collective-permute-start.12) | collective-permute-done | bytes 1048608 | tf_op jit(solution)/shard_map/ppermute | solution.py:29
  79.1 2.3 %shard_map.74 = bf16[8,256,256]{2,1,0:T(8,128)(2,1)} custom-call(s32[8,256]{1,0:T(8,128)S(1)} %fusion.26.p_ref, bf16[2,2,4,4,8,256]{5,4,3,2,1,0:T(8,128)(2,1)S(1)} %get-tuple-element.18.refs_0_, bf16[2,2,4,4,8,256]{5,4,3,2,1,0:T(8,128)(2,1)S(1)} %collective-permute-done.4.refs_1_, bf16[2,2,4,4,8,256]{5,4,3,2,1,0:T(8,128)(2,1)S(1)} %collective-permute-done.5.refs_2_, ...), custom_call_target="tpu_custom_call" | custom-call | bytes 65536 | tf_op jit(solution)/shard_map/pallas_call | solution.py:78
  81.4 2.7 %all-to-all-done.1.m_ref = bf16[8,1024,256]{2,1,0:T(8,128)(2,1)} async-done(((bf16[8,1024,256]{2,1,0:T(8,128)(2,1)}), bf16[8,1024,256]{2,1,0:T(8,128)(2,1)}, u32[]{:S(2)}, u32[]{:S(2)}) %all-to-all-start.1) | async-done | bytes 4194336 | tf_op jit(solution)/shard_map/all_to_all | solution.py:321
  84.1 3.6 %all-to-all-start.2 = ((bf16[8,256,256]{2,1,0:T(8,128)(2,1)}), bf16[8,256,256]{2,1,0:T(8,128)(2,1)S(1)}, u32[]{:S(2)}, u32[]{:S(2)}) async-start(bf16[8,256,256]{2,1,0:T(8,128)(2,1)} %shard_map.74), calls=%async_computation.2 | async-start | bytes 2097152 | tf_op jit(solution)/shard_map/all_to_all | solution.py:368
  87.9 3.7 %shard_map.75 = bf16[1024,2048]{1,0:T(8,128)(2,1)} custom-call(bf16[8,1024,256]{2,1,0:T(8,128)(2,1)} %all-to-all-done.1.m_ref), custom_call_target="tpu_custom_call" | custom-call | bytes 8388608 | tf_op jit(solution)/shard_map/pallas_call | solution.py:168
  91.6 10.6 %all-to-all-done.2.r_ref = bf16[8,256,256]{2,1,0:T(8,128)(2,1)S(1)} async-done(((bf16[8,256,256]{2,1,0:T(8,128)(2,1)}), bf16[8,256,256]{2,1,0:T(8,128)(2,1)S(1)}, u32[]{:S(2)}, u32[]{:S(2)}) %all-to-all-start.2) | async-done | bytes 1048608 | tf_op jit(solution)/shard_map/all_to_all | solution.py:368
  102.2 1.9 %shard_map.76 = bf16[256,8,256]{2,1,0:T(8,128)(2,1)} custom-call(s32[256,1]{1,0:T(8,128)S(1)} %copy.33.s_ref, bf16[8,256,256]{2,1,0:T(8,128)(2,1)S(1)} %all-to-all-done.2.r_ref, f32[8,256,256]{2,1,0:T(8,128)S(1)} %copy-done.1), custom_call_target="tpu_custom_call" | custom-call | flops 3145728 | bytes 4194304 | tf_op jit(solution)/shard_map/pallas_call | solution.py:265
  (45 shorter events, 8.3 us)
Async XLA Ops:
  1.9 17.5 %all-to-all-start = ((s32[16,1,256]{2,1,0:T(1,128)}), s32[16,1,256]{2,1,0:T(1,128)S(1)}, u32[]{:S(2)}, u32[]{:S(2)}) async-start(s32[16,1,256]{2,1,0:T(1,128)} %broadcast_in_dim.3), calls=%async_computation | async-start | bytes 32768 | tf_op jit(solution)/shard_map/all_to_all | solution.py:309
  19.4 64.7 %all-to-all-start.1 = ((bf16[8,1024,256]{2,1,0:T(8,128)(2,1)}), bf16[8,1024,256]{2,1,0:T(8,128)(2,1)}, u32[]{:S(2)}, u32[]{:S(2)}) async-start(bf16[8,1024,256]{2,1,0:T(8,128)(2,1)} %bitcast.45), calls=%async_computation.1 | async-start | bytes 8388608 | tf_op jit(solution)/shard_map/all_to_all | solution.py:321
  28.0 1.3 %collective-permute-start = (s32[2,4,8,32]{3,2,1,0:T(8,128)S(1)}, s32[2,4,8,32]{3,2,1,0:T(8,128)S(1)}, u32[]{:S(2)}, u32[]{:S(2)}) collective-permute-start(s32[2,4,8,32]{3,2,1,0:T(8,128)S(1)} %squeeze.17), channel_id=1, source_target_pairs={{0,1},{1,0},{2,3},{3,2},{16,17},{17,16},{18,19},{19,18},{4,5},{5,4... | collective-permute-start | bytes 24584 | tf_op jit(solution)/shard_map/ppermute | solution.py:29
  29.3 4.5 %collective-permute-start.1 = (s32[2,2,8,32]{3,2,1,0:T(8,128)S(1)}, s32[2,2,8,32]{3,2,1,0:T(8,128)S(1)}, u32[]{:S(2)}, u32[]{:S(2)}) collective-permute-start(s32[2,2,8,32]{3,2,1,0:T(8,128)S(1)} %get-tuple-element.39), channel_id=1, source_target_pairs={{0,12},{1,13},{2,14},{3,15},{16,28},{17,29},{18,30},{19,31},{4,0},... | collective-permute-start | bytes 12296 | tf_op jit(solution)/shard_map/ppermute | solution.py:29
  32.2 5.2 %collective-permute-start.2 = (s32[2,2,8,32]{3,2,1,0:T(8,128)S(1)}, s32[2,2,8,32]{3,2,1,0:T(8,128)S(1)}, u32[]{:S(2)}, u32[]{:S(2)}) collective-permute-start(s32[2,2,8,32]{3,2,1,0:T(8,128)S(1)} %get-tuple-element.41), channel_id=1, source_target_pairs={{0,8},{1,9},{2,10},{3,11},{16,24},{17,25},{18,26},{19,27},{4,12},{... | collective-permute-start | bytes 12296 | tf_op jit(solution)/shard_map/ppermute | solution.py:29
  33.0 4.9 %collective-permute-start.3 = (s32[2,2,8,32]{3,2,1,0:T(8,128)S(1)}, s32[2,2,8,32]{3,2,1,0:T(8,128)S(1)}, u32[]{:S(2)}, u32[]{:S(2)}) collective-permute-start(s32[2,2,8,32]{3,2,1,0:T(8,128)S(1)} %get-tuple-element.40), channel_id=1, source_target_pairs={{0,4},{1,5},{2,6},{3,7},{16,20},{17,21},{18,22},{19,23},{4,8},{5,9... | collective-permute-start | bytes 12296 | tf_op jit(solution)/shard_map/ppermute | solution.py:29
  38.1 2.2 %copy-start = (bf16[1,8192,256]{2,1,0:T(8,128)(2,1)S(1)}, bf16[1,8192,256]{2,1,0:T(8,128)(2,1)}, u32[]{:S(2)}) copy-start(bf16[1,8192,256]{2,1,0:T(8,128)(2,1)} %param.5) | copy-start | bytes 12582916
  42.9 18.0 %collective-permute-start.8 = (bf16[4,2,4,4,8,256]{5,4,3,2,1,0:T(8,128)(2,1)S(1)}, bf16[4,2,4,4,8,256]{5,4,3,2,1,0:T(8,128)(2,1)S(1)}, u32[]{:S(2)}, u32[]{:S(2)}) collective-permute-start(bf16[4,2,4,4,8,256]{5,4,3,2,1,0:T(8,128)(2,1)S(1)} %get-tuple-element.23), channel_id=1, source_target_pairs={{0,18},{1,19},{2,16},{3,17},{16,2},{17,3},{18,0},{19,1},{4,22},{5,... | collective-permute-start | bytes 1572872 | tf_op jit(solution)/shard_map/ppermute | solution.py:29
  46.2 13.6 %collective-permute-start.4 = (bf16[2,2,4,4,8,256]{5,4,3,2,1,0:T(8,128)(2,1)S(1)}, bf16[2,2,4,4,8,256]{5,4,3,2,1,0:T(8,128)(2,1)S(1)}, u32[]{:S(2)}, u32[]{:S(2)}) collective-permute-start(bf16[2,2,4,4,8,256]{5,4,3,2,1,0:T(8,128)(2,1)S(1)} %get-tuple-element.19), channel_id=1, source_target_pairs={{0,4},{1,5},{2,6},{3,7},{16,20},{17,21},{18,22},{19,23},{4,8},{5,9... | collective-permute-start | bytes 786440 | tf_op jit(solution)/shard_map/ppermute | solution.py:29
  46.2 13.6 %collective-permute-start.5 = (bf16[2,2,4,4,8,256]{5,4,3,2,1,0:T(8,128)(2,1)S(1)}, bf16[2,2,4,4,8,256]{5,4,3,2,1,0:T(8,128)(2,1)S(1)}, u32[]{:S(2)}, u32[]{:S(2)}) collective-permute-start(bf16[2,2,4,4,8,256]{5,4,3,2,1,0:T(8,128)(2,1)S(1)} %get-tuple-element.20), channel_id=1, source_target_pairs={{0,8},{1,9},{2,10},{3,11},{16,24},{17,25},{18,26},{19,27},{4,12},{... | collective-permute-start | bytes 786440 | tf_op jit(solution)/shard_map/ppermute | solution.py:29
  48.0 12.4 %collective-permute-start.6 = (bf16[2,2,4,4,8,256]{5,4,3,2,1,0:T(8,128)(2,1)S(1)}, bf16[2,2,4,4,8,256]{5,4,3,2,1,0:T(8,128)(2,1)S(1)}, u32[]{:S(2)}, u32[]{:S(2)}) collective-permute-start(bf16[2,2,4,4,8,256]{5,4,3,2,1,0:T(8,128)(2,1)S(1)} %get-tuple-element.21), channel_id=1, source_target_pairs={{0,12},{1,13},{2,14},{3,15},{16,28},{17,29},{18,30},{19,31},{4,0},... | collective-permute-start | bytes 786440 | tf_op jit(solution)/shard_map/ppermute | solution.py:29
  60.5 15.7 %collective-permute-start.7 = (bf16[4,2,4,4,8,256]{5,4,3,2,1,0:T(8,128)(2,1)S(1)}, bf16[4,2,4,4,8,256]{5,4,3,2,1,0:T(8,128)(2,1)S(1)}, u32[]{:S(2)}, u32[]{:S(2)}) collective-permute-start(bf16[4,2,4,4,8,256]{5,4,3,2,1,0:T(8,128)(2,1)S(1)} %shard_map.70), channel_id=1, source_target_pairs={{0,18},{1,19},{2,16},{3,17},{16,2},{17,3},{18,0},{19,1},{4,22},{5,... | collective-permute-start | bytes 1572872 | tf_op jit(solution)/shard_map/ppermute | solution.py:29
  61.0 10.8 %collective-permute-start.10 = (bf16[2,2,4,4,8,256]{5,4,3,2,1,0:T(8,128)(2,1)S(1)}, bf16[2,2,4,4,8,256]{5,4,3,2,1,0:T(8,128)(2,1)S(1)}, u32[]{:S(2)}, u32[]{:S(2)}) collective-permute-start(bf16[2,2,4,4,8,256]{5,4,3,2,1,0:T(8,128)(2,1)S(1)} %get-tuple-element.25), channel_id=1, source_target_pairs={{0,8},{1,9},{2,10},{3,11},{16,24},{17,25},{18,26},{19,27},{4,12},{... | collective-permute-start | bytes 786440 | tf_op jit(solution)/shard_map/ppermute | solution.py:29
  62.6 13.5 %collective-permute-start.11 = (bf16[2,2,4,4,8,256]{5,4,3,2,1,0:T(8,128)(2,1)S(1)}, bf16[2,2,4,4,8,256]{5,4,3,2,1,0:T(8,128)(2,1)S(1)}, u32[]{:S(2)}, u32[]{:S(2)}) collective-permute-start(bf16[2,2,4,4,8,256]{5,4,3,2,1,0:T(8,128)(2,1)S(1)} %get-tuple-element.26), channel_id=1, source_target_pairs={{0,12},{1,13},{2,14},{3,15},{16,28},{17,29},{18,30},{19,31},{4,0},... | collective-permute-start | bytes 786440 | tf_op jit(solution)/shard_map/ppermute | solution.py:29
  64.6 11.5 %collective-permute-start.9 = (bf16[2,2,4,4,8,256]{5,4,3,2,1,0:T(8,128)(2,1)S(1)}, bf16[2,2,4,4,8,256]{5,4,3,2,1,0:T(8,128)(2,1)S(1)}, u32[]{:S(2)}, u32[]{:S(2)}) collective-permute-start(bf16[2,2,4,4,8,256]{5,4,3,2,1,0:T(8,128)(2,1)S(1)} %get-tuple-element.24), channel_id=1, source_target_pairs={{0,4},{1,5},{2,6},{3,7},{16,20},{17,21},{18,22},{19,23},{4,8},{5,9... | collective-permute-start | bytes 786440 | tf_op jit(solution)/shard_map/ppermute | solution.py:29
  76.2 11.5 %copy-start.2 = (s32[256]{0:T(256)S(1)}, s32[256]{0:T(256)}, u32[]{:S(2)}) copy-start(s32[256]{0:T(256)} %param.6) | copy-start | bytes 3076
  76.2 2.9 %collective-permute-start.12 = (bf16[16,4,4,8,256]{4,3,2,1,0:T(8,128)(2,1)S(1)}, bf16[16,4,4,8,256]{4,3,2,1,0:T(8,128)(2,1)S(1)}, u32[]{:S(2)}, u32[]{:S(2)}) collective-permute-start(bf16[16,4,4,8,256]{4,3,2,1,0:T(8,128)(2,1)S(1)} %shard_map.73), channel_id=1, source_target_pairs={{0,1},{1,0},{2,3},{3,2},{16,17},{17,16},{18,19},{19,18},{4,5},{5,4... | collective-permute-start | bytes 3145736 | tf_op jit(solution)/shard_map/ppermute | solution.py:29
  84.1 18.1 %all-to-all-start.2 = ((bf16[8,256,256]{2,1,0:T(8,128)(2,1)}), bf16[8,256,256]{2,1,0:T(8,128)(2,1)S(1)}, u32[]{:S(2)}, u32[]{:S(2)}) async-start(bf16[8,256,256]{2,1,0:T(8,128)(2,1)} %shard_map.74), calls=%async_computation.2 | async-start | bytes 2097152 | tf_op jit(solution)/shard_map/all_to_all | solution.py:368
  87.8 14.4 %copy-start.1 = (f32[8,256,256]{2,1,0:T(8,128)S(1)}, f32[8,256,256]{2,1,0:T(8,128)}, u32[]{:S(2)}) copy-start(f32[8,256,256]{2,1,0:T(8,128)} %shard_map.68.n_ref) | copy-start | bytes 6291460
